TPU v7x, 32 devices: a whole 2x2x4 slice. The times are simulated.
32 devices in a mesh: ms: 2 (over x), date: 4 (over y, core), pix: 4 (over z).
Axes of the slice: x: 2, y: 2, z: 4, core: 2. Of those that a mesh axis runs over, the one named last changes fastest.
Arguments:
- slc_stack: float32 [2, 64, 128, 128], P(None, ('ms', 'date'), 'pix'), may hold values from -6 to 6
Outputs:
- linked_phases: float32 [2, 64, 128, 128], P(None, ('ms', 'date'), 'pix')
- compressed_slc: float32 [2, 2, 128, 128], P(None, 'ms', 'pix', 'date')
All inputs are finite; a program needn't handle non-finite values.
Results may differ from a plain program's by a relative error of at most 0.0001.
Values sent between devices are 32-bit elements; how exact they have to be, the bound alone decides.
No kernel may reach another device: no remote copies, remote signals or barrier semaphores. Data moves between devices by JAX's collectives and lax.ppermute only.
A program may use at most 128 MiB of HBM per device.

v0:
```python
import math

import jax
import jax.numpy as jnp
from jax import lax
from jax.sharding import PartitionSpec as P

HALF = 5
ITERS = 3


epsilon = 1e-06
date_block = 8
pixel_target = 1024


def extended(block, sides, width):
    for axis, dim in sides:
        count = lax.axis_size(axis)
        forward = [(i, i + 1) for i in range(count - 1)]
        backward = [(target, source) for source, target in forward]
        low = lax.ppermute(
            lax.slice_in_dim(block, block.shape[dim] - width, None, axis=dim), axis, forward
        )
        high = lax.ppermute(lax.slice_in_dim(block, 0, width, axis=dim), axis, backward)
        block = jnp.concatenate([low, block, high], axis=dim)
    return block


def from_behind(value, axis, steps):
    count = lax.axis_size(axis)
    initial, last = (max(0, -steps), min(count, count - steps))
    return lax.ppermute(value, axis, [(source, source + steps) for source in range(initial, last)])


def band_height(row_count, col_count):
    height = row_count
    while height * col_count > pixel_target and height % 2 == 0:
        height = height // 2
    return height


def window_area():
    return float((2 * HALF + 1) ** 2)


def box_sum(values, row_count, col_count):
    window_width = 2 * HALF + 1
    running = values[..., 0:row_count, :]
    for offset in range(1, window_width):
        running = running + values[..., offset : offset + row_count, :]
    summed = running[..., 0:col_count]
    for offset in range(1, window_width):
        summed = summed + running[..., offset : offset + col_count]
    return summed.reshape(summed.shape[:-2] + (row_count * col_count,))


def window_along(values, count, axis_index):
    length = values.shape[axis_index]
    pairs = lax.slice_in_dim(values, 0, length - 1, axis=axis_index) + lax.slice_in_dim(
        values, 1, length, axis=axis_index
    )
    quads = lax.slice_in_dim(pairs, 0, length - 3, axis=axis_index) + lax.slice_in_dim(
        pairs, 2, length - 1, axis=axis_index
    )
    eights = lax.slice_in_dim(quads, 0, length - 7, axis=axis_index) + lax.slice_in_dim(
        quads, 4, length - 3, axis=axis_index
    )
    summed = lax.slice_in_dim(eights, 0, count, axis=axis_index) + lax.slice_in_dim(
        pairs, 8, 8 + count, axis=axis_index
    )
    return summed + lax.slice_in_dim(values, 10, 10 + count, axis=axis_index)


def box_leading(values, row_count, col_count):
    return window_along(window_along(values, row_count, 0), col_count, 1)


def cross_sums(left_data, right_data, row_count, col_count):
    left_real = left_data[0][:, None]
    left_imag = left_data[1][:, None]
    right_real = right_data[0][None]
    right_imag = right_data[1][None]
    real_part = box_sum(left_real * right_real + left_imag * right_imag, row_count, col_count)
    imag_part = box_sum(left_imag * right_real - left_real * right_imag, row_count, col_count)
    return (real_part, imag_part)


def own_covariance(row_band, row_count, col_count):
    date_count = row_band.shape[1]
    leading = row_band.transpose(2, 3, 0, 1)
    padded_rows = leading.shape[0]
    padded_cols = leading.shape[1]
    right_real = leading[:, :, 0][:, :, None, :]
    right_imag = leading[:, :, 1][:, :, None, :]

    def one_block(position):
        left_data = lax.dynamic_slice_in_dim(leading, position * date_block, date_block, 3)
        left_real = left_data[:, :, 0][:, :, :, None]
        left_imag = left_data[:, :, 1][:, :, :, None]
        flat_shape = (padded_rows, padded_cols, date_block * date_count)
        prod_real = (left_real * right_real + left_imag * right_imag).reshape(flat_shape)
        prod_imag = (left_imag * right_real - left_real * right_imag).reshape(flat_shape)
        return (
            box_leading(prod_real, row_count, col_count),
            box_leading(prod_imag, row_count, col_count),
        )

    block_count = date_count // date_block
    real_part, imag_part = lax.map(one_block, jnp.arange(block_count, dtype=jnp.int32))
    flat_size = row_count * col_count

    def reorder(part):
        shaped = part.reshape(block_count, row_count, col_count, date_block, date_count)
        return shaped.transpose(0, 3, 4, 1, 2).reshape(date_count, date_count, flat_size)

    return (reorder(real_part), reorder(imag_part))


def inverse_amplitude(data, row_count, col_count):
    energy = box_sum(data[0] * data[0] + data[1] * data[1], row_count, col_count)
    return lax.rsqrt(energy / window_area() + epsilon)


def coherence(real_part, imag_part, left_scale, right_scale):
    factor = left_scale[:, None] * right_scale[None] / window_area()
    return (real_part * factor, imag_part * factor)


def apply_matrix(matrix, vector):
    highest = lax.Precision.HIGHEST
    new_real = jnp.einsum("ijp,jp->ip", matrix[0], vector[0], precision=highest) - jnp.einsum(
        "ijp,jp->ip", matrix[1], vector[1], precision=highest
    )
    new_imag = jnp.einsum("ijp,jp->ip", matrix[0], vector[1], precision=highest) + jnp.einsum(
        "ijp,jp->ip", matrix[1], vector[0], precision=highest
    )
    return (new_real, new_imag)


def apply_adjoint(matrix, vector):
    highest = lax.Precision.HIGHEST
    new_real = jnp.einsum("jip,jp->ip", matrix[0], vector[0], precision=highest) + jnp.einsum(
        "jip,jp->ip", matrix[1], vector[1], precision=highest
    )
    new_imag = jnp.einsum("jip,jp->ip", matrix[0], vector[1], precision=highest) - jnp.einsum(
        "jip,jp->ip", matrix[1], vector[0], precision=highest
    )
    return (new_real, new_imag)


def link_own(row_band, row_count, col_count):
    date_count = row_band.shape[1]
    real_part, imag_part = own_covariance(row_band, row_count, col_count)
    scale_own = inverse_amplitude(row_band, row_count, col_count)
    matrix = coherence(real_part, imag_part, scale_own, scale_own)
    vec_real = jnp.ones(scale_own.shape, jnp.float32)
    vec_imag = jnp.zeros(scale_own.shape, jnp.float32)
    for repeat in range(ITERS):
        new_real, new_imag = apply_matrix(matrix, (vec_real, vec_imag))
        mean_square = jnp.sum(new_real * new_real + new_imag * new_imag, axis=0) / date_count
        factor = lax.rsqrt(mean_square + epsilon)
        vec_real = new_real * factor
        vec_imag = new_imag * factor
    centre = row_band[:, :, HALF : HALF + row_count, HALF : HALF + col_count].reshape(
        2, date_count, row_count * col_count
    )
    root = math.sqrt(date_count)
    comp_real = jnp.sum(vec_real * centre[0] + vec_imag * centre[1], axis=0) / root
    comp_imag = jnp.sum(vec_real * centre[1] - vec_imag * centre[0], axis=0) / root
    return jnp.stack([comp_real, comp_imag])


def link_window(row_band, slot_band, row_count, col_count):
    date_count = row_band.shape[1]
    slot_count = slot_band.shape[1]
    scale_own = inverse_amplitude(row_band, row_count, col_count)
    scale_slot = inverse_amplitude(slot_band, row_count, col_count)
    own_real, own_imag = own_covariance(row_band, row_count, col_count)
    own_matrix = coherence(own_real, own_imag, scale_own, scale_own)
    slot_real, slot_imag = cross_sums(slot_band, slot_band, row_count, col_count)
    slot_matrix = coherence(slot_real, slot_imag, scale_slot, scale_slot)
    mixed_real, mixed_imag = cross_sums(slot_band, row_band, row_count, col_count)
    mixed_matrix = coherence(mixed_real, mixed_imag, scale_slot, scale_own)
    slot_vec = (jnp.ones(scale_slot.shape, jnp.float32), jnp.zeros(scale_slot.shape, jnp.float32))
    own_vec = (jnp.ones(scale_own.shape, jnp.float32), jnp.zeros(scale_own.shape, jnp.float32))
    for repeat in range(ITERS):
        first_term = apply_matrix(slot_matrix, slot_vec)
        second_term = apply_matrix(mixed_matrix, own_vec)
        third_term = apply_adjoint(mixed_matrix, slot_vec)
        fourth_term = apply_matrix(own_matrix, own_vec)
        slot_new = (first_term[0] + second_term[0], first_term[1] + second_term[1])
        own_new = (third_term[0] + fourth_term[0], third_term[1] + fourth_term[1])
        mean_square = (
            jnp.sum(slot_new[0] * slot_new[0] + slot_new[1] * slot_new[1], axis=0)
            + jnp.sum(own_new[0] * own_new[0] + own_new[1] * own_new[1], axis=0)
        ) / (slot_count + date_count)
        factor = lax.rsqrt(mean_square + epsilon)
        slot_vec = (slot_new[0] * factor, slot_new[1] * factor)
        own_vec = (own_new[0] * factor, own_new[1] * factor)
    return jnp.stack([own_vec[0], own_vec[1]])


def body(slc_stack):
    regrouped = lax.all_to_all(slc_stack, "date", split_axis=3, concat_axis=1, tiled=True)
    padded = extended(regrouped, (("date", 3), ("pix", 2)), HALF)
    date_count = padded.shape[1]
    row_count = padded.shape[2] - 2 * HALF
    col_count = padded.shape[3] - 2 * HALF
    band_rows = band_height(row_count, col_count)
    band_count = row_count // band_rows
    positions = jnp.arange(band_count, dtype=jnp.int32)

    def first_band(position):
        return link_own(padded, band_rows, col_count)

    pieces = lax.map(first_band, positions)
    compressed = (
        pieces.reshape(band_count, 2, band_rows, col_count)
        .transpose(1, 0, 2, 3)
        .reshape(2, row_count, col_count)
    )
    bordered = extended(compressed, (("date", 2), ("pix", 1)), HALF)
    slot_count = min(3, lax.axis_size("ms") - 1)
    earlier = [from_behind(bordered, "ms", shift_by) for shift_by in range(1, slot_count + 1)]
    slot_images = jnp.stack(earlier, axis=1)

    def second_band(position):
        return link_window(padded, slot_images, band_rows, col_count)

    linked_pieces = lax.map(second_band, positions)
    linked = (
        linked_pieces.reshape(band_count, 2, date_count, band_rows, col_count)
        .transpose(1, 2, 0, 3, 4)
        .reshape(2, date_count, row_count, col_count)
    )
    restored = lax.all_to_all(linked, "date", split_axis=1, concat_axis=3, tiled=True)
    return (restored, compressed[:, None])


def solution(mesh):
    in_specs = (P(None, ("ms", "date"), "pix", None),)
    out_specs = (P(None, ("ms", "date"), "pix", None), P(None, "ms", "pix", "date"))
    return jax.shard_map(body, mesh=mesh, in_specs=in_specs, out_specs=out_specs, check_vma=False)
```

profile of v0, /device:TPU:0, one launch (start us, length us, event | category | flops | bytes accessed | tf_op | source)
XLA Modules:
  0.0 537.9 jit_solution(6031641294905163451)
XLA Ops:
  2.5 10.1 %all_to_all.36 = f32[4,1,16384]{2,1,0:T(1,128)S(1)} all-to-all(f32[4,1,16384]{2,1,0:T(1,128)S(1)} %reshape.798), channel_id=1, replica_groups=mesh['ms'=2,'date'=4,'pix'=4] {'date'}, dimensions={0} | all-to-all | bytes 524288 | tf_op jit(solution)/shard_map/all_to_all | solution.py:205
  48.8 361.6 %while.25 = (s32[]{:T(128)}, f32[4,32,32,256]{3,1,2,0:T(8,128)}, f32[4,32,32,256]{3,1,2,0:T(8,128)}, s32[4]{0:T(128)S(1)}, f32[42,42,2,32]{1,0,3,2:T(8,128)}, /*...) while((s32[]{:T(128)}, f32[4,32,32,256]{3,1,2,0:T(8,128)}, ...), condition=%wide.region_1.2_spmd, body=%wide.region_0.1_spmd.sunk | while | flops 9377799 | bytes 139076240 | solution.py:110
  53.2 7.1 %multiply_subtract_fusion.3 = (f32[42,42,8,32]{3,2,0,1:T(8,128)S(1)}, f32[42,42,8,32]{3,2,0,1:T(8,128)}) fusion(f32[42,42,32]{2,0,1:T(8,128)} %bitcast.250, f32[42,42,8]{2,0,1:T(8,128)S(1)} %bitcast.257, f32[42,42,32]{2,0,1:T(8,128)} %bitcast.253, f32[42,42,8]{2,0,1:T(8,128)} %bitcast.258), kind=kLoop, calls=%fused_computation.clone.1 | loop fusion | flops 2709504 | bytes 4177152 | tf_op jit(solution)/shard_map/while/body/eval_jaxpr/while/body/eval_jaxpr/sub | solution.py:103
  63.7 8.2 %slice_add_fusion.151 = f32[39,42,8,32]{3,2,0,1:T(8,128)} fusion(f32[41,42,8,32]{3,2,0,1:T(8,128)} %slice_add_fusion.150), kind=kLoop, calls=%fused_computation.4.clone.1 | loop fusion | flops 419328 | bytes 5031936 | tf_op jit(solution)/shard_map/while/body/eval_jaxpr/while/body/eval_jaxpr/add | solution.py:63
  71.9 9.6 %fusion.44 = (f32[35,42,8,32]{3,2,0,1:T(8,128)}, f32[35,42,8,32]{3,2,0,1:T(8,128)}) fusion(f32[39,42,8,32]{3,2,0,1:T(8,128)} %slice_add_fusion.151), kind=kLoop, calls=%fused_computation.262.clone.1 | loop fusion | bytes 6021120 | tf_op jit(solution)/shard_map/while/body/eval_jaxpr/while/body/eval_jaxpr/slice | solution.py:66
  81.5 9.2 %slice_add_fusion.152 = f32[32,42,8,32]{3,2,0,1:T(8,128)} fusion(f32[42,42,8,32]{3,2,0,1:T(8,128)S(1)} %get-tuple-element.303, f32[41,42,8,32]{3,2,0,1:T(8,128)} %slice_add_fusion.150, f32[35,42,8,32]{3,2,0,1:T(8,128)} %get-tuple-element.304, f32[35,42,8,32]{3,2,0,1:T(8,128)} %get-tuple-element.305), kind=kLoop, calls=%fused_computation.6.clone.1 | loop fusion | flops 1032192 | bytes 6881280 | tf_op jit(solution)/shard_map/while/body/eval_jaxpr/while/body/eval_jaxpr/add | solution.py:72
  103.3 8.3 %slice_add_fusion.156 = f32[39,42,8,32]{3,2,0,1:T(8,128)} fusion(f32[41,42,8,32]{3,2,0,1:T(8,128)} %slice_add_fusion.155), kind=kLoop, calls=%fused_computation.5.clone.1 | loop fusion | flops 419328 | bytes 5031936 | tf_op jit(solution)/shard_map/while/body/eval_jaxpr/while/body/eval_jaxpr/add | solution.py:63
  111.6 9.7 %fusion.46 = (f32[35,42,8,32]{3,2,0,1:T(8,128)}, f32[35,42,8,32]{3,2,0,1:T(8,128)}) fusion(f32[39,42,8,32]{3,2,0,1:T(8,128)} %slice_add_fusion.156), kind=kLoop, calls=%fused_computation.263.clone.1 | loop fusion | bytes 6021120 | tf_op jit(solution)/shard_map/while/body/eval_jaxpr/while/body/eval_jaxpr/slice | solution.py:66
  121.3 9.1 %slice_add_fusion.157 = f32[32,42,8,32]{3,2,0,1:T(8,128)} fusion(f32[42,42,8,32]{3,2,0,1:T(8,128)S(1)} %bitcast.256, f32[41,42,8,32]{3,2,0,1:T(8,128)} %slice_add_fusion.155, f32[35,42,8,32]{3,2,0,1:T(8,128)} %get-tuple-element.309, f32[35,42,8,32]{3,2,0,1:T(8,128)} %get-tuple-element.310), kind=kLoop, calls=%fused_computation.9.clone.1 | loop fusion | flops 1032192 | bytes 6881280 | tf_op jit(solution)/shard_map/while/body/eval_jaxpr/while/body/eval_jaxpr/add | solution.py:72
  154.1 8.2 %slice_add_fusion.151 = f32[39,42,8,32]{3,2,0,1:T(8,128)} fusion(f32[41,42,8,32]{3,2,0,1:T(8,128)} %slice_add_fusion.150), kind=kLoop, calls=%fused_computation.4.clone.1 | loop fusion | flops 419328 | bytes 5031936 | tf_op jit(solution)/shard_map/while/body/eval_jaxpr/while/body/eval_jaxpr/add | solution.py:63
  162.3 9.6 %fusion.44 = (f32[35,42,8,32]{3,2,0,1:T(8,128)}, f32[35,42,8,32]{3,2,0,1:T(8,128)}) fusion(f32[39,42,8,32]{3,2,0,1:T(8,128)} %slice_add_fusion.151), kind=kLoop, calls=%fused_computation.262.clone.1 | loop fusion | bytes 6021120 | tf_op jit(solution)/shard_map/while/body/eval_jaxpr/while/body/eval_jaxpr/slice | solution.py:66
  171.9 9.2 %slice_add_fusion.152 = f32[32,42,8,32]{3,2,0,1:T(8,128)} fusion(f32[42,42,8,32]{3,2,0,1:T(8,128)S(1)} %get-tuple-element.303, f32[41,42,8,32]{3,2,0,1:T(8,128)} %slice_add_fusion.150, f32[35,42,8,32]{3,2,0,1:T(8,128)} %get-tuple-element.304, f32[35,42,8,32]{3,2,0,1:T(8,128)} %get-tuple-element.305), kind=kLoop, calls=%fused_computation.6.clone.1 | loop fusion | flops 1032192 | bytes 6881280 | tf_op jit(solution)/shard_map/while/body/eval_jaxpr/while/body/eval_jaxpr/add | solution.py:72
  193.7 8.3 %slice_add_fusion.156 = f32[39,42,8,32]{3,2,0,1:T(8,128)} fusion(f32[41,42,8,32]{3,2,0,1:T(8,128)} %slice_add_fusion.155), kind=kLoop, calls=%fused_computation.5.clone.1 | loop fusion | flops 419328 | bytes 5031936 | tf_op jit(solution)/shard_map/while/body/eval_jaxpr/while/body/eval_jaxpr/add | solution.py:63
  202.0 9.7 %fusion.46 = (f32[35,42,8,32]{3,2,0,1:T(8,128)}, f32[35,42,8,32]{3,2,0,1:T(8,128)}) fusion(f32[39,42,8,32]{3,2,0,1:T(8,128)} %slice_add_fusion.156), kind=kLoop, calls=%fused_computation.263.clone.1 | loop fusion | bytes 6021120 | tf_op jit(solution)/shard_map/while/body/eval_jaxpr/while/body/eval_jaxpr/slice | solution.py:66
  211.7 9.1 %slice_add_fusion.157 = f32[32,42,8,32]{3,2,0,1:T(8,128)} fusion(f32[42,42,8,32]{3,2,0,1:T(8,128)S(1)} %bitcast.256, f32[41,42,8,32]{3,2,0,1:T(8,128)} %slice_add_fusion.155, f32[35,42,8,32]{3,2,0,1:T(8,128)} %get-tuple-element.309, f32[35,42,8,32]{3,2,0,1:T(8,128)} %get-tuple-element.310), kind=kLoop, calls=%fused_computation.9.clone.1 | loop fusion | flops 1032192 | bytes 6881280 | tf_op jit(solution)/shard_map/while/body/eval_jaxpr/while/body/eval_jaxpr/add | solution.py:72
  234.0 7.1 %multiply_subtract_fusion.3 = (f32[42,42,8,32]{3,2,0,1:T(8,128)S(1)}, f32[42,42,8,32]{3,2,0,1:T(8,128)}) fusion(f32[42,42,32]{2,0,1:T(8,128)} %bitcast.250, f32[42,42,8]{2,0,1:T(8,128)S(1)} %bitcast.257, f32[42,42,32]{2,0,1:T(8,128)} %bitcast.253, f32[42,42,8]{2,0,1:T(8,128)} %bitcast.258), kind=kLoop, calls=%fused_computation.clone.1 | loop fusion | flops 2709504 | bytes 4177152 | tf_op jit(solution)/shard_map/while/body/eval_jaxpr/while/body/eval_jaxpr/sub | solution.py:103
  244.5 8.2 %slice_add_fusion.151 = f32[39,42,8,32]{3,2,0,1:T(8,128)} fusion(f32[41,42,8,32]{3,2,0,1:T(8,128)} %slice_add_fusion.150), kind=kLoop, calls=%fused_computation.4.clone.1 | loop fusion | flops 419328 | bytes 5031936 | tf_op jit(solution)/shard_map/while/body/eval_jaxpr/while/body/eval_jaxpr/add | solution.py:63
  252.6 9.6 %fusion.44 = (f32[35,42,8,32]{3,2,0,1:T(8,128)}, f32[35,42,8,32]{3,2,0,1:T(8,128)}) fusion(f32[39,42,8,32]{3,2,0,1:T(8,128)} %slice_add_fusion.151), kind=kLoop, calls=%fused_computation.262.clone.1 | loop fusion | bytes 6021120 | tf_op jit(solution)/shard_map/while/body/eval_jaxpr/while/body/eval_jaxpr/slice | solution.py:66
  262.2 9.2 %slice_add_fusion.152 = f32[32,42,8,32]{3,2,0,1:T(8,128)} fusion(f32[42,42,8,32]{3,2,0,1:T(8,128)S(1)} %get-tuple-element.303, f32[41,42,8,32]{3,2,0,1:T(8,128)} %slice_add_fusion.150, f32[35,42,8,32]{3,2,0,1:T(8,128)} %get-tuple-element.304, f32[35,42,8,32]{3,2,0,1:T(8,128)} %get-tuple-element.305), kind=kLoop, calls=%fused_computation.6.clone.1 | loop fusion | flops 1032192 | bytes 6881280 | tf_op jit(solution)/shard_map/while/body/eval_jaxpr/while/body/eval_jaxpr/add | solution.py:72
  284.0 8.3 %slice_add_fusion.156 = f32[39,42,8,32]{3,2,0,1:T(8,128)} fusion(f32[41,42,8,32]{3,2,0,1:T(8,128)} %slice_add_fusion.155), kind=kLoop, calls=%fused_computation.5.clone.1 | loop fusion | flops 419328 | bytes 5031936 | tf_op jit(solution)/shard_map/while/body/eval_jaxpr/while/body/eval_jaxpr/add | solution.py:63
  292.3 9.7 %fusion.46 = (f32[35,42,8,32]{3,2,0,1:T(8,128)}, f32[35,42,8,32]{3,2,0,1:T(8,128)}) fusion(f32[39,42,8,32]{3,2,0,1:T(8,128)} %slice_add_fusion.156), kind=kLoop, calls=%fused_computation.263.clone.1 | loop fusion | bytes 6021120 | tf_op jit(solution)/shard_map/while/body/eval_jaxpr/while/body/eval_jaxpr/slice | solution.py:66
  302.0 9.1 %slice_add_fusion.157 = f32[32,42,8,32]{3,2,0,1:T(8,128)} fusion(f32[42,42,8,32]{3,2,0,1:T(8,128)S(1)} %bitcast.256, f32[41,42,8,32]{3,2,0,1:T(8,128)} %slice_add_fusion.155, f32[35,42,8,32]{3,2,0,1:T(8,128)} %get-tuple-element.309, f32[35,42,8,32]{3,2,0,1:T(8,128)} %get-tuple-element.310), kind=kLoop, calls=%fused_computation.9.clone.1 | loop fusion | flops 1032192 | bytes 6881280 | tf_op jit(solution)/shard_map/while/body/eval_jaxpr/while/body/eval_jaxpr/add | solution.py:72
  334.8 8.2 %slice_add_fusion.151 = f32[39,42,8,32]{3,2,0,1:T(8,128)} fusion(f32[41,42,8,32]{3,2,0,1:T(8,128)} %slice_add_fusion.150), kind=kLoop, calls=%fused_computation.4.clone.1 | loop fusion | flops 419328 | bytes 5031936 | tf_op jit(solution)/shard_map/while/body/eval_jaxpr/while/body/eval_jaxpr/add | solution.py:63
  343.0 9.6 %fusion.44 = (f32[35,42,8,32]{3,2,0,1:T(8,128)}, f32[35,42,8,32]{3,2,0,1:T(8,128)}) fusion(f32[39,42,8,32]{3,2,0,1:T(8,128)} %slice_add_fusion.151), kind=kLoop, calls=%fused_computation.262.clone.1 | loop fusion | bytes 6021120 | tf_op jit(solution)/shard_map/while/body/eval_jaxpr/while/body/eval_jaxpr/slice | solution.py:66
  352.6 9.2 %slice_add_fusion.152 = f32[32,42,8,32]{3,2,0,1:T(8,128)} fusion(f32[42,42,8,32]{3,2,0,1:T(8,128)S(1)} %get-tuple-element.303, f32[41,42,8,32]{3,2,0,1:T(8,128)} %slice_add_fusion.150, f32[35,42,8,32]{3,2,0,1:T(8,128)} %get-tuple-element.304, f32[35,42,8,32]{3,2,0,1:T(8,128)} %get-tuple-element.305), kind=kLoop, calls=%fused_computation.6.clone.1 | loop fusion | flops 1032192 | bytes 6881280 | tf_op jit(solution)/shard_map/while/body/eval_jaxpr/while/body/eval_jaxpr/add | solution.py:72
  374.4 8.3 %slice_add_fusion.156 = f32[39,42,8,32]{3,2,0,1:T(8,128)} fusion(f32[41,42,8,32]{3,2,0,1:T(8,128)} %slice_add_fusion.155), kind=kLoop, calls=%fused_computation.5.clone.1 | loop fusion | flops 419328 | bytes 5031936 | tf_op jit(solution)/shard_map/while/body/eval_jaxpr/while/body/eval_jaxpr/add | solution.py:63
  382.7 9.7 %fusion.46 = (f32[35,42,8,32]{3,2,0,1:T(8,128)}, f32[35,42,8,32]{3,2,0,1:T(8,128)}) fusion(f32[39,42,8,32]{3,2,0,1:T(8,128)} %slice_add_fusion.156), kind=kLoop, calls=%fused_computation.263.clone.1 | loop fusion | bytes 6021120 | tf_op jit(solution)/shard_map/while/body/eval_jaxpr/while/body/eval_jaxpr/slice | solution.py:66
  392.4 9.1 %slice_add_fusion.157 = f32[32,42,8,32]{3,2,0,1:T(8,128)} fusion(f32[42,42,8,32]{3,2,0,1:T(8,128)S(1)} %bitcast.256, f32[41,42,8,32]{3,2,0,1:T(8,128)} %slice_add_fusion.155, f32[35,42,8,32]{3,2,0,1:T(8,128)} %get-tuple-element.309, f32[35,42,8,32]{3,2,0,1:T(8,128)} %get-tuple-element.310), kind=kLoop, calls=%fused_computation.9.clone.1 | loop fusion | flops 1032192 | bytes 6881280 | tf_op jit(solution)/shard_map/while/body/eval_jaxpr/while/body/eval_jaxpr/add | solution.py:72
  410.4 14.4 %copy.246 = f32[4,32,32,256]{2,1,3,0:T(8,128)} copy(f32[4,32,32,256]{3,1,2,0:T(8,128)} %get-tuple-element.64) | data formatting | bytes 8388608 | tf_op jit(solution)/shard_map/while/body/eval_jaxpr/reshape | solution.py:114
  424.8 14.3 %reshape.715 = f32[32,32,1024]{2,1,0:T(8,128)} reshape(f32[4,8,32,32,32]{4,3,2,1,0:T(8,128)} %bitcast.259) | data formatting | bytes 8388608 | tf_op jit(solution)/shard_map/while/body/eval_jaxpr/reshape | solution.py:115
  444.3 14.4 %copy.245 = f32[4,32,32,256]{2,1,3,0:T(8,128)} copy(f32[4,32,32,256]{3,1,2,0:T(8,128)} %get-tuple-element.63) | data formatting | bytes 8388608 | tf_op jit(solution)/shard_map/while/body/eval_jaxpr/reshape | solution.py:114
  458.8 13.7 %reshape.713 = f32[32,32,1024]{2,1,0:T(8,128)} reshape(f32[4,8,32,32,32]{4,3,2,1,0:T(8,128)} %bitcast.260) | data formatting | bytes 8388608 | tf_op jit(solution)/shard_map/while/body/eval_jaxpr/reshape | solution.py:115
  (273 shorter events, 235.8 us)
Async XLA Ops:
  15.4 5.9 %copy-start.18 = (f32[2,8,32,4,32]{4,3,2,1,0:T(4,128)}, f32[2,8,32,4,32]{4,3,2,1,0:T(4,128)S(1)}, u32[]{:S(2)}) copy-start(f32[2,8,32,4,32]{4,3,2,1,0:T(4,128)S(1)} %copy.244) | copy-start | bytes 786436
  15.6 26.9 %copy-start.9 = (f32[2,4,8,32,32]{4,3,2,1,0:T(8,128)}, f32[2,4,8,32,32]{4,3,2,1,0:T(8,128)S(1)}, u32[]{:S(2)}) copy-start(f32[2,4,8,32,32]{4,3,2,1,0:T(8,128)S(1)} %copy.38) | copy-start | bytes 786436
  18.9 6.2 %collective-permute-start.1 = (f32[2,32,32,5]{2,1,3,0:T(8,128)S(1)}, f32[2,32,32,5]{2,1,3,0:T(8,128)S(1)}, u32[]{:S(2)}, u32[]{:S(2)}) collective-permute-start(f32[2,32,32,5]{2,1,3,0:T(8,128)S(1)} %copy.40), channel_id=1, source_target_pairs={{4,0},{8,4},{12,8},{5,1},{9,5},{13,9},{6,2},{10,6},{14,10},{7,3},{... | collective-permute-start | bytes 122888 | tf_op jit(solution)/shard_map/ppermute | solution.py:25
  21.4 4.4 collective-permute-start
  25.5 17.0 %copy-start.11 = (f32[2,32,32,5]{3,2,1,0:T(8,128)}, f32[2,32,32,5]{3,2,1,0:T(8,128)S(1)}, u32[]{:S(2)}) copy-start(f32[2,32,32,5]{3,2,1,0:T(8,128)S(1)} %copy.42) | copy-start | bytes 122884
  27.3 15.2 %copy-start.13 = (f32[2,32,32,5]{3,2,1,0:T(8,128)}, f32[2,32,32,5]{3,2,1,0:T(8,128)S(1)}, u32[]{:S(2)}) copy-start(f32[2,32,32,5]{3,2,1,0:T(8,128)S(1)} %copy.41) | copy-start | bytes 122884
  27.3 7.7 %copy-start.19 = (f32[2,8,32,4,32]{4,3,2,1,0:T(4,128)S(1)}, f32[2,8,32,4,32]{4,3,2,1,0:T(4,128)}, u32[]{:S(2)}) copy-start(f32[2,8,32,4,32]{4,3,2,1,0:T(4,128)} %copy-done.18) | copy-start | bytes 786436
  28.4 14.1 %collective-permute-start.3 = (f32[2,32,5,42]{3,2,1,0:T(8,128)}, f32[2,32,5,42]{3,2,1,0:T(8,128)S(1)}, u32[]{:S(2)}, u32[]{:S(2)}) collective-permute-start(f32[2,32,5,42]{3,2,1,0:T(8,128)} %get-tuple-element.209), channel_id=1, source_target_pairs={{1,0},{2,1},{3,2},{5,4},{6,5},{7,6},{9,8},{10,9},{11,10},{13,12},{... | collective-permute-start | bytes 161288 | tf_op jit(solution)/shard_map/ppermute | solution.py:25
  29.7 12.8 %collective-permute-start.2 = (f32[2,32,5,42]{3,2,1,0:T(8,128)}, f32[2,32,5,42]{3,2,1,0:T(8,128)}, u32[]{:S(2)}, u32[]{:S(2)}) collective-permute-start(f32[2,32,5,42]{3,2,1,0:T(8,128)} %get-tuple-element.208), channel_id=1, source_target_pairs={{0,1},{1,2},{2,3},{4,5},{5,6},{6,7},{8,9},{9,10},{10,11},{12,13},{... | collective-permute-start | bytes 161288 | tf_op jit(solution)/shard_map/ppermute | solution.py:22
  90.6 9.3 %slice-start = ((s8[7225344]{0:T(1024)(128)(4,1)}), s8[3031040]{0:T(1024)(128)(4,1)S(1)}, s32[]{:S(2)}) async-start(s8[7225344]{0:T(1024)(128)(4,1)} %bitcast.255), calls=%async_computation.2 | async-start | bytes 6062080 | tf_op jit(solution)/shard_map/while/body/eval_jaxpr/while
  95.8 4.1 slice-start.1
  181.0 9.3 %slice-start = ((s8[7225344]{0:T(1024)(128)(4,1)}), s8[3031040]{0:T(1024)(128)(4,1)S(1)}, s32[]{:S(2)}) async-start(s8[7225344]{0:T(1024)(128)(4,1)} %bitcast.255), calls=%async_computation.2 | async-start | bytes 6062080 | tf_op jit(solution)/shard_map/while/body/eval_jaxpr/while
  186.2 4.1 slice-start.1
  271.4 9.3 %slice-start = ((s8[7225344]{0:T(1024)(128)(4,1)}), s8[3031040]{0:T(1024)(128)(4,1)S(1)}, s32[]{:S(2)}) async-start(s8[7225344]{0:T(1024)(128)(4,1)} %bitcast.255), calls=%async_computation.2 | async-start | bytes 6062080 | tf_op jit(solution)/shard_map/while/body/eval_jaxpr/while
  276.6 4.1 slice-start.1
  361.7 9.3 %slice-start = ((s8[7225344]{0:T(1024)(128)(4,1)}), s8[3031040]{0:T(1024)(128)(4,1)S(1)}, s32[]{:S(2)}) async-start(s8[7225344]{0:T(1024)(128)(4,1)} %bitcast.255), calls=%async_computation.2 | async-start | bytes 6062080 | tf_op jit(solution)/shard_map/while/body/eval_jaxpr/while
  366.9 4.1 slice-start.1
  424.8 14.3 %copy-start.10 = (f32[2,4,8,32,32]{4,3,2,1,0:T(8,128)S(1)}, f32[2,4,8,32,32]{4,3,2,1,0:T(8,128)}, u32[]{:S(2)}) copy-start(f32[2,4,8,32,32]{4,3,2,1,0:T(8,128)} %copy-done.9) | copy-start | bytes 786436
  424.8 14.3 %copy-start.12 = (f32[2,32,32,5]{3,2,1,0:T(8,128)S(1)}, f32[2,32,32,5]{3,2,1,0:T(8,128)}, u32[]{:S(2)}) copy-start(f32[2,32,32,5]{3,2,1,0:T(8,128)} %copy-done.11) | copy-start | bytes 122884
  424.8 14.3 %copy-start.14 = (f32[2,32,32,5]{3,2,1,0:T(8,128)S(1)}, f32[2,32,32,5]{3,2,1,0:T(8,128)}, u32[]{:S(2)}) copy-start(f32[2,32,32,5]{3,2,1,0:T(8,128)} %copy-done.13) | copy-start | bytes 122884
  424.8 14.3 %copy-start.21 = (f32[2,32,5,42]{3,2,1,0:T(8,128)S(1)}, f32[2,32,5,42]{3,2,1,0:T(8,128)}, u32[]{:S(2)}) copy-start(f32[2,32,5,42]{3,2,1,0:T(8,128)} %copy-done.20) | copy-start | bytes 161284
  472.5 6.4 %copy-start.3 = (f32[32,32,1024]{2,1,0:T(8,128)S(1)}, f32[32,32,1024]{2,1,0:T(8,128)}, u32[]{:S(2)}) copy-start(f32[32,32,1024]{2,1,0:T(8,128)} %reshape.715) | copy-start | bytes 12582916
  472.5 6.4 %copy-start.5 = (f32[32,32,1024]{2,1,0:T(8,128)S(1)}, f32[32,32,1024]{2,1,0:T(8,128)}, u32[]{:S(2)}) copy-start(f32[32,32,1024]{2,1,0:T(8,128)} %reshape.713) | copy-start | bytes 12582916
  482.4 22.4 %copy-start.17 = (f32[2,32,42,42]{3,2,1,0:T(8,128)S(1)}, f32[2,32,42,42]{3,2,1,0:T(8,128)}, u32[]{:S(2)}) copy-start(f32[2,32,42,42]{3,2,1,0:T(8,128)} %copy-done.16) | copy-start | bytes 1354756
  486.4 5.0 collective-permute-start.5
  487.7 4.6 collective-permute-start.4
  492.4 5.8 %collective-permute-start.7 = (f32[2,5,42]{2,1,0:T(8,128)S(1)}, f32[2,5,42]{2,1,0:T(8,128)S(1)}, u32[]{:S(2)}, u32[]{:S(2)}) collective-permute-start(f32[2,5,42]{2,1,0:T(8,128)S(1)} %get-tuple-element.225), channel_id=1, source_target_pairs={{1,0},{2,1},{3,2},{5,4},{6,5},{7,6},{9,8},{10,9},{11,10},{13,12},{... | collective-permute-start | bytes 5048 | tf_op jit(solution)/shard_map/ppermute | solution.py:25
  493.6 5.9 %collective-permute-start.6 = (f32[2,5,42]{2,1,0:T(8,128)S(1)}, f32[2,5,42]{2,1,0:T(8,128)S(1)}, u32[]{:S(2)}, u32[]{:S(2)}) collective-permute-start(f32[2,5,42]{2,1,0:T(8,128)S(1)} %get-tuple-element.224), channel_id=1, source_target_pairs={{0,1},{1,2},{2,3},{4,5},{5,6},{6,7},{8,9},{9,10},{10,11},{12,13},{... | collective-permute-start | bytes 5048 | tf_op jit(solution)/shard_map/ppermute | solution.py:22
  499.6 5.1 collective-permute-start.8
  510.2 5.7 %copy-start.4 = (f32[32,32,1024]{2,1,0:T(8,128)S(1)}, f32[32,32,1024]{2,1,0:T(8,128)}, u32[]{:S(2)}) copy-start(f32[32,32,1024]{2,1,0:T(8,128)} %reshape.715) | copy-start | bytes 12582916
  510.2 5.9 %copy-start.6 = (f32[32,32,1024]{2,1,0:T(8,128)S(1)}, f32[32,32,1024]{2,1,0:T(8,128)}, u32[]{:S(2)}) copy-start(f32[32,32,1024]{2,1,0:T(8,128)} %reshape.713) | copy-start | bytes 12582916
  521.4 12.7 %all-to-all-start.1 = ((f32[4,1,16384]{2,1,0:T(1,128)}), f32[4,1,16384]{2,1,0:T(1,128)S(1)}, u32[]{:S(2)}, u32[]{:S(2)}) async-start(f32[4,1,16384]{2,1,0:T(1,128)} %reshape.800), calls=%async_computation.1 | async-start | bytes 524288 | tf_op jit(solution)/shard_map/all_to_all | solution.py:237
  (25 other events, 50.9 us)
where the time goes:
time: 545 us; the launch traced here: 538 us
  other arithmetic  251 us (46%)
  local copies, waits for them, and re-layouts  230 us (42%)
  starting transfers between devices  32.4 us (6%)
  blocking collectives  10.1 us (2%)
  waiting for transfers between devices  9.41 us (2%)
    slice x16, local copies, waits for them, and re-layouts, window_along(): lax.slice_in_dim(quads, 0, length - 7, axis=axis_index)  85.7 us
    add x8, other arithmetic, window_along(): return summed + lax.slice_in_dim(values, 10, 10 + count, axis=axis_index)  73.1 us
    add x16, other arithmetic, window_along(): lax.slice_in_dim(pairs, 0, length - 3, axis=axis_index)  66.9 us
    add x8, local copies, waits for them, and re-layouts, window_along(): return summed + lax.slice_in_dim(values, 10, 10 + count, axis=axis_index)  37 us
    add x16, other arithmetic, window_along(): lax.slice_in_dim(values, 0, length - 1, axis=axis_index)  35.8 us
    reshape x2, local copies, waits for them, and re-layouts, reorder(): part.reshape(block_count, row_count, col_count, date_block, date_count)  28.9 us
    sub x4, other arithmetic, one_block(): left_imag * right_real - left_real * right_imag  28.4 us
    reshape x2, local copies, waits for them, and re-layouts, reorder(): shaped.transpose(0, 3, 4, 1, 2).reshape(date_count, date_count, flat_size)  28 us
  transfers between devices with their start and end apart: 10, of which 5 were waited for; matrix products, arithmetic and copies ran while one was open for 2% of the time, Pallas kernels for 0%

commit v1 on v0

v1 whole, which is shorter than its diff:
```python
import functools
import math

import jax
import jax.numpy as jnp
from jax import lax
from jax.experimental import pallas as pl
from jax.experimental.pallas import tpu as pltpu
from jax.sharding import PartitionSpec as P

HALF = 5
ITERS = 3
WIDTH = 2 * HALF + 1
AREA = float(WIDTH**2)
EPSILON = 1e-06
SUB = 8
LANES = 128
F32 = jnp.float32
BF16 = jnp.bfloat16


def row_sums(values, count):
    suffix = [None] * WIDTH
    running = values[WIDTH - 1]
    suffix[WIDTH - 1] = running
    for row in range(WIDTH - 2, -1, -1):
        running = running + values[row]
        suffix[row] = running
    out = [suffix[0]]
    prefix = None
    for row in range(1, count):
        term = values[WIDTH - 1 + row]
        prefix = term if prefix is None else prefix + term
        out.append(suffix[row] + prefix)
    return out


def put_split(x_ref, row, chunk, value):
    high = value.astype(BF16)
    low = (value - high.astype(F32)).astype(BF16)
    total = x_ref.shape[1] // 2
    x_ref[pl.ds(row, value.shape[0]), pl.ds(chunk * LANES, LANES)] = high
    x_ref[pl.ds(row, value.shape[0]), pl.ds(total + chunk * LANES, LANES)] = low


def products(x_ref, a_ref, other, rows):
    chunks, dates = a_ref.shape[2], a_ref.shape[3]
    for chunk in range(chunks):
        for first in range(0, dates, SUB):
            at = pl.ds(first, SUB)
            real, imag = [], []
            for row in range(rows + 2 * HALF):
                left_real, left_imag = a_ref[row, 0, chunk, at, :], a_ref[row, 1, chunk, at, :]
                right_real, right_imag = other(row, chunk)
                real.append(left_real * right_real + left_imag * right_imag)
                imag.append(left_imag * right_real - left_real * right_imag)
            for c, values in enumerate((real, imag)):
                for row, total in enumerate(row_sums(values, rows)):
                    put_split(x_ref, (row * 2 + c) * dates + first, chunk, total)


def energies(x_ref, a_ref, rows):
    chunks, dates = a_ref.shape[2], a_ref.shape[3]
    for chunk in range(chunks):
        for first in range(0, dates, SUB):
            at = pl.ds(first, SUB)
            values = []
            for row in range(rows + 2 * HALF):
                real, imag = a_ref[row, 0, chunk, at, :], a_ref[row, 1, chunk, at, :]
                values.append(real * real + imag * imag)
            for row, total in enumerate(row_sums(values, rows)):
                put_split(x_ref, row * dates + first, chunk, total)


def across(x_ref, size, band_ref, chunk):
    band = band_ref[:, pl.ds(chunk * LANES, LANES)]
    return jnp.dot(x_ref[0:size, :], band, preferred_element_type=F32)


def matvec(s_ref, v_ref, row, chunk, dates):
    blocks = dates // SUB
    real, imag = [None] * blocks, [None] * blocks
    for q in range(dates):
        v_real, v_imag = v_ref[0, pl.ds(q, 1), :], v_ref[1, pl.ds(q, 1), :]
        for b in range(blocks):
            s_real = s_ref[q, row, chunk, 0, pl.ds(b * SUB, SUB), :]
            s_imag = s_ref[q, row, chunk, 1, pl.ds(b * SUB, SUB), :]
            new_real = s_real * v_real - s_imag * v_imag
            new_imag = s_real * v_imag + s_imag * v_real
            real[b] = new_real if real[b] is None else real[b] + new_real
            imag[b] = new_imag if imag[b] is None else imag[b] + new_imag
    return jnp.concatenate(real, 0), jnp.concatenate(imag, 0)


def total_square(real, imag):
    return jnp.sum(real * real + imag * imag, axis=0, keepdims=True)


def each_row(rows, chunks, one_row):
    for chunk in range(chunks):
        lax.fori_loop(0, rows, functools.partial(one_row, chunk), 0)


def own_kernel(a_ref, band_ref, s_ref, r_ref, w_ref, comp_ref, x_ref, v_ref):
    rows, chunks, dates, _ = r_ref.shape

    energies(x_ref, a_ref, rows)
    for chunk in range(chunks):
        power = across(x_ref, rows * dates, band_ref, chunk)
        scale = lax.rsqrt(power / AREA + EPSILON)
        r_ref[:, chunk] = scale.reshape(rows, dates, LANES)

    def one_date(q, carry):
        def other(row, chunk):
            return a_ref[row, 0, chunk, pl.ds(q, 1), :], a_ref[row, 1, chunk, pl.ds(q, 1), :]

        products(x_ref, a_ref, other, rows)
        for chunk in range(chunks):
            summed = across(x_ref, rows * 2 * dates, band_ref, chunk)
            s_ref[q, :, chunk] = summed.reshape(rows, 2, dates, LANES)
        return carry

    lax.fori_loop(0, dates, one_date, 0)

    def one_row(chunk, row, carry):
        scale = r_ref[row, chunk]
        v_ref[0] = scale
        v_ref[1] = jnp.zeros_like(scale)
        for repeat in range(ITERS):
            real, imag = matvec(s_ref, v_ref, row, chunk, dates)
            real, imag = real * (scale / AREA), imag * (scale / AREA)
            if repeat == 0:
                w_ref[row, chunk, 0] = real
                w_ref[row, chunk, 1] = imag
            factor = lax.rsqrt(total_square(real, imag) / dates + EPSILON)
            real, imag = real * factor, imag * factor
            if repeat < ITERS - 1:
                v_ref[0] = real * scale
                v_ref[1] = imag * scale
        centre_real, centre_imag = a_ref[row + HALF, 0, chunk], a_ref[row + HALF, 1, chunk]
        root = math.sqrt(dates)
        comp_real = jnp.sum(real * centre_real + imag * centre_imag, axis=0, keepdims=True)
        comp_imag = jnp.sum(real * centre_imag - imag * centre_real, axis=0, keepdims=True)
        comp_ref[0, chunk, pl.ds(row, 1), :] = comp_real / root
        comp_ref[1, chunk, pl.ds(row, 1), :] = comp_imag / root
        return carry

    each_row(rows, chunks, one_row)


def window_kernel(
    slots, a_ref, z_ref, band_ref, s_ref, r_ref, w_ref, out_ref, x_ref, m_ref, zz_ref, rz_ref, v_ref, vz_ref
):
    rows, chunks, dates, _ = r_ref.shape

    energies(x_ref, z_ref, rows)
    for chunk in range(chunks):
        power = across(x_ref, rows * SUB, band_ref, chunk)
        rz_ref[:, chunk] = lax.rsqrt(power / AREA + EPSILON).reshape(rows, SUB, LANES)
    for slot in range(slots):

        def other(row, chunk, slot=slot):
            return z_ref[row, 0, chunk, pl.ds(slot, 1), :], z_ref[row, 1, chunk, pl.ds(slot, 1), :]

        products(x_ref, a_ref, other, rows)
        for chunk in range(chunks):
            summed = across(x_ref, rows * 2 * dates, band_ref, chunk)
            m_ref[slot, :, chunk] = summed.reshape(rows, 2, dates, LANES)
        products(x_ref, z_ref, other, rows)
        for chunk in range(chunks):
            summed = across(x_ref, rows * 2 * SUB, band_ref, chunk)
            zz_ref[slot, :, chunk] = summed.reshape(rows, 2, SUB, LANES)

    place = lax.broadcasted_iota(jnp.int32, (SUB, LANES), 0)

    def one_row(chunk, row, carry):
        scale = r_ref[row, chunk]
        scale_z = rz_ref[row, chunk]
        v_ref[0] = scale
        v_ref[1] = jnp.zeros_like(scale)
        vz_ref[0] = scale_z
        vz_ref[1] = jnp.zeros_like(scale_z)
        for repeat in range(ITERS):
            if repeat == 0:
                real, imag = w_ref[row, chunk, 0], w_ref[row, chunk, 1]
            else:
                real, imag = matvec(s_ref, v_ref, row, chunk, dates)
                real, imag = real * (scale / AREA), imag * (scale / AREA)
            add_real, add_imag = jnp.zeros_like(real), jnp.zeros_like(imag)
            z_real, z_imag = jnp.zeros_like(scale_z), jnp.zeros_like(scale_z)
            old_real, old_imag = v_ref[0], v_ref[1]
            for slot in range(slots):
                v_real, v_imag = vz_ref[0, pl.ds(slot, 1), :], vz_ref[1, pl.ds(slot, 1), :]
                m_real, m_imag = m_ref[slot, row, chunk, 0], m_ref[slot, row, chunk, 1]
                add_real = add_real + m_real * v_real - m_imag * v_imag
                add_imag = add_imag + m_real * v_imag + m_imag * v_real
                sum_real = jnp.sum(m_real * old_real + m_imag * old_imag, axis=0, keepdims=True)
                sum_imag = jnp.sum(m_real * old_imag - m_imag * old_real, axis=0, keepdims=True)
                z_real = z_real + jnp.where(place == slot, sum_real, 0.0)
                z_imag = z_imag + jnp.where(place == slot, sum_imag, 0.0)
                zz_real, zz_imag = zz_ref[slot, row, chunk, 0], zz_ref[slot, row, chunk, 1]
                z_real = z_real + zz_real * v_real - zz_imag * v_imag
                z_imag = z_imag + zz_real * v_imag + zz_imag * v_real
            real = real + add_real * (scale / AREA)
            imag = imag + add_imag * (scale / AREA)
            z_real = jnp.where(place < slots, z_real * (scale_z / AREA), 0.0)
            z_imag = jnp.where(place < slots, z_imag * (scale_z / AREA), 0.0)
            square = total_square(real, imag) + total_square(z_real, z_imag)
            factor = lax.rsqrt(square / (slots + dates) + EPSILON)
            real, imag = real * factor, imag * factor
            if repeat < ITERS - 1:
                v_ref[0] = real * scale
                v_ref[1] = imag * scale
                vz_ref[0] = z_real * factor * scale_z
                vz_ref[1] = z_imag * factor * scale_z
        out_ref[row, chunk, 0] = real
        out_ref[row, chunk, 1] = imag
        return carry

    each_row(rows, chunks, one_row)


def vmem():
    return pl.BlockSpec(memory_space=pltpu.VMEM)


def params(limit=48):
    return pltpu.CompilerParams(vmem_limit_bytes=limit * 2**20)


def link_own(a, band):
    rows, chunks, dates = a.shape[0] - 2 * HALF, a.shape[2], a.shape[3]
    return pl.pallas_call(
        own_kernel,
        out_shape=(
            jax.ShapeDtypeStruct((dates, rows, chunks, 2, dates, LANES), F32),
            jax.ShapeDtypeStruct((rows, chunks, dates, LANES), F32),
            jax.ShapeDtypeStruct((rows, chunks, 2, dates, LANES), F32),
            jax.ShapeDtypeStruct((2, chunks, rows, LANES), F32),
        ),
        in_specs=[vmem()] * 2,
        out_specs=[vmem()] * 4,
        scratch_shapes=[
            pltpu.VMEM((rows * 2 * dates, band.shape[0]), BF16),
            pltpu.VMEM((2, dates, LANES), F32),
        ],
        compiler_params=params(),
        name="link_own",
    )(a, band)


def link_window(a, z, band, s, r, w, slots):
    rows, chunks, dates, _ = r.shape
    return pl.pallas_call(
        functools.partial(window_kernel, slots),
        out_shape=jax.ShapeDtypeStruct((rows, chunks, 2, dates, LANES), F32),
        in_specs=[vmem()] * 6,
        out_specs=vmem(),
        scratch_shapes=[
            pltpu.VMEM((rows * 2 * dates, band.shape[0]), BF16),
            pltpu.VMEM((slots, rows, chunks, 2, dates, LANES), F32),
            pltpu.VMEM((slots, rows, chunks, 2, SUB, LANES), F32),
            pltpu.VMEM((rows, chunks, SUB, LANES), F32),
            pltpu.VMEM((2, dates, LANES), F32),
            pltpu.VMEM((2, SUB, LANES), F32),
        ],
        compiler_params=params(),
        name="link_window",
    )(a, z, band, s, r, w)


def swap(value, step):
    count = lax.axis_size("date")
    return lax.ppermute(value, "date", [(i, i ^ step) for i in range(count)])


def gather_windows(x):
    count, slabs = lax.axis_size("date"), lax.axis_size("pix")
    me = lax.axis_index("date")
    lead = x.transpose(2, 0, 1, 3)
    rows = lead.shape[0] // count
    tall = rows + 2 * HALF
    direct = rows >= HALF and count > 1
    if direct:
        padded = jnp.pad(lead, ((HALF, HALF), (0, 0), (0, 0), (0, 0)))
    else:
        ups = [(k, k + 1) for k in range(slabs - 1)]
        downs = [(b, a) for a, b in ups]
        above = lax.ppermute(lead[-HALF:], "pix", ups)
        below = lax.ppermute(lead[:HALF], "pix", downs)
        padded = jnp.concatenate([above, lead, below], 0)

    def window(target):
        return lax.dynamic_slice_in_dim(padded, target * rows, tall, 0)

    parts = [window(me)] + [swap(window(me ^ step), step) for step in range(1, count)]
    whole = jnp.concatenate(parts, 2)
    if not direct:
        return whole
    edges = []
    for step in range(count):
        up_from = step
        down_from = (step + 1) % count
        pairs = []
        for k in range(slabs):
            if k + 1 < slabs:
                pairs.append((up_from * slabs + k, k + 1))
            if k > 0:
                pairs.append((down_from * slabs + k, (count - 1) * slabs + k - 1))
        sent = jnp.where(me == up_from, lead[-HALF:], lead[:HALF])
        edges.append(lax.ppermute(sent, ("date", "pix"), pairs))
    top = jnp.concatenate([edges[j] for j in range(count)], 2)
    last = count - 1
    bottom = jnp.concatenate([edges[((last ^ j) - 1) % count] for j in range(count)], 2)
    first_rows = jnp.where(me == 0, top, whole[:HALF])
    last_rows = jnp.where(me == last, bottom, whole[-HALF:])
    return jnp.concatenate([first_rows, whole[HALF:-HALF], last_rows], 0)


def earlier_windows(compressed, shift_by):
    stacks, count, slabs = lax.axis_size("ms"), lax.axis_size("date"), lax.axis_size("pix")
    rows = compressed.shape[1]
    reach = -(-HALF // rows)
    blocks = count * slabs

    def index(stack, block):
        k, d = divmod(block, count)
        return (stack * count + d) * slabs + k

    lead = compressed.transpose(1, 0, 2)
    parts = []
    for offset in range(-reach, reach + 1):
        low = max(0, -HALF - offset * rows)
        high = min(rows, rows + HALF - offset * rows)
        pairs = []
        for stack in range(stacks - shift_by):
            for block in range(blocks):
                target = block - offset
                if 0 <= target < blocks:
                    pairs.append((index(stack, block), index(stack + shift_by, target)))
        parts.append(lax.ppermute(lead[low:high], ("ms", "date", "pix"), pairs))
    return jnp.concatenate(parts, 0)


def body(slc_stack):
    count = lax.axis_size("date")
    me = lax.axis_index("date")
    a = gather_windows(slc_stack)
    cols = a.shape[3]
    chunks = cols // LANES
    a = a.reshape(a.shape[:3] + (chunks, LANES)).transpose(0, 1, 3, 2, 4)
    rows = a.shape[0] - 2 * HALF
    places = jnp.arange(cols, dtype=jnp.int32)
    band = (jnp.abs(places[:, None] - places[None, :]) <= HALF).astype(BF16)
    band = jnp.concatenate([band, band], 0)
    s, r, w, compressed = link_own(a, band)
    compressed = compressed.transpose(0, 2, 1, 3).reshape(2, rows, cols)
    slots = min(3, lax.axis_size("ms") - 1)
    z = jnp.stack([earlier_windows(compressed, shift_by) for shift_by in range(1, slots + 1)], 2)
    z = jnp.pad(z, ((0, 0), (0, 0), (0, SUB - slots), (0, 0)))
    z = z.reshape(z.shape[:3] + (chunks, LANES)).transpose(0, 1, 3, 2, 4)
    linked = link_window(a, z, band, s, r, w, slots)
    own = slc_stack.shape[1]
    sent = []
    for j in range(count):
        dates = linked[:, :, :, j * own : (j + 1) * own].transpose(2, 3, 0, 1, 4).reshape(2, own, rows, cols)
        sent.append(jnp.concatenate([dates, compressed[:, None]], 1))
    out = jnp.zeros((2, own + 1, rows * count, cols), F32)
    for step in range(count):
        piece = swap(sent[step], step) if step else sent[0]
        out = lax.dynamic_update_slice_in_dim(out, piece, (me ^ step) * rows, 2)
    width = cols // count
    mine = lax.dynamic_slice_in_dim(out[:, own:], me * width, width, 3)
    return (out[:, :own], mine)


def solution(mesh):
    in_specs = (P(None, ("ms", "date"), "pix", None),)
    out_specs = (P(None, ("ms", "date"), "pix", None), P(None, "ms", "pix", "date"))
    return jax.shard_map(body, mesh=mesh, in_specs=in_specs, out_specs=out_specs, check_vma=False)
```

time: 545 us -> 62 us (0.11); the launches traced: 538 us -> 61.3 us
  other arithmetic: 251 us -> 0.19 us
  local copies, waits for them, and re-layouts: 230 us -> 2.88 us
  Pallas kernels: 0 us -> 23.9 us
  blocking collectives: 10.1 us -> 0 us
  starting transfers between devices: 32.4 us -> 25.6 us
    add x53 -> x0, other arithmetic: 181 us -> none  [the longest x8 73.1 us: window_along(): return summed + lax.slice_in_dim(values, 10, 10 + count, axis=axis_index)]
    slice x28 -> x3, local copies, waits for them, and re-layouts: 98.2 us -> 0.73 us  [the longest x1 0.72 us: body(): return (out[:, :own], mine)]
    reshape x8 -> x1, local copies, waits for them, and re-layouts: 57.5 us -> 0.02 us  [body(): linked[:, :, :, j * own:(j + 1) * own].transpose(2, 3, 0, 1, 4)]
    add x8 -> x0, local copies, waits for them, and re-layouts: 37 us -> none  [window_along(): return summed + lax.slice_in_dim(values, 10, 10 + count, axis=axis_index)]
    sub x5 -> x0, other arithmetic: 28.4 us -> none  [the longest x4 28.4 us: one_block(): left_imag * right_real - left_real * right_imag]
    pallas_call x0 -> x2, Pallas kernels: none -> 23.9 us  [the longest x1 16.8 us: link_own(): pl.pallas_call(own_kernel, out_shape=(jax.ShapeDtypeStruct((dates, rows,...]
    dot_general x8 -> x0, other arithmetic: 22.5 us -> none  [the longest x5 16 us: apply_matrix(): jnp.einsum('ijp,jp->ip', matrix[0], vector[0], precision=highest)]
    while x66 -> x0, local copies, waits for them, and re-layouts: 19.1 us -> none
  transfers between devices with their start and end apart: 10 -> 13, of which waited for: 5 -> 5; matrix products, arithmetic and copies ran while one was open for 2% -> 0% of each run, Pallas kernels for 0% -> 0%
where the time goes in v1:
time: 62 us; the launch traced here: 61.3 us
  starting transfers between devices  25.6 us (41%)
  Pallas kernels  23.9 us (39%)
  waiting for transfers between devices  7.86 us (13%)
  local copies, waits for them, and re-layouts  2.88 us (5%)
  between operations  0.92 us (1%)
    pallas_call x1, Pallas kernels, link_own(): pl.pallas_call(own_kernel, out_shape=(jax.ShapeDtypeStruct((dates, rows,...  16.8 us
    ppermute x6, starting transfers between devices, swap(): return lax.ppermute(value, 'date', [(i, i ^ step) for i in range(count)])  13.1 us
    pallas_call x1, Pallas kernels, link_window(): pl.pallas_call(functools.partial(window_kernel, slots), out_shape=jax.Sha...  7.12 us
    ppermute x3, starting transfers between devices, earlier_windows(): parts.append(lax.ppermute(lead[low:high], ('ms', 'date', 'pix'), pairs))  6.81 us
    ppermute x6, waiting for transfers between devices, swap(): return lax.ppermute(value, 'date', [(i, i ^ step) for i in range(count)])  6.29 us
    ppermute x4, starting transfers between devices, gather_windows(): edges.append(lax.ppermute(sent, ('date', 'pix'), pairs))  5.67 us
  transfers between devices with their start and end apart: 13, of which 5 were waited for; matrix products, arithmetic and copies ran while one was open for 0% of the time, Pallas kernels for 0%

profile of v1, /device:TPU:0, one launch (start us, length us, event | category | flops | bytes accessed | tf_op | source)
XLA Modules:
  0.0 61.3 jit_solution(10923613154077070013)
XLA Ops:
  0.6 1.1 %copy.19 = f32[2,8,32,128]{3,1,0,2:T(8,128)S(1)} copy(f32[2,8,32,128]{3,2,1,0:T(8,128)} %param.1) | data formatting | bytes 524288 | tf_op args[0]
  1.8 0.1 pad_dynamic-slice_fusion.3
  1.9 0.5 collective-permute-start.4
  2.4 2.6 %collective-permute-start.5 = (f32[18,2,8,128]{3,2,1,0:T(8,128)S(1)}, f32[18,2,8,128]{3,2,1,0:T(8,128)S(1)}, u32[]{:S(2)}, u32[]{:S(2)}) collective-permute-start(f32[18,2,8,128]{3,2,1,0:T(8,128)S(1)} %get-tuple-element.22), channel_id=1, source_target_pairs={{0,8},{4,12},{8,0},{12,4},{1,9},{5,13},{9,1},{13,5},{2,10},{6,14},... | collective-permute-start | bytes 442376 | tf_op jit(solution)/shard_map/ppermute | solution.py:274
  5.0 0.1 collective-permute-start.6
  5.1 3.7 %collective-permute-start = (f32[5,2,8,128]{3,2,1,0:T(8,128)S(1)}, f32[5,2,8,128]{3,2,1,0:T(8,128)S(1)}, u32[]{:S(2)}, u32[]{:S(2)}) collective-permute-start(f32[5,2,8,128]{3,2,1,0:T(8,128)S(1)} %get-tuple-element.18), channel_id=1, source_target_pairs={{0,1},{1,2},{5,12},{2,3},{6,13},{7,14},{16,17},{17,18},{21,28},{18... | collective-permute-start | bytes 122888 | tf_op jit(solution)/shard_map/ppermute | solution.py:311
  8.8 0.7 %collective-permute-start.1 = (f32[5,2,8,128]{3,2,1,0:T(8,128)S(1)}, f32[5,2,8,128]{3,2,1,0:T(8,128)S(1)}, u32[]{:S(2)}, u32[]{:S(2)}) collective-permute-start(f32[5,2,8,128]{3,2,1,0:T(8,128)S(1)} %get-tuple-element.19), channel_id=1, source_target_pairs={{4,1},{5,2},{9,12},{6,3},{10,13},{11,14},{20,17},{21,18},{25,28},{... | collective-permute-start | bytes 122888 | tf_op jit(solution)/shard_map/ppermute | solution.py:311
  9.5 1.0 %collective-permute-done = f32[5,2,8,128]{3,2,1,0:T(8,128)S(1)} collective-permute-done((f32[5,2,8,128]{3,2,1,0:T(8,128)S(1)}, f32[5,2,8,128]{3,2,1,0:T(8,128)S(1)}, u32[]{:S(2)}, u32[]{:S(2)}) %collective-permute-start) | collective-permute-done | bytes 40992 | tf_op jit(solution)/shard_map/ppermute | solution.py:311
  10.4 0.7 %collective-permute-start.2 = (f32[5,2,8,128]{3,2,1,0:T(8,128)S(1)}, f32[5,2,8,128]{3,2,1,0:T(8,128)S(1)}, u32[]{:S(2)}, u32[]{:S(2)}) collective-permute-start(f32[5,2,8,128]{3,2,1,0:T(8,128)S(1)} %get-tuple-element.16), channel_id=1, source_target_pairs={{8,1},{9,2},{13,12},{10,3},{14,13},{15,14},{24,17},{25,18},{29,28}... | collective-permute-start | bytes 122888 | tf_op jit(solution)/shard_map/ppermute | solution.py:311
  11.1 0.0 collective-permute-done.1
  11.1 0.7 %collective-permute-start.3 = (f32[5,2,8,128]{3,2,1,0:T(8,128)S(1)}, f32[5,2,8,128]{3,2,1,0:T(8,128)S(1)}, u32[]{:S(2)}, u32[]{:S(2)}) collective-permute-start(f32[5,2,8,128]{3,2,1,0:T(8,128)S(1)} %get-tuple-element.17), channel_id=1, source_target_pairs={{12,1},{13,2},{1,12},{14,3},{2,13},{3,14},{28,17},{29,18},{17,28},... | collective-permute-start | bytes 122888 | tf_op jit(solution)/shard_map/ppermute | solution.py:311
  11.8 0.0 collective-permute-done.2
  11.8 0.0 collective-permute-done.3
  11.8 0.0 collective-permute-done.4
  11.8 0.5 collective-permute-done.6
  12.4 0.1 fusion.2.a_ref
  12.4 16.8 %link_own.1 = (f32[32,8,1,2,32,128]{5,4,3,2,1,0:T(8,128)}, f32[8,1,32,128]{3,2,1,0:T(8,128)S(1)}, f32[8,1,2,32,128]{4,3,2,1,0:T(8,128)S(1)}, f32[2,1,8,128]{3,2,1,0:T(8,128)S(1)}) custom-call(f32[18,2,1,32,128]{4,3,2,1,0:T(8,128)S(1)} %fusion.2.a_ref, bf16[256,128]{1,0:T(8,128)(2,1)S(1)} %add_convert_fusion.band_ref), custom_call_target="tpu_custom_call" | custom-call | tf_op jit(solution)/shard_map/link_own/pallas_call | solution.py:233
  29.2 3.4 %collective-permute-start.8 = (f32[8,2,128]{2,1,0:T(2,128)S(1)}, f32[8,2,128]{2,1,0:T(2,128)S(1)}, u32[]{:S(2)}, u32[]{:S(2)}) collective-permute-start(f32[8,2,128]{2,1,0:T(2,128)S(1)} %bitcast.32), channel_id=1, source_target_pairs={{0,16},{4,20},{8,24},{12,28},{1,17},{5,21},{9,25},{13,29},{2,18},{... | collective-permute-start | bytes 24584 | tf_op jit(solution)/shard_map/ppermute | solution.py:341
  32.6 2.7 %collective-permute-start.7 = (f32[5,2,128]{2,1,0:T(2,128)S(1)}, f32[5,2,128]{2,1,0:T(2,128)S(1)}, u32[]{:S(2)}, u32[]{:S(2)}) collective-permute-start(f32[5,2,128]{2,1,0:T(2,128)S(1)} %get-tuple-element.28), channel_id=1, source_target_pairs={{0,20},{4,24},{8,28},{12,17},{1,21},{5,25},{9,29},{13,18},{2,22},{... | collective-permute-start | bytes 15368 | tf_op jit(solution)/shard_map/ppermute | solution.py:341
  35.4 0.7 %collective-permute-start.9 = (f32[5,2,128]{2,1,0:T(2,128)S(1)}, f32[5,2,128]{2,1,0:T(2,128)S(1)}, u32[]{:S(2)}, u32[]{:S(2)}) collective-permute-start(f32[5,2,128]{2,1,0:T(2,128)S(1)} %get-tuple-element.29), channel_id=1, source_target_pairs={{4,16},{8,20},{12,24},{1,28},{5,17},{9,21},{13,25},{2,29},{6,18},{... | collective-permute-start | bytes 15368 | tf_op jit(solution)/shard_map/ppermute | solution.py:341
  36.1 0.6 collective-permute-done.7
  36.7 0.0 collective-permute-done.9
  36.7 0.0 collective-permute-done.8
  36.7 7.1 %link_window.1 = f32[8,1,2,32,128]{4,3,2,1,0:T(8,128)S(1)} custom-call(f32[18,2,1,32,128]{4,3,2,1,0:T(8,128)S(1)} %fusion.2.a_ref, f32[18,2,1,8,128]{4,3,2,1,0:T(8,128)S(1)} %pad_bitcast_fusion.z_ref, bf16[256,128]{1,0:T(8,128)(2,1)S(1)} %add_convert_fusion.band_ref, f32[32,8,1,2,32,128]{5,4,3,2,1,0:T(8,128)} %get-tuple-element.7.s_ref, ...), custom_call_target="tpu_custom_call" | custom-call | tf_op jit(solution)/shard_map/link_window/pallas_call | solution.py:254
  43.9 4.3 %collective-permute-start.10 = (f32[2,9,8,128]{3,1,0,2:T(8,128)S(1)}, f32[2,9,8,128]{3,1,0,2:T(8,128)S(1)}, u32[]{:S(2)}, u32[]{:S(2)}) collective-permute-start(f32[2,9,8,128]{3,1,0,2:T(8,128)S(1)} %get-tuple-element.25), channel_id=1, source_target_pairs={{0,4},{4,0},{8,12},{12,8},{1,5},{5,1},{9,13},{13,9},{2,6},{6,2},{1... | collective-permute-start | bytes 221192 | tf_op jit(solution)/shard_map/ppermute | solution.py:274
  48.3 5.6 %collective-permute-start.11 = (f32[2,9,8,128]{3,1,0,2:T(8,128)S(1)}, f32[2,9,8,128]{3,1,0,2:T(8,128)S(1)}, u32[]{:S(2)}, u32[]{:S(2)}) collective-permute-start(f32[2,9,8,128]{3,1,0,2:T(8,128)S(1)} %get-tuple-element.26), channel_id=1, source_target_pairs={{0,8},{4,12},{8,0},{12,4},{1,9},{5,13},{9,1},{13,5},{2,10},{6,14},... | collective-permute-start | bytes 221192 | tf_op jit(solution)/shard_map/ppermute | solution.py:274
  53.8 0.0 collective-permute-start.12
  53.9 0.1 copy_dynamic-update-slice_fusion.3
  54.0 4.1 %collective-permute-done.11 = f32[2,9,8,128]{3,1,0,2:T(8,128)S(1)} collective-permute-done((f32[2,9,8,128]{3,1,0,2:T(8,128)S(1)}, f32[2,9,8,128]{3,1,0,2:T(8,128)S(1)}, u32[]{:S(2)}, u32[]{:S(2)}) %collective-permute-start.11) | collective-permute-done | bytes 73760 | tf_op jit(solution)/shard_map/ppermute | solution.py:274
  58.2 1.7 %collective-permute-done.12 = f32[2,9,8,128]{3,1,0,2:T(8,128)S(1)} collective-permute-done((f32[2,9,8,128]{3,1,0,2:T(8,128)S(1)}, f32[2,9,8,128]{3,1,0,2:T(8,128)S(1)}, u32[]{:S(2)}, u32[]{:S(2)}) %collective-permute-start.12) | collective-permute-done | bytes 73760 | tf_op jit(solution)/shard_map/ppermute | solution.py:274
  59.9 0.7 %slice.66 = f32[2,8,32,128]{3,2,1,0:T(8,128)} slice(f32[2,9,32,128]{3,2,1,0:T(8,128)S(1)} %copy_dynamic-update-slice_fusion), slice={[0:2], [0:8], [0:32], [0:128]} | slice | bytes 524288 | tf_op jit(solution)/shard_map/slice | solution.py:374
  60.6 0.7 %constant_dynamic-slice_fusion = f32[2,1,32,32]{3,2,1,0:T(8,128)} fusion(f32[2,1,32,128]{3,2,1,0:T(8,128)S(1)} %slice.67, s32[]{:T(128)S(6)} %select_n.87), kind=kLoop, calls=%fused_computation.46 | loop fusion | bytes 16388 | tf_op jit(solution)/shard_map/dynamic_slice | solution.py:373
  (18 shorter events, 0.4 us)
Async XLA Ops:
  1.9 9.9 %collective-permute-start.4 = (f32[18,2,8,128]{3,2,1,0:T(8,128)S(1)}, f32[18,2,8,128]{3,2,1,0:T(8,128)S(1)}, u32[]{:S(2)}, u32[]{:S(2)}) collective-permute-start(f32[18,2,8,128]{3,2,1,0:T(8,128)S(1)} %get-tuple-element.21), channel_id=1, source_target_pairs={{0,4},{4,0},{8,12},{12,8},{1,5},{5,1},{9,13},{13,9},{2,6},{6,2},{1... | collective-permute-start | bytes 442376 | tf_op jit(solution)/shard_map/ppermute | solution.py:274
  2.4 9.4 %collective-permute-start.5 = (f32[18,2,8,128]{3,2,1,0:T(8,128)S(1)}, f32[18,2,8,128]{3,2,1,0:T(8,128)S(1)}, u32[]{:S(2)}, u32[]{:S(2)}) collective-permute-start(f32[18,2,8,128]{3,2,1,0:T(8,128)S(1)} %get-tuple-element.22), channel_id=1, source_target_pairs={{0,8},{4,12},{8,0},{12,4},{1,9},{5,13},{9,1},{13,5},{2,10},{6,14},... | collective-permute-start | bytes 442376 | tf_op jit(solution)/shard_map/ppermute | solution.py:274
  5.0 7.3 %collective-permute-start.6 = (f32[18,2,8,128]{3,2,1,0:T(8,128)S(1)}, f32[18,2,8,128]{3,2,1,0:T(8,128)S(1)}, u32[]{:S(2)}, u32[]{:S(2)}) collective-permute-start(f32[18,2,8,128]{3,2,1,0:T(8,128)S(1)} %get-tuple-element.23), channel_id=1, source_target_pairs={{0,12},{4,8},{8,4},{12,0},{1,13},{5,9},{9,5},{13,1},{2,14},{6,10},... | collective-permute-start | bytes 442376 | tf_op jit(solution)/shard_map/ppermute | solution.py:274
  5.1 5.4 %collective-permute-start = (f32[5,2,8,128]{3,2,1,0:T(8,128)S(1)}, f32[5,2,8,128]{3,2,1,0:T(8,128)S(1)}, u32[]{:S(2)}, u32[]{:S(2)}) collective-permute-start(f32[5,2,8,128]{3,2,1,0:T(8,128)S(1)} %get-tuple-element.18), channel_id=1, source_target_pairs={{0,1},{1,2},{5,12},{2,3},{6,13},{7,14},{16,17},{17,18},{21,28},{18... | collective-permute-start | bytes 122888 | tf_op jit(solution)/shard_map/ppermute | solution.py:311
  8.8 2.3 %collective-permute-start.1 = (f32[5,2,8,128]{3,2,1,0:T(8,128)S(1)}, f32[5,2,8,128]{3,2,1,0:T(8,128)S(1)}, u32[]{:S(2)}, u32[]{:S(2)}) collective-permute-start(f32[5,2,8,128]{3,2,1,0:T(8,128)S(1)} %get-tuple-element.19), channel_id=1, source_target_pairs={{4,1},{5,2},{9,12},{6,3},{10,13},{11,14},{20,17},{21,18},{25,28},{... | collective-permute-start | bytes 122888 | tf_op jit(solution)/shard_map/ppermute | solution.py:311
  10.4 1.4 %collective-permute-start.2 = (f32[5,2,8,128]{3,2,1,0:T(8,128)S(1)}, f32[5,2,8,128]{3,2,1,0:T(8,128)S(1)}, u32[]{:S(2)}, u32[]{:S(2)}) collective-permute-start(f32[5,2,8,128]{3,2,1,0:T(8,128)S(1)} %get-tuple-element.16), channel_id=1, source_target_pairs={{8,1},{9,2},{13,12},{10,3},{14,13},{15,14},{24,17},{25,18},{29,28}... | collective-permute-start | bytes 122888 | tf_op jit(solution)/shard_map/ppermute | solution.py:311
  11.1 0.7 %collective-permute-start.3 = (f32[5,2,8,128]{3,2,1,0:T(8,128)S(1)}, f32[5,2,8,128]{3,2,1,0:T(8,128)S(1)}, u32[]{:S(2)}, u32[]{:S(2)}) collective-permute-start(f32[5,2,8,128]{3,2,1,0:T(8,128)S(1)} %get-tuple-element.17), channel_id=1, source_target_pairs={{12,1},{13,2},{1,12},{14,3},{2,13},{3,14},{28,17},{29,18},{17,28},... | collective-permute-start | bytes 122888 | tf_op jit(solution)/shard_map/ppermute | solution.py:311
  29.2 7.5 %collective-permute-start.8 = (f32[8,2,128]{2,1,0:T(2,128)S(1)}, f32[8,2,128]{2,1,0:T(2,128)S(1)}, u32[]{:S(2)}, u32[]{:S(2)}) collective-permute-start(f32[8,2,128]{2,1,0:T(2,128)S(1)} %bitcast.32), channel_id=1, source_target_pairs={{0,16},{4,20},{8,24},{12,28},{1,17},{5,21},{9,25},{13,29},{2,18},{... | collective-permute-start | bytes 24584 | tf_op jit(solution)/shard_map/ppermute | solution.py:341
  32.6 4.0 %collective-permute-start.7 = (f32[5,2,128]{2,1,0:T(2,128)S(1)}, f32[5,2,128]{2,1,0:T(2,128)S(1)}, u32[]{:S(2)}, u32[]{:S(2)}) collective-permute-start(f32[5,2,128]{2,1,0:T(2,128)S(1)} %get-tuple-element.28), channel_id=1, source_target_pairs={{0,20},{4,24},{8,28},{12,17},{1,21},{5,25},{9,29},{13,18},{2,22},{... | collective-permute-start | bytes 15368 | tf_op jit(solution)/shard_map/ppermute | solution.py:341
  35.4 1.3 %collective-permute-start.9 = (f32[5,2,128]{2,1,0:T(2,128)S(1)}, f32[5,2,128]{2,1,0:T(2,128)S(1)}, u32[]{:S(2)}, u32[]{:S(2)}) collective-permute-start(f32[5,2,128]{2,1,0:T(2,128)S(1)} %get-tuple-element.29), channel_id=1, source_target_pairs={{4,16},{8,20},{12,24},{1,28},{5,17},{9,21},{13,25},{2,29},{6,18},{... | collective-permute-start | bytes 15368 | tf_op jit(solution)/shard_map/ppermute | solution.py:341
  43.9 10.0 %collective-permute-start.10 = (f32[2,9,8,128]{3,1,0,2:T(8,128)S(1)}, f32[2,9,8,128]{3,1,0,2:T(8,128)S(1)}, u32[]{:S(2)}, u32[]{:S(2)}) collective-permute-start(f32[2,9,8,128]{3,1,0,2:T(8,128)S(1)} %get-tuple-element.25), channel_id=1, source_target_pairs={{0,4},{4,0},{8,12},{12,8},{1,5},{5,1},{9,13},{13,9},{2,6},{6,2},{1... | collective-permute-start | bytes 221192 | tf_op jit(solution)/shard_map/ppermute | solution.py:274
  48.3 9.9 %collective-permute-start.11 = (f32[2,9,8,128]{3,1,0,2:T(8,128)S(1)}, f32[2,9,8,128]{3,1,0,2:T(8,128)S(1)}, u32[]{:S(2)}, u32[]{:S(2)}) collective-permute-start(f32[2,9,8,128]{3,1,0,2:T(8,128)S(1)} %get-tuple-element.26), channel_id=1, source_target_pairs={{0,8},{4,12},{8,0},{12,4},{1,9},{5,13},{9,1},{13,5},{2,10},{6,14},... | collective-permute-start | bytes 221192 | tf_op jit(solution)/shard_map/ppermute | solution.py:274
  53.8 6.0 %collective-permute-start.12 = (f32[2,9,8,128]{3,1,0,2:T(8,128)S(1)}, f32[2,9,8,128]{3,1,0,2:T(8,128)S(1)}, u32[]{:S(2)}, u32[]{:S(2)}) collective-permute-start(f32[2,9,8,128]{3,1,0,2:T(8,128)S(1)} %get-tuple-element.24), channel_id=1, source_target_pairs={{0,12},{4,8},{8,4},{12,0},{1,13},{5,9},{9,5},{13,1},{2,14},{6,10},... | collective-permute-start | bytes 221192 | tf_op jit(solution)/shard_map/ppermute | solution.py:274

commit v2 on v1

--- a/solution.py
+++ b/solution.py
@@ -35,38 +35,37 @@
     return out
 
 
-def put_split(x_ref, row, chunk, value):
+def put_split(x_ref, at, chunk, value):
     high = value.astype(BF16)
     low = (value - high.astype(F32)).astype(BF16)
     total = x_ref.shape[1] // 2
-    x_ref[pl.ds(row, value.shape[0]), pl.ds(chunk * LANES, LANES)] = high
-    x_ref[pl.ds(row, value.shape[0]), pl.ds(total + chunk * LANES, LANES)] = low
-
-
-def products(x_ref, a_ref, other, rows):
-    chunks, dates = a_ref.shape[2], a_ref.shape[3]
+    x_ref[pl.ds(at, value.shape[0]), pl.ds(chunk * LANES, LANES)] = high
+    x_ref[pl.ds(at, value.shape[0]), pl.ds(total + chunk * LANES, LANES)] = low
+
+
+def products(x_ref, blocks, other, rows, chunks):
     for chunk in range(chunks):
-        for first in range(0, dates, SUB):
+        for place, (ref, first) in enumerate(blocks):
             at = pl.ds(first, SUB)
             real, imag = [], []
             for row in range(rows + 2 * HALF):
-                left_real, left_imag = a_ref[row, 0, chunk, at, :], a_ref[row, 1, chunk, at, :]
+                left_real, left_imag = ref[row, 0, chunk, at, :], ref[row, 1, chunk, at, :]
                 right_real, right_imag = other(row, chunk)
                 real.append(left_real * right_real + left_imag * right_imag)
                 imag.append(left_imag * right_real - left_real * right_imag)
-            for c, values in enumerate((real, imag)):
-                for row, total in enumerate(row_sums(values, rows)):
-                    put_split(x_ref, (row * 2 + c) * dates + first, chunk, total)
-
-
-def energies(x_ref, a_ref, rows):
-    chunks, dates = a_ref.shape[2], a_ref.shape[3]
+            sums = zip(row_sums(real, rows), row_sums(imag, rows))
+            for row, both in enumerate(sums):
+                put_split(x_ref, (row * len(blocks) + place) * 2 * SUB, chunk, jnp.concatenate(both, 0))
+
+
+def energies(x_ref, ref, rows, chunks, dates):
+    step = math.gcd(dates, 2 * SUB)
     for chunk in range(chunks):
-        for first in range(0, dates, SUB):
-            at = pl.ds(first, SUB)
+        for first in range(0, dates, step):
+            at = pl.ds(first, step)
             values = []
             for row in range(rows + 2 * HALF):
-                real, imag = a_ref[row, 0, chunk, at, :], a_ref[row, 1, chunk, at, :]
+                real, imag = ref[row, 0, chunk, at, :], ref[row, 1, chunk, at, :]
                 values.append(real * real + imag * imag)
             for row, total in enumerate(row_sums(values, rows)):
                 put_split(x_ref, row * dates + first, chunk, total)
@@ -77,18 +76,47 @@
     return jnp.dot(x_ref[0:size, :], band, preferred_element_type=F32)
 
 
-def matvec(s_ref, v_ref, row, chunk, dates):
+def spread(ref, *place):
+    return ref[place[:-1] + (pl.ds(place[-1], SUB, stride=0), slice(None))]
+
+
+def accumulate(total, term):
+    return term if total is None else total + term
+
+
+def matvec(s_ref, v_ref, base, dates):
     blocks = dates // SUB
     real, imag = [None] * blocks, [None] * blocks
     for q in range(dates):
-        v_real, v_imag = v_ref[0, pl.ds(q, 1), :], v_ref[1, pl.ds(q, 1), :]
+        v_real, v_imag = spread(v_ref, 0, q), spread(v_ref, 1, q)
         for b in range(blocks):
-            s_real = s_ref[q, row, chunk, 0, pl.ds(b * SUB, SUB), :]
-            s_imag = s_ref[q, row, chunk, 1, pl.ds(b * SUB, SUB), :]
-            new_real = s_real * v_real - s_imag * v_imag
-            new_imag = s_real * v_imag + s_imag * v_real
-            real[b] = new_real if real[b] is None else real[b] + new_real
-            imag[b] = new_imag if imag[b] is None else imag[b] + new_imag
+            at = q * dates + b * SUB
+            s_real = s_ref[pl.ds(base + at, SUB), :]
+            s_imag = s_ref[pl.ds(base + dates * dates + at, SUB), :]
+            real[b] = accumulate(real[b], s_real * v_real - s_imag * v_imag)
+            imag[b] = accumulate(imag[b], s_real * v_imag + s_imag * v_real)
+    return jnp.concatenate(real, 0), jnp.concatenate(imag, 0)
+
+
+def fill_and_apply(s_ref, v_ref, base, dates):
+    blocks = dates // SUB
+    real, imag = [None] * blocks, [None] * blocks
+    half = dates * dates
+    for q in range(dates):
+        v_real = spread(v_ref, 0, q)
+        for b in range(blocks):
+            at = pl.ds(base + q * dates + b * SUB, SUB)
+            at_imag = pl.ds(base + half + q * dates + b * SUB, SUB)
+            if b < q // SUB:
+                turned = base + b * SUB * dates + q
+                s_real = s_ref[pl.ds(turned, SUB, stride=dates), :]
+                s_imag = -s_ref[pl.ds(turned + half, SUB, stride=dates), :]
+                s_ref[at, :] = s_real
+                s_ref[at_imag, :] = s_imag
+            else:
+                s_real, s_imag = s_ref[at, :], s_ref[at_imag, :]
+            real[b] = accumulate(real[b], s_real * v_real)
+            imag[b] = accumulate(imag[b], s_imag * v_real)
     return jnp.concatenate(real, 0), jnp.concatenate(imag, 0)
 
 
@@ -101,33 +129,50 @@
         lax.fori_loop(0, rows, functools.partial(one_row, chunk), 0)
 
 
-def own_kernel(a_ref, band_ref, s_ref, r_ref, w_ref, comp_ref, x_ref, v_ref):
+def own_kernel(a_ref, band_ref, s_ref, r_ref, w_ref, comp_ref, v_ref, *x_refs):
     rows, chunks, dates, _ = r_ref.shape
-
-    energies(x_ref, a_ref, rows)
+    blocks = dates // SUB
+    half = dates * dates
+    group = len(x_refs)
+
+    energies(x_refs[0], a_ref, rows, chunks, dates)
     for chunk in range(chunks):
-        power = across(x_ref, rows * dates, band_ref, chunk)
+        power = across(x_refs[0], rows * dates, band_ref, chunk)
         scale = lax.rsqrt(power / AREA + EPSILON)
         r_ref[:, chunk] = scale.reshape(rows, dates, LANES)
 
-    def one_date(q, carry):
-        def other(row, chunk):
-            return a_ref[row, 0, chunk, pl.ds(q, 1), :], a_ref[row, 1, chunk, pl.ds(q, 1), :]
-
-        products(x_ref, a_ref, other, rows)
-        for chunk in range(chunks):
-            summed = across(x_ref, rows * 2 * dates, band_ref, chunk)
-            s_ref[q, :, chunk] = summed.reshape(rows, 2, dates, LANES)
-        return carry
-
-    lax.fori_loop(0, dates, one_date, 0)
+    for q_block in range(blocks):
+        kept = [(a_ref, b * SUB) for b in range(q_block, blocks)]
+
+        def one_group(turn, carry, q_block=q_block, kept=kept):
+            for u in range(group):
+                q = q_block * SUB + turn * group + u
+
+                def other(row, chunk, q=q):
+                    return spread(a_ref, row, 0, chunk, q), spread(a_ref, row, 1, chunk, q)
+
+                products(x_refs[u], kept, other, rows, chunks)
+                for chunk in range(chunks):
+                    summed = across(x_refs[u], rows * len(kept) * 2 * SUB, band_ref, chunk)
+                    for row in range(rows):
+                        for place, (_, first) in enumerate(kept):
+                            for c in range(2):
+                                value = summed[((row * len(kept) + place) * 2 + c) * SUB :][:SUB]
+                                at = (row * chunks + chunk) * 2 * half + c * half + q * dates + first
+                                s_ref[pl.ds(pl.multiple_of(at, SUB), SUB), :] = value
+            return carry
+
+        lax.fori_loop(0, SUB // group, one_group, 0)
 
     def one_row(chunk, row, carry):
+        base = pl.multiple_of((row * chunks + chunk) * 2 * half, SUB)
         scale = r_ref[row, chunk]
         v_ref[0] = scale
-        v_ref[1] = jnp.zeros_like(scale)
         for repeat in range(ITERS):
-            real, imag = matvec(s_ref, v_ref, row, chunk, dates)
+            if repeat == 0:
+                real, imag = fill_and_apply(s_ref, v_ref, base, dates)
+            else:
+                real, imag = matvec(s_ref, v_ref, base, dates)
             real, imag = real * (scale / AREA), imag * (scale / AREA)
             if repeat == 0:
                 w_ref[row, chunk, 0] = real
@@ -152,28 +197,35 @@
     slots, a_ref, z_ref, band_ref, s_ref, r_ref, w_ref, out_ref, x_ref, m_ref, zz_ref, rz_ref, v_ref, vz_ref
 ):
     rows, chunks, dates, _ = r_ref.shape
-
-    energies(x_ref, z_ref, rows)
+    blocks = dates // SUB
+    half = dates * dates
+
+    energies(x_ref, z_ref, rows, chunks, SUB)
     for chunk in range(chunks):
         power = across(x_ref, rows * SUB, band_ref, chunk)
         rz_ref[:, chunk] = lax.rsqrt(power / AREA + EPSILON).reshape(rows, SUB, LANES)
+    kept = [(a_ref, b * SUB) for b in range(blocks)] + [(z_ref, 0)]
     for slot in range(slots):
 
         def other(row, chunk, slot=slot):
-            return z_ref[row, 0, chunk, pl.ds(slot, 1), :], z_ref[row, 1, chunk, pl.ds(slot, 1), :]
-
-        products(x_ref, a_ref, other, rows)
+            return spread(z_ref, row, 0, chunk, slot), spread(z_ref, row, 1, chunk, slot)
+
+        products(x_ref, kept, other, rows, chunks)
         for chunk in range(chunks):
-            summed = across(x_ref, rows * 2 * dates, band_ref, chunk)
-            m_ref[slot, :, chunk] = summed.reshape(rows, 2, dates, LANES)
-        products(x_ref, z_ref, other, rows)
-        for chunk in range(chunks):
-            summed = across(x_ref, rows * 2 * SUB, band_ref, chunk)
-            zz_ref[slot, :, chunk] = summed.reshape(rows, 2, SUB, LANES)
+            summed = across(x_ref, rows * len(kept) * 2 * SUB, band_ref, chunk)
+            for row in range(rows):
+                for place, (_, first) in enumerate(kept):
+                    for c in range(2):
+                        value = summed[((row * len(kept) + place) * 2 + c) * SUB :][:SUB]
+                        if place < blocks:
+                            m_ref[slot, row, chunk, c, pl.ds(first, SUB), :] = value
+                        else:
+                            zz_ref[slot, row, chunk, c] = value
 
     place = lax.broadcasted_iota(jnp.int32, (SUB, LANES), 0)
 
     def one_row(chunk, row, carry):
+        base = pl.multiple_of((row * chunks + chunk) * 2 * half, SUB)
         scale = r_ref[row, chunk]
         scale_z = rz_ref[row, chunk]
         v_ref[0] = scale
@@ -184,7 +236,7 @@
             if repeat == 0:
                 real, imag = w_ref[row, chunk, 0], w_ref[row, chunk, 1]
             else:
-                real, imag = matvec(s_ref, v_ref, row, chunk, dates)
+                real, imag = matvec(s_ref, v_ref, base, dates)
                 real, imag = real * (scale / AREA), imag * (scale / AREA)
             add_real, add_imag = jnp.zeros_like(real), jnp.zeros_like(imag)
             z_real, z_imag = jnp.zeros_like(scale_z), jnp.zeros_like(scale_z)
@@ -224,26 +276,24 @@
     return pl.BlockSpec(memory_space=pltpu.VMEM)
 
 
-def params(limit=48):
+def params(limit=24):
     return pltpu.CompilerParams(vmem_limit_bytes=limit * 2**20)
 
 
-def link_own(a, band):
+def link_own(a, band, group=4):
     rows, chunks, dates = a.shape[0] - 2 * HALF, a.shape[2], a.shape[3]
     return pl.pallas_call(
         own_kernel,
         out_shape=(
-            jax.ShapeDtypeStruct((dates, rows, chunks, 2, dates, LANES), F32),
+            jax.ShapeDtypeStruct((rows * chunks * 2 * dates * dates, LANES), F32),
             jax.ShapeDtypeStruct((rows, chunks, dates, LANES), F32),
             jax.ShapeDtypeStruct((rows, chunks, 2, dates, LANES), F32),
             jax.ShapeDtypeStruct((2, chunks, rows, LANES), F32),
         ),
         in_specs=[vmem()] * 2,
         out_specs=[vmem()] * 4,
-        scratch_shapes=[
-            pltpu.VMEM((rows * 2 * dates, band.shape[0]), BF16),
-            pltpu.VMEM((2, dates, LANES), F32),
-        ],
+        scratch_shapes=[pltpu.VMEM((2, dates, LANES), F32)]
+        + [pltpu.VMEM((rows * 2 * dates, band.shape[0]), BF16)] * group,
         compiler_params=params(),
         name="link_own",
     )(a, band)
@@ -257,7 +307,7 @@
         in_specs=[vmem()] * 6,
         out_specs=vmem(),
         scratch_shapes=[
-            pltpu.VMEM((rows * 2 * dates, band.shape[0]), BF16),
+            pltpu.VMEM((rows * 2 * (dates + SUB), band.shape[0]), BF16),
             pltpu.VMEM((slots, rows, chunks, 2, dates, LANES), F32),
             pltpu.VMEM((slots, rows, chunks, 2, SUB, LANES), F32),
             pltpu.VMEM((rows, chunks, SUB, LANES), F32),

time: 62 us -> 57.8 us (0.932)
  Pallas kernels: 23.9 us -> 13.1 us
  local copies, waits for them, and re-layouts: 2.88 us -> 9.49 us
    pallas_call x1, Pallas kernels: 16.8 us -> 9.45 us  [link_own(): pl.pallas_call(own_kernel, out_shape=(jax.ShapeDtypeStruct((rows * chunks...]
    unnamed x1 -> x5, local copies, waits for them, and re-layouts: 1.11 us -> 7.72 us
    pallas_call x1, Pallas kernels: 7.12 us -> 3.61 us  [link_window(): pl.pallas_call(functools.partial(window_kernel, slots), out_shape=jax.Sha...]
where the time goes in v2:
time: 57.8 us; the launch traced here: 57.1 us
  starting transfers between devices  25.6 us (44%)
  Pallas kernels  13.1 us (23%)
  local copies, waits for them, and re-layouts  9.49 us (16%)
  waiting for transfers between devices  7.86 us (14%)
  between operations  0.94 us (2%)
    ppermute x6, starting transfers between devices, swap(): return lax.ppermute(value, 'date', [(i, i ^ step) for i in range(count)])  13.1 us
    pallas_call x1, Pallas kernels, link_own(): pl.pallas_call(own_kernel, out_shape=(jax.ShapeDtypeStruct((rows * chunks...  9.45 us
    unnamed x5, local copies, waits for them, and re-layouts  7.72 us
    ppermute x3, starting transfers between devices, earlier_windows(): parts.append(lax.ppermute(lead[low:high], ('ms', 'date', 'pix'), pairs))  6.81 us
    ppermute x6, waiting for transfers between devices, swap(): return lax.ppermute(value, 'date', [(i, i ^ step) for i in range(count)])  6.29 us
    ppermute x4, starting transfers between devices, gather_windows(): edges.append(lax.ppermute(sent, ('date', 'pix'), pairs))  5.67 us
    pallas_call x1, Pallas kernels, link_window(): pl.pallas_call(functools.partial(window_kernel, slots), out_shape=jax.Sha...  3.61 us
  transfers between devices with their start and end apart: 13, of which 5 were waited for; matrix products, arithmetic and copies ran while one was open for 0% of the time, Pallas kernels for 0%

profile of v2, /device:TPU:0, one launch (start us, length us, event | category | flops | bytes accessed | tf_op | source)
XLA Modules:
  0.0 57.1 jit_solution(4327154619273730431)
XLA Ops:
  0.6 1.1 %copy.19 = f32[2,8,32,128]{3,1,0,2:T(8,128)S(1)} copy(f32[2,8,32,128]{3,2,1,0:T(8,128)} %param.1) | data formatting | bytes 524288 | tf_op args[0]
  1.8 0.1 pad_dynamic-slice_fusion.3
  1.9 0.5 collective-permute-start.4
  2.4 2.6 %collective-permute-start.5 = (f32[18,2,8,128]{3,2,1,0:T(8,128)S(1)}, f32[18,2,8,128]{3,2,1,0:T(8,128)S(1)}, u32[]{:S(2)}, u32[]{:S(2)}) collective-permute-start(f32[18,2,8,128]{3,2,1,0:T(8,128)S(1)} %get-tuple-element.22), channel_id=1, source_target_pairs={{0,8},{4,12},{8,0},{12,4},{1,9},{5,13},{9,1},{13,5},{2,10},{6,14},... | collective-permute-start | bytes 442376 | tf_op jit(solution)/shard_map/ppermute | solution.py:324
  5.0 0.1 collective-permute-start.6
  5.1 3.7 %collective-permute-start = (f32[5,2,8,128]{3,2,1,0:T(8,128)S(1)}, f32[5,2,8,128]{3,2,1,0:T(8,128)S(1)}, u32[]{:S(2)}, u32[]{:S(2)}) collective-permute-start(f32[5,2,8,128]{3,2,1,0:T(8,128)S(1)} %get-tuple-element.18), channel_id=1, source_target_pairs={{0,1},{1,2},{5,12},{2,3},{6,13},{7,14},{16,17},{17,18},{21,28},{18... | collective-permute-start | bytes 122888 | tf_op jit(solution)/shard_map/ppermute | solution.py:361
  8.8 0.7 %collective-permute-start.1 = (f32[5,2,8,128]{3,2,1,0:T(8,128)S(1)}, f32[5,2,8,128]{3,2,1,0:T(8,128)S(1)}, u32[]{:S(2)}, u32[]{:S(2)}) collective-permute-start(f32[5,2,8,128]{3,2,1,0:T(8,128)S(1)} %get-tuple-element.19), channel_id=1, source_target_pairs={{4,1},{5,2},{9,12},{6,3},{10,13},{11,14},{20,17},{21,18},{25,28},{... | collective-permute-start | bytes 122888 | tf_op jit(solution)/shard_map/ppermute | solution.py:361
  9.5 1.0 %collective-permute-done = f32[5,2,8,128]{3,2,1,0:T(8,128)S(1)} collective-permute-done((f32[5,2,8,128]{3,2,1,0:T(8,128)S(1)}, f32[5,2,8,128]{3,2,1,0:T(8,128)S(1)}, u32[]{:S(2)}, u32[]{:S(2)}) %collective-permute-start) | collective-permute-done | bytes 40992 | tf_op jit(solution)/shard_map/ppermute | solution.py:361
  10.4 0.7 %collective-permute-start.2 = (f32[5,2,8,128]{3,2,1,0:T(8,128)S(1)}, f32[5,2,8,128]{3,2,1,0:T(8,128)S(1)}, u32[]{:S(2)}, u32[]{:S(2)}) collective-permute-start(f32[5,2,8,128]{3,2,1,0:T(8,128)S(1)} %get-tuple-element.16), channel_id=1, source_target_pairs={{8,1},{9,2},{13,12},{10,3},{14,13},{15,14},{24,17},{25,18},{29,28}... | collective-permute-start | bytes 122888 | tf_op jit(solution)/shard_map/ppermute | solution.py:361
  11.1 0.0 collective-permute-done.1
  11.1 0.7 %collective-permute-start.3 = (f32[5,2,8,128]{3,2,1,0:T(8,128)S(1)}, f32[5,2,8,128]{3,2,1,0:T(8,128)S(1)}, u32[]{:S(2)}, u32[]{:S(2)}) collective-permute-start(f32[5,2,8,128]{3,2,1,0:T(8,128)S(1)} %get-tuple-element.17), channel_id=1, source_target_pairs={{12,1},{13,2},{1,12},{14,3},{2,13},{3,14},{28,17},{29,18},{17,28},... | collective-permute-start | bytes 122888 | tf_op jit(solution)/shard_map/ppermute | solution.py:361
  11.8 0.0 collective-permute-done.3
  11.8 0.5 collective-permute-done.6
  12.4 0.1 fusion.2.a_ref
  12.4 9.5 %link_own.1 = (f32[16384,128]{1,0:T(8,128)S(1)}, f32[8,1,32,128]{3,2,1,0:T(8,128)S(1)}, f32[8,1,2,32,128]{4,3,2,1,0:T(8,128)S(1)}, f32[2,1,8,128]{3,2,1,0:T(8,128)S(1)}) custom-call(f32[18,2,1,32,128]{4,3,2,1,0:T(8,128)S(1)} %fusion.2.a_ref, bf16[256,128]{1,0:T(8,128)(2,1)S(1)} %add_convert_fusion.band_ref), custom_call_target="tpu_custom_call" | custom-call | tf_op jit(solution)/shard_map/link_own/pallas_call | solution.py:285
  21.9 3.2 %copy-done = f32[16384,128]{1,0:T(8,128)} copy-done((f32[16384,128]{1,0:T(8,128)}, f32[16384,128]{1,0:T(8,128)S(1)}, u32[]{:S(2)}) %copy-start) | copy-done | bytes 8388632
  25.1 3.4 %collective-permute-start.8 = (f32[8,2,128]{2,1,0:T(2,128)S(1)}, f32[8,2,128]{2,1,0:T(2,128)S(1)}, u32[]{:S(2)}, u32[]{:S(2)}) collective-permute-start(f32[8,2,128]{2,1,0:T(2,128)S(1)} %bitcast.32), channel_id=1, source_target_pairs={{0,16},{4,20},{8,24},{12,28},{1,17},{5,21},{9,25},{13,29},{2,18},{... | collective-permute-start | bytes 24584 | tf_op jit(solution)/shard_map/ppermute | solution.py:391
  28.6 2.7 %collective-permute-start.7 = (f32[5,2,128]{2,1,0:T(2,128)S(1)}, f32[5,2,128]{2,1,0:T(2,128)S(1)}, u32[]{:S(2)}, u32[]{:S(2)}) collective-permute-start(f32[5,2,128]{2,1,0:T(2,128)S(1)} %get-tuple-element.28), channel_id=1, source_target_pairs={{0,20},{4,24},{8,28},{12,17},{1,21},{5,25},{9,29},{13,18},{2,22},{... | collective-permute-start | bytes 15368 | tf_op jit(solution)/shard_map/ppermute | solution.py:391
  31.3 0.7 %collective-permute-start.9 = (f32[5,2,128]{2,1,0:T(2,128)S(1)}, f32[5,2,128]{2,1,0:T(2,128)S(1)}, u32[]{:S(2)}, u32[]{:S(2)}) collective-permute-start(f32[5,2,128]{2,1,0:T(2,128)S(1)} %get-tuple-element.29), channel_id=1, source_target_pairs={{4,16},{8,20},{12,24},{1,28},{5,17},{9,21},{13,25},{2,29},{6,18},{... | collective-permute-start | bytes 15368 | tf_op jit(solution)/shard_map/ppermute | solution.py:391
  32.0 0.6 %collective-permute-done.7 = f32[5,2,128]{2,1,0:T(2,128)S(1)} collective-permute-done((f32[5,2,128]{2,1,0:T(2,128)S(1)}, f32[5,2,128]{2,1,0:T(2,128)S(1)}, u32[]{:S(2)}, u32[]{:S(2)}) %collective-permute-start.7) | collective-permute-done | bytes 5152 | tf_op jit(solution)/shard_map/ppermute | solution.py:391
  32.6 0.0 collective-permute-done.9
  32.6 0.0 collective-permute-done.8
  32.7 3.4 %copy-done.1 = f32[16384,128]{1,0:T(8,128)S(1)} copy-done((f32[16384,128]{1,0:T(8,128)S(1)}, f32[16384,128]{1,0:T(8,128)}, u32[]{:S(2)}) %copy-start.1) | copy-done | bytes 8388632
  36.1 3.6 %link_window.1 = f32[8,1,2,32,128]{4,3,2,1,0:T(8,128)S(1)} custom-call(f32[18,2,1,32,128]{4,3,2,1,0:T(8,128)S(1)} %fusion.2.a_ref, f32[18,2,1,8,128]{4,3,2,1,0:T(8,128)S(1)} %pad_bitcast_fusion.z_ref, bf16[256,128]{1,0:T(8,128)(2,1)S(1)} %add_convert_fusion.band_ref, f32[16384,128]{1,0:T(8,128)S(1)} %copy-done.1, ...), custom_call_target="tpu_custom_call" | custom-call | tf_op jit(solution)/shard_map/link_window/pallas_call | solution.py:304
  39.8 4.3 %collective-permute-start.10 = (f32[2,9,8,128]{3,1,0,2:T(8,128)S(1)}, f32[2,9,8,128]{3,1,0,2:T(8,128)S(1)}, u32[]{:S(2)}, u32[]{:S(2)}) collective-permute-start(f32[2,9,8,128]{3,1,0,2:T(8,128)S(1)} %get-tuple-element.25), channel_id=1, source_target_pairs={{0,4},{4,0},{8,12},{12,8},{1,5},{5,1},{9,13},{13,9},{2,6},{6,2},{1... | collective-permute-start | bytes 221192 | tf_op jit(solution)/shard_map/ppermute | solution.py:324
  44.1 5.6 %collective-permute-start.11 = (f32[2,9,8,128]{3,1,0,2:T(8,128)S(1)}, f32[2,9,8,128]{3,1,0,2:T(8,128)S(1)}, u32[]{:S(2)}, u32[]{:S(2)}) collective-permute-start(f32[2,9,8,128]{3,1,0,2:T(8,128)S(1)} %get-tuple-element.26), channel_id=1, source_target_pairs={{0,8},{4,12},{8,0},{12,4},{1,9},{5,13},{9,1},{13,5},{2,10},{6,14},... | collective-permute-start | bytes 221192 | tf_op jit(solution)/shard_map/ppermute | solution.py:324
  49.6 0.0 collective-permute-start.12
  49.7 0.1 copy_dynamic-update-slice_fusion.3
  49.8 4.1 %collective-permute-done.11 = f32[2,9,8,128]{3,1,0,2:T(8,128)S(1)} collective-permute-done((f32[2,9,8,128]{3,1,0,2:T(8,128)S(1)}, f32[2,9,8,128]{3,1,0,2:T(8,128)S(1)}, u32[]{:S(2)}, u32[]{:S(2)}) %collective-permute-start.11) | collective-permute-done | bytes 73760 | tf_op jit(solution)/shard_map/ppermute | solution.py:324
  54.0 1.7 %collective-permute-done.12 = f32[2,9,8,128]{3,1,0,2:T(8,128)S(1)} collective-permute-done((f32[2,9,8,128]{3,1,0,2:T(8,128)S(1)}, f32[2,9,8,128]{3,1,0,2:T(8,128)S(1)}, u32[]{:S(2)}, u32[]{:S(2)}) %collective-permute-start.12) | collective-permute-done | bytes 73760 | tf_op jit(solution)/shard_map/ppermute | solution.py:324
  55.7 0.7 %slice.66 = f32[2,8,32,128]{3,2,1,0:T(8,128)} slice(f32[2,9,32,128]{3,2,1,0:T(8,128)S(1)} %copy_dynamic-update-slice_fusion), slice={[0:2], [0:8], [0:32], [0:128]} | slice | bytes 524288 | tf_op jit(solution)/shard_map/slice | solution.py:424
  56.4 0.7 %constant_dynamic-slice_fusion = f32[2,1,32,32]{3,2,1,0:T(8,128)} fusion(f32[2,1,32,128]{3,2,1,0:T(8,128)S(1)} %slice.67, s32[]{:T(128)S(6)} %select_n.87), kind=kLoop, calls=%fused_computation.46 | loop fusion | bytes 16388 | tf_op jit(solution)/shard_map/dynamic_slice | solution.py:423
  (22 shorter events, 0.4 us)
Async XLA Ops:
  1.9 9.9 %collective-permute-start.4 = (f32[18,2,8,128]{3,2,1,0:T(8,128)S(1)}, f32[18,2,8,128]{3,2,1,0:T(8,128)S(1)}, u32[]{:S(2)}, u32[]{:S(2)}) collective-permute-start(f32[18,2,8,128]{3,2,1,0:T(8,128)S(1)} %get-tuple-element.21), channel_id=1, source_target_pairs={{0,4},{4,0},{8,12},{12,8},{1,5},{5,1},{9,13},{13,9},{2,6},{6,2},{1... | collective-permute-start | bytes 442376 | tf_op jit(solution)/shard_map/ppermute | solution.py:324
  2.4 9.4 %collective-permute-start.5 = (f32[18,2,8,128]{3,2,1,0:T(8,128)S(1)}, f32[18,2,8,128]{3,2,1,0:T(8,128)S(1)}, u32[]{:S(2)}, u32[]{:S(2)}) collective-permute-start(f32[18,2,8,128]{3,2,1,0:T(8,128)S(1)} %get-tuple-element.22), channel_id=1, source_target_pairs={{0,8},{4,12},{8,0},{12,4},{1,9},{5,13},{9,1},{13,5},{2,10},{6,14},... | collective-permute-start | bytes 442376 | tf_op jit(solution)/shard_map/ppermute | solution.py:324
  5.0 7.3 %collective-permute-start.6 = (f32[18,2,8,128]{3,2,1,0:T(8,128)S(1)}, f32[18,2,8,128]{3,2,1,0:T(8,128)S(1)}, u32[]{:S(2)}, u32[]{:S(2)}) collective-permute-start(f32[18,2,8,128]{3,2,1,0:T(8,128)S(1)} %get-tuple-element.23), channel_id=1, source_target_pairs={{0,12},{4,8},{8,4},{12,0},{1,13},{5,9},{9,5},{13,1},{2,14},{6,10},... | collective-permute-start | bytes 442376 | tf_op jit(solution)/shard_map/ppermute | solution.py:324
  5.1 5.4 %collective-permute-start = (f32[5,2,8,128]{3,2,1,0:T(8,128)S(1)}, f32[5,2,8,128]{3,2,1,0:T(8,128)S(1)}, u32[]{:S(2)}, u32[]{:S(2)}) collective-permute-start(f32[5,2,8,128]{3,2,1,0:T(8,128)S(1)} %get-tuple-element.18), channel_id=1, source_target_pairs={{0,1},{1,2},{5,12},{2,3},{6,13},{7,14},{16,17},{17,18},{21,28},{18... | collective-permute-start | bytes 122888 | tf_op jit(solution)/shard_map/ppermute | solution.py:361
  8.8 2.3 %collective-permute-start.1 = (f32[5,2,8,128]{3,2,1,0:T(8,128)S(1)}, f32[5,2,8,128]{3,2,1,0:T(8,128)S(1)}, u32[]{:S(2)}, u32[]{:S(2)}) collective-permute-start(f32[5,2,8,128]{3,2,1,0:T(8,128)S(1)} %get-tuple-element.19), channel_id=1, source_target_pairs={{4,1},{5,2},{9,12},{6,3},{10,13},{11,14},{20,17},{21,18},{25,28},{... | collective-permute-start | bytes 122888 | tf_op jit(solution)/shard_map/ppermute | solution.py:361
  10.4 1.4 %collective-permute-start.2 = (f32[5,2,8,128]{3,2,1,0:T(8,128)S(1)}, f32[5,2,8,128]{3,2,1,0:T(8,128)S(1)}, u32[]{:S(2)}, u32[]{:S(2)}) collective-permute-start(f32[5,2,8,128]{3,2,1,0:T(8,128)S(1)} %get-tuple-element.16), channel_id=1, source_target_pairs={{8,1},{9,2},{13,12},{10,3},{14,13},{15,14},{24,17},{25,18},{29,28}... | collective-permute-start | bytes 122888 | tf_op jit(solution)/shard_map/ppermute | solution.py:361
  11.1 0.7 %collective-permute-start.3 = (f32[5,2,8,128]{3,2,1,0:T(8,128)S(1)}, f32[5,2,8,128]{3,2,1,0:T(8,128)S(1)}, u32[]{:S(2)}, u32[]{:S(2)}) collective-permute-start(f32[5,2,8,128]{3,2,1,0:T(8,128)S(1)} %get-tuple-element.17), channel_id=1, source_target_pairs={{12,1},{13,2},{1,12},{14,3},{2,13},{3,14},{28,17},{29,18},{17,28},... | collective-permute-start | bytes 122888 | tf_op jit(solution)/shard_map/ppermute | solution.py:361
  21.9 3.2 %copy-start = (f32[16384,128]{1,0:T(8,128)}, f32[16384,128]{1,0:T(8,128)S(1)}, u32[]{:S(2)}) copy-start(f32[16384,128]{1,0:T(8,128)S(1)} %get-tuple-element.7.s_ref) | copy-start | bytes 25165828
  25.1 7.5 %collective-permute-start.8 = (f32[8,2,128]{2,1,0:T(2,128)S(1)}, f32[8,2,128]{2,1,0:T(2,128)S(1)}, u32[]{:S(2)}, u32[]{:S(2)}) collective-permute-start(f32[8,2,128]{2,1,0:T(2,128)S(1)} %bitcast.32), channel_id=1, source_target_pairs={{0,16},{4,20},{8,24},{12,28},{1,17},{5,21},{9,25},{13,29},{2,18},{... | collective-permute-start | bytes 24584 | tf_op jit(solution)/shard_map/ppermute | solution.py:391
  28.6 4.1 %collective-permute-start.7 = (f32[5,2,128]{2,1,0:T(2,128)S(1)}, f32[5,2,128]{2,1,0:T(2,128)S(1)}, u32[]{:S(2)}, u32[]{:S(2)}) collective-permute-start(f32[5,2,128]{2,1,0:T(2,128)S(1)} %get-tuple-element.28), channel_id=1, source_target_pairs={{0,20},{4,24},{8,28},{12,17},{1,21},{5,25},{9,29},{13,18},{2,22},{... | collective-permute-start | bytes 15368 | tf_op jit(solution)/shard_map/ppermute | solution.py:391
  31.3 1.3 %collective-permute-start.9 = (f32[5,2,128]{2,1,0:T(2,128)S(1)}, f32[5,2,128]{2,1,0:T(2,128)S(1)}, u32[]{:S(2)}, u32[]{:S(2)}) collective-permute-start(f32[5,2,128]{2,1,0:T(2,128)S(1)} %get-tuple-element.29), channel_id=1, source_target_pairs={{4,16},{8,20},{12,24},{1,28},{5,17},{9,21},{13,25},{2,29},{6,18},{... | collective-permute-start | bytes 15368 | tf_op jit(solution)/shard_map/ppermute | solution.py:391
  32.7 3.4 %copy-start.1 = (f32[16384,128]{1,0:T(8,128)S(1)}, f32[16384,128]{1,0:T(8,128)}, u32[]{:S(2)}) copy-start(f32[16384,128]{1,0:T(8,128)} %copy-done) | copy-start | bytes 25165828
  39.8 10.0 %collective-permute-start.10 = (f32[2,9,8,128]{3,1,0,2:T(8,128)S(1)}, f32[2,9,8,128]{3,1,0,2:T(8,128)S(1)}, u32[]{:S(2)}, u32[]{:S(2)}) collective-permute-start(f32[2,9,8,128]{3,1,0,2:T(8,128)S(1)} %get-tuple-element.25), channel_id=1, source_target_pairs={{0,4},{4,0},{8,12},{12,8},{1,5},{5,1},{9,13},{13,9},{2,6},{6,2},{1... | collective-permute-start | bytes 221192 | tf_op jit(solution)/shard_map/ppermute | solution.py:324
  44.1 9.8 %collective-permute-start.11 = (f32[2,9,8,128]{3,1,0,2:T(8,128)S(1)}, f32[2,9,8,128]{3,1,0,2:T(8,128)S(1)}, u32[]{:S(2)}, u32[]{:S(2)}) collective-permute-start(f32[2,9,8,128]{3,1,0,2:T(8,128)S(1)} %get-tuple-element.26), channel_id=1, source_target_pairs={{0,8},{4,12},{8,0},{12,4},{1,9},{5,13},{9,1},{13,5},{2,10},{6,14},... | collective-permute-start | bytes 221192 | tf_op jit(solution)/shard_map/ppermute | solution.py:324
  49.6 6.0 %collective-permute-start.12 = (f32[2,9,8,128]{3,1,0,2:T(8,128)S(1)}, f32[2,9,8,128]{3,1,0,2:T(8,128)S(1)}, u32[]{:S(2)}, u32[]{:S(2)}) collective-permute-start(f32[2,9,8,128]{3,1,0,2:T(8,128)S(1)} %get-tuple-element.24), channel_id=1, source_target_pairs={{0,12},{4,8},{8,4},{12,0},{1,13},{5,9},{9,5},{13,1},{2,14},{6,10},... | collective-permute-start | bytes 221192 | tf_op jit(solution)/shard_map/ppermute | solution.py:324

commit v3 on v2

--- a/solution.py
+++ b/solution.py
@@ -324,47 +324,58 @@
     return lax.ppermute(value, "date", [(i, i ^ step) for i in range(count)])
 
 
-def gather_windows(x):
+def pick(cond, on_true, on_false):
+    return jnp.where(cond, on_true, on_false)
+
+
+def paired_windows(x):
+    slabs = lax.axis_size("pix")
+    me = lax.axis_index("date")
+    near = me < 2
+    even = (me & 1) == 0
+    lead = x.transpose(2, 0, 1, 3)
+    rows = lead.shape[0] // 4
+    reach = 2 * rows + HALF
+    low, high = lead[:reach], lead[-reach:]
+    top, bottom = lead[:HALF], lead[-HALF:]
+    straight, crossed = [], []
+    for core in range(2):
+        for k in range(slabs):
+            if k + 1 < slabs:
+                straight.append((core * slabs + k, core * slabs + k + 1))
+                crossed.append(((2 + core) * slabs + k, core * slabs + k + 1))
+            if k > 0:
+                straight.append(((2 + core) * slabs + k, (2 + core) * slabs + k - 1))
+                crossed.append((core * slabs + k, (2 + core) * slabs + k - 1))
+    edge_own = lax.ppermute(pick(near, bottom, top), ("date", "pix"), straight)
+    edge_far = lax.ppermute(pick(near, top, bottom), ("date", "pix"), crossed)
+    far = swap(pick(near, high, low), 2)
+    own = jnp.concatenate([pick(near, low, high), far], 2)
+    edge = jnp.concatenate([edge_own, edge_far], 2)
+    both = pick(near, jnp.concatenate([edge, own], 0), jnp.concatenate([own, edge], 0))
+    tall = rows + 2 * HALF
+    first, second = both[:tall], both[rows:]
+    other = swap(pick(even, second, first), 1)
+    return jnp.concatenate([pick(even, first, second), other], 2)
+
+
+def plain_windows(x):
     count, slabs = lax.axis_size("date"), lax.axis_size("pix")
-    me = lax.axis_index("date")
+    me = lax.axis_index("date").astype(jnp.uint32)
     lead = x.transpose(2, 0, 1, 3)
     rows = lead.shape[0] // count
     tall = rows + 2 * HALF
-    direct = rows >= HALF and count > 1
-    if direct:
-        padded = jnp.pad(lead, ((HALF, HALF), (0, 0), (0, 0), (0, 0)))
-    else:
-        ups = [(k, k + 1) for k in range(slabs - 1)]
-        downs = [(b, a) for a, b in ups]
-        above = lax.ppermute(lead[-HALF:], "pix", ups)
-        below = lax.ppermute(lead[:HALF], "pix", downs)
-        padded = jnp.concatenate([above, lead, below], 0)
+    ups = [(k, k + 1) for k in range(slabs - 1)]
+    downs = [(b, a) for a, b in ups]
+    above = lax.ppermute(lead[-HALF:], "pix", ups)
+    below = lax.ppermute(lead[:HALF], "pix", downs)
+    padded = jnp.concatenate([above, lead, below], 0)
 
     def window(target):
         return lax.dynamic_slice_in_dim(padded, target * rows, tall, 0)
 
     parts = [window(me)] + [swap(window(me ^ step), step) for step in range(1, count)]
-    whole = jnp.concatenate(parts, 2)
-    if not direct:
-        return whole
-    edges = []
-    for step in range(count):
-        up_from = step
-        down_from = (step + 1) % count
-        pairs = []
-        for k in range(slabs):
-            if k + 1 < slabs:
-                pairs.append((up_from * slabs + k, k + 1))
-            if k > 0:
-                pairs.append((down_from * slabs + k, (count - 1) * slabs + k - 1))
-        sent = jnp.where(me == up_from, lead[-HALF:], lead[:HALF])
-        edges.append(lax.ppermute(sent, ("date", "pix"), pairs))
-    top = jnp.concatenate([edges[j] for j in range(count)], 2)
-    last = count - 1
-    bottom = jnp.concatenate([edges[((last ^ j) - 1) % count] for j in range(count)], 2)
-    first_rows = jnp.where(me == 0, top, whole[:HALF])
-    last_rows = jnp.where(me == last, bottom, whole[-HALF:])
-    return jnp.concatenate([first_rows, whole[HALF:-HALF], last_rows], 0)
+    return jnp.concatenate(parts, 2)
 
 
 def earlier_windows(compressed, shift_by):
@@ -392,17 +403,84 @@
     return jnp.concatenate(parts, 0)
 
 
+def assemble_kernel(offsets, place_ref, *refs):
+    pieces, (out_ref, mine_ref, whole_ref, sem) = refs[: len(offsets)], refs[len(offsets) :]
+    own, rows = out_ref.shape[1], pieces[0].shape[2]
+    copies = []
+    for offset, piece in zip(offsets, pieces):
+        row = pl.multiple_of((place_ref[0] ^ offset) * rows, rows)
+        copy = pltpu.make_async_copy(
+            piece.at[:, pl.ds(0, own)], out_ref.at[:, :, pl.ds(row, rows), :], sem.at[len(copies)]
+        )
+        copy.start()
+        copies.append(copy)
+        whole_ref[:, pl.ds(row, rows), :] = piece[:, own]
+    width = mine_ref.shape[3]
+    cols = whole_ref.shape[2]
+    for c in range(2):
+        rolled = pltpu.roll(whole_ref[c], lax.rem(cols - place_ref[0] * width, cols), 1)
+        mine_ref[c, 0] = rolled[:, :width]
+    for copy in copies:
+        copy.wait()
+
+
+def assemble(pieces, offsets, place, count):
+    _, own, rows, cols = pieces[0].shape
+    own = own - 1
+    return pl.pallas_call(
+        functools.partial(assemble_kernel, offsets),
+        out_shape=(
+            jax.ShapeDtypeStruct((2, own, rows * count, cols), F32),
+            jax.ShapeDtypeStruct((2, 1, rows * count, cols // count), F32),
+        ),
+        in_specs=[pl.BlockSpec(memory_space=pltpu.SMEM)] + [vmem()] * len(pieces),
+        out_specs=(pl.BlockSpec(memory_space=pl.ANY), vmem()),
+        scratch_shapes=[pltpu.VMEM((2, rows * count, cols), F32), pltpu.SemaphoreType.DMA((len(pieces),))],
+        compiler_params=params(8),
+        name="assemble",
+    )(place, *pieces)
+
+
+def scatter(blocks, compressed, me, place):
+    count = lax.axis_size("date")
+    _, own, rows, cols = blocks[0].shape
+    if count == 4 and rows % SUB == 0:
+        image = compressed[:, None]
+        mine, far, sibling, far_sibling = blocks
+        got = swap(jnp.concatenate([far, far_sibling, image], 1), 2)
+        to_send = jnp.stack(
+            [jnp.concatenate([sibling, image], 1), got[:, own:]], 0
+        )
+        near = swap(to_send, 1)
+        pieces = [
+            jnp.concatenate([mine, image], 1),
+            jnp.concatenate([got[:, :own], got[:, 2 * own :]], 1),
+            near[0],
+            near[1],
+        ]
+        return assemble(pieces, (0, 2, 1, 3), place, count)
+    out = jnp.zeros((2, own + 1, rows * count, cols), F32)
+    for step in range(count):
+        piece = jnp.concatenate([blocks[step], compressed[:, None]], 1)
+        piece = swap(piece, step) if step else piece
+        out = lax.dynamic_update_slice_in_dim(out, piece, (me ^ step) * rows, 2)
+    width = cols // count
+    return (out[:, :own], lax.dynamic_slice_in_dim(out[:, own:], me * width, width, 3))
+
+
 def body(slc_stack):
     count = lax.axis_size("date")
-    me = lax.axis_index("date")
-    a = gather_windows(slc_stack)
+    rows = slc_stack.shape[2] // count
+    a = paired_windows(slc_stack) if count == 4 and rows >= HALF else plain_windows(slc_stack)
     cols = a.shape[3]
     chunks = cols // LANES
     a = a.reshape(a.shape[:3] + (chunks, LANES)).transpose(0, 1, 3, 2, 4)
-    rows = a.shape[0] - 2 * HALF
     places = jnp.arange(cols, dtype=jnp.int32)
     band = (jnp.abs(places[:, None] - places[None, :]) <= HALF).astype(BF16)
     band = jnp.concatenate([band, band], 0)
+    me = lax.axis_index("date").astype(jnp.uint32)
+    place = lax.axis_index("date").astype(jnp.int32).reshape(1)
+    a, me, place = lax.optimization_barrier((a, me, place))
     s, r, w, compressed = link_own(a, band)
     compressed = compressed.transpose(0, 2, 1, 3).reshape(2, rows, cols)
     slots = min(3, lax.axis_size("ms") - 1)
@@ -411,17 +489,11 @@
     z = z.reshape(z.shape[:3] + (chunks, LANES)).transpose(0, 1, 3, 2, 4)
     linked = link_window(a, z, band, s, r, w, slots)
     own = slc_stack.shape[1]
-    sent = []
-    for j in range(count):
-        dates = linked[:, :, :, j * own : (j + 1) * own].transpose(2, 3, 0, 1, 4).reshape(2, own, rows, cols)
-        sent.append(jnp.concatenate([dates, compressed[:, None]], 1))
-    out = jnp.zeros((2, own + 1, rows * count, cols), F32)
-    for step in range(count):
-        piece = swap(sent[step], step) if step else sent[0]
-        out = lax.dynamic_update_slice_in_dim(out, piece, (me ^ step) * rows, 2)
-    width = cols // count
-    mine = lax.dynamic_slice_in_dim(out[:, own:], me * width, width, 3)
-    return (out[:, :own], mine)
+    blocks = [
+        linked[:, :, :, j * own : (j + 1) * own].transpose(2, 3, 0, 1, 4).reshape(2, own, rows, cols)
+        for j in range(count)
+    ]
+    return scatter(blocks, compressed, me, place)
 
 
 def solution(mesh):

time: 57.8 us -> 47.2 us (0.82)
  starting transfers between devices: 25.6 us -> 16.5 us
  local copies, waits for them, and re-layouts: 9.49 us -> 1.27 us
  waiting for transfers between devices: 7.86 us -> 13.3 us
  Pallas kernels: 13.1 us -> 14.4 us
    ppermute x6 -> x4, starting transfers between devices: 13.1 us -> 2.88 us  [swap(): return lax.ppermute(value, 'date', [(i, i ^ step) for i in range(count)])]
    unnamed x5 -> x2, local copies, waits for them, and re-layouts: 7.72 us -> 1.11 us
    ppermute x6 -> x4, waiting for transfers between devices: 6.29 us -> 11.1 us  [swap(): return lax.ppermute(value, 'date', [(i, i ^ step) for i in range(count)])]
    ppermute x4 -> x2, starting transfers between devices: 5.67 us -> 8.24 us  [the longest x1 7.58 us: paired_windows(): edge_own = lax.ppermute(pick(near, bottom, top), ('date', 'pix'), straight)]
    ppermute x3, starting transfers between devices: 6.81 us -> 5.35 us  [earlier_windows(): parts.append(lax.ppermute(lead[low:high], ('ms', 'date', 'pix'), pairs))]
    pallas_call x0 -> x1, Pallas kernels: none -> 1.35 us  [assemble(): pl.pallas_call(functools.partial(assemble_kernel, offsets), out_shape=(ja...]
    dynamic_slice x2 -> x0, local copies, waits for them, and re-layouts: 0.79 us -> none  [the longest x1 0.69 us: body(): mine = lax.dynamic_slice_in_dim(out[:, own:], me * width, width, 3)]
    slice x2 -> x3, local copies, waits for them, and re-layouts: 0.72 us -> 0.03 us  [the longest x1 0.02 us: body(): linked[:, :, :, j * own:(j + 1) * own].transpose(2, 3, 0, 1, 4)]
  transfers between devices with their start and end apart: 13 -> 9, of which waited for: 5 -> 6; matrix products, arithmetic and copies ran while one was open for 0% -> 0% of each run, Pallas kernels for 0% -> 0%
where the time goes in v3:
time: 47.2 us; the launch traced here: 46.6 us
  starting transfers between devices  16.5 us (35%)
  Pallas kernels  14.4 us (31%)
  waiting for transfers between devices  13.3 us (28%)
  local copies, waits for them, and re-layouts  1.27 us (3%)
  between operations  0.85 us (2%)
    ppermute x4, waiting for transfers between devices, swap(): return lax.ppermute(value, 'date', [(i, i ^ step) for i in range(count)])  11.1 us
    pallas_call x1, Pallas kernels, link_own(): pl.pallas_call(own_kernel, out_shape=(jax.ShapeDtypeStruct((rows * chunks...  9.45 us
    ppermute x1, starting transfers between devices, paired_windows(): edge_own = lax.ppermute(pick(near, bottom, top), ('date', 'pix'), straight)  7.58 us
    ppermute x3, starting transfers between devices, earlier_windows(): parts.append(lax.ppermute(lead[low:high], ('ms', 'date', 'pix'), pairs))  5.35 us
    pallas_call x1, Pallas kernels, link_window(): pl.pallas_call(functools.partial(window_kernel, slots), out_shape=jax.Sha...  3.62 us
    ppermute x4, starting transfers between devices, swap(): return lax.ppermute(value, 'date', [(i, i ^ step) for i in range(count)])  2.88 us
    ppermute x1, waiting for transfers between devices, paired_windows(): edge_own = lax.ppermute(pick(near, bottom, top), ('date', 'pix'), straight)  1.54 us
    pallas_call x1, Pallas kernels, assemble(): pl.pallas_call(functools.partial(assemble_kernel, offsets), out_shape=(ja...  1.35 us
  transfers between devices with their start and end apart: 9, of which 6 were waited for; matrix products, arithmetic and copies ran while one was open for 0% of the time, Pallas kernels for 0%

profile of v3, /device:TPU:0, one launch (start us, length us, event | category | flops | bytes accessed | tf_op | source)
XLA Modules:
  0.0 46.6 jit_solution(4908977289384546525)
XLA Ops:
  0.6 1.1 %copy.19 = f32[2,8,32,128]{3,1,0,2:T(8,128)S(1)} copy(f32[2,8,32,128]{3,2,1,0:T(8,128)} %param.1) | data formatting | bytes 524288 | tf_op args[0]
  1.8 0.7 %collective-permute-start.1 = (f32[5,2,8,128]{3,2,1,0:T(8,128)S(1)}, f32[5,2,8,128]{3,2,1,0:T(8,128)S(1)}, u32[]{:S(2)}, u32[]{:S(2)}) collective-permute-start(f32[5,2,8,128]{3,2,1,0:T(8,128)S(1)} %get-tuple-element.20), channel_id=1, source_target_pairs={{8,1},{9,2},{1,8},{10,3},{2,9},{3,10},{12,5},{13,6},{5,12},{14,7},... | collective-permute-start | bytes 122888 | tf_op jit(solution)/shard_map/ppermute | solution.py:351
  2.4 7.6 %collective-permute-start = (f32[5,2,8,128]{3,2,1,0:T(8,128)S(1)}, f32[5,2,8,128]{3,2,1,0:T(8,128)S(1)}, u32[]{:S(2)}, u32[]{:S(2)}) collective-permute-start(f32[5,2,8,128]{3,2,1,0:T(8,128)S(1)} %get-tuple-element.21), channel_id=1, source_target_pairs={{0,1},{1,2},{9,8},{2,3},{10,9},{11,10},{4,5},{5,6},{13,12},{6,7},{... | collective-permute-start | bytes 122888 | tf_op jit(solution)/shard_map/ppermute | solution.py:350
  10.1 0.1 collective-permute-start.2
  10.1 1.5 %collective-permute-done = f32[5,2,8,128]{3,2,1,0:T(8,128)S(1)} collective-permute-done((f32[5,2,8,128]{3,2,1,0:T(8,128)S(1)}, f32[5,2,8,128]{3,2,1,0:T(8,128)S(1)}, u32[]{:S(2)}, u32[]{:S(2)}) %collective-permute-start) | collective-permute-done | bytes 40992 | tf_op jit(solution)/shard_map/ppermute | solution.py:350
  11.7 0.0 collective-permute-done.1
  11.7 4.0 %collective-permute-done.2 = f32[21,2,8,128]{3,2,1,0:T(8,128)S(1)} collective-permute-done((f32[21,2,8,128]{3,2,1,0:T(8,128)S(1)}, f32[21,2,8,128]{3,2,1,0:T(8,128)S(1)}, u32[]{:S(2)}, u32[]{:S(2)}) %collective-permute-start.2) | collective-permute-done | bytes 172064 | tf_op jit(solution)/shard_map/ppermute | solution.py:324
  15.7 0.1 slice_select_fusion.1
  15.8 0.1 collective-permute-start.3
  15.9 1.5 %collective-permute-done.3 = f32[18,2,16,128]{3,2,1,0:T(8,128)S(1)} collective-permute-done((f32[18,2,16,128]{3,2,1,0:T(8,128)S(1)}, f32[18,2,16,128]{3,2,1,0:T(8,128)S(1)}, u32[]{:S(2)}, u32[]{:S(2)}) %collective-permute-start.3) | collective-permute-done | bytes 294944 | tf_op jit(solution)/shard_map/ppermute | solution.py:324
  17.4 0.1 maximum_bitcast_fusion.a_ref
  17.5 9.4 %link_own.1 = (f32[16384,128]{1,0:T(8,128)S(1)}, f32[8,1,32,128]{3,2,1,0:T(8,128)S(1)}, f32[8,1,2,32,128]{4,3,2,1,0:T(8,128)S(1)}, f32[2,1,8,128]{3,2,1,0:T(8,128)S(1)}) custom-call(f32[18,2,1,32,128]{4,3,2,1,0:T(8,128)S(1)} %maximum_bitcast_fusion.a_ref, bf16[256,128]{1,0:T(8,128)(2,1)S(1)} %add_convert_fusion.band_ref), custom_call_target="tpu_custom_call" | custom-call | tf_op jit(solution)/shard_map/link_own/pallas_call | solution.py:285
  27.0 3.4 %collective-permute-start.5 = (f32[8,2,128]{2,1,0:T(2,128)S(1)}, f32[8,2,128]{2,1,0:T(2,128)S(1)}, u32[]{:S(2)}, u32[]{:S(2)}) collective-permute-start(f32[8,2,128]{2,1,0:T(2,128)S(1)} %bitcast.41), channel_id=1, source_target_pairs={{0,16},{4,20},{8,24},{12,28},{1,17},{5,21},{9,25},{13,29},{2,18},{... | collective-permute-start | bytes 24584 | tf_op jit(solution)/shard_map/ppermute | solution.py:402
  30.4 1.3 %collective-permute-start.4 = (f32[5,2,128]{2,1,0:T(2,128)S(1)}, f32[5,2,128]{2,1,0:T(2,128)S(1)}, u32[]{:S(2)}, u32[]{:S(2)}) collective-permute-start(f32[5,2,128]{2,1,0:T(2,128)S(1)} %get-tuple-element.28), channel_id=1, source_target_pairs={{0,20},{4,24},{8,28},{12,17},{1,21},{5,25},{9,29},{13,18},{2,22},{... | collective-permute-start | bytes 15368 | tf_op jit(solution)/shard_map/ppermute | solution.py:402
  31.7 0.7 %collective-permute-start.6 = (f32[5,2,128]{2,1,0:T(2,128)S(1)}, f32[5,2,128]{2,1,0:T(2,128)S(1)}, u32[]{:S(2)}, u32[]{:S(2)}) collective-permute-start(f32[5,2,128]{2,1,0:T(2,128)S(1)} %get-tuple-element.29), channel_id=1, source_target_pairs={{4,16},{8,20},{12,24},{1,28},{5,17},{9,21},{13,25},{2,29},{6,18},{... | collective-permute-start | bytes 15368 | tf_op jit(solution)/shard_map/ppermute | solution.py:402
  32.4 0.7 %collective-permute-done.4 = f32[5,2,128]{2,1,0:T(2,128)S(1)} collective-permute-done((f32[5,2,128]{2,1,0:T(2,128)S(1)}, f32[5,2,128]{2,1,0:T(2,128)S(1)}, u32[]{:S(2)}, u32[]{:S(2)}) %collective-permute-start.4) | collective-permute-done | bytes 5152 | tf_op jit(solution)/shard_map/ppermute | solution.py:402
  33.0 0.0 collective-permute-done.6
  33.0 0.0 collective-permute-done.5
  33.1 3.6 %link_window.1 = f32[8,1,2,32,128]{4,3,2,1,0:T(8,128)S(1)} custom-call(f32[18,2,1,32,128]{4,3,2,1,0:T(8,128)S(1)} %maximum_bitcast_fusion.a_ref, f32[18,2,1,8,128]{4,3,2,1,0:T(8,128)S(1)} %pad_bitcast_fusion.z_ref, bf16[256,128]{1,0:T(8,128)(2,1)S(1)} %add_convert_fusion.band_ref, f32[16384,128]{1,0:T(8,128)S(1)} %get-tuple-element.11.s_ref, ...), custom_call_target="tpu_custom_call" | custom-call | tf_op jit(solution)/shard_map/link_window/pallas_call | solution.py:304
  36.8 2.6 %collective-permute-start.7 = (f32[2,17,8,128]{3,2,1,0:T(8,128)S(1)}, f32[2,17,8,128]{3,2,1,0:T(8,128)S(1)}, u32[]{:S(2)}, u32[]{:S(2)}) collective-permute-start(f32[2,17,8,128]{3,2,1,0:T(8,128)S(1)} %pad_maximum_fusion.1), channel_id=1, source_target_pairs={{0,8},{4,12},{8,0},{12,4},{1,9},{5,13},{9,1},{13,5},{2,10},{6,14},... | collective-permute-start | bytes 417800 | tf_op jit(solution)/shard_map/ppermute | solution.py:324
  39.4 4.3 %collective-permute-done.7 = f32[2,17,8,128]{3,2,1,0:T(8,128)S(1)} collective-permute-done((f32[2,17,8,128]{3,2,1,0:T(8,128)S(1)}, f32[2,17,8,128]{3,2,1,0:T(8,128)S(1)}, u32[]{:S(2)}, u32[]{:S(2)}) %collective-permute-start.7) | collective-permute-done | bytes 139296 | tf_op jit(solution)/shard_map/ppermute | solution.py:324
  43.8 0.2 collective-permute-start.8
  44.0 1.2 %collective-permute-done.8 = f32[2,2,9,8,128]{4,3,2,1,0:T(8,128)S(1)} collective-permute-done((f32[2,2,9,8,128]{4,3,2,1,0:T(8,128)S(1)}, f32[2,2,9,8,128]{4,3,2,1,0:T(8,128)S(1)}, u32[]{:S(2)}, u32[]{:S(2)}) %collective-permute-start.8) | collective-permute-done | bytes 147488 | tf_op jit(solution)/shard_map/ppermute | solution.py:324
  45.2 1.3 %assemble.1 = (f32[2,8,32,128]{3,2,1,0:T(8,128)}, f32[2,1,32,32]{3,2,1,0:T(8,128)}) custom-call(s32[1]{0:T(128)} %bitcast.2.place_ref, f32[2,9,8,128]{3,2,1,0:T(8,128)S(1)} %get-tuple-element.27.refs_0_, f32[2,9,8,128]{3,2,1,0:T(8,128)S(1)} %pad_maximum_fusion.4.refs_1_, f32[2,9,8,128]{3,2,1,0:T(8,128)S(1)} %get-tuple-element.25.refs_2_, ...), custom_call_target="tpu_custom_call" | custom-call | tf_op jit(solution)/shard_map/assemble/pallas_call | solution.py:430
  (22 shorter events, 0.3 us)
Async XLA Ops:
  1.8 9.9 %collective-permute-start.1 = (f32[5,2,8,128]{3,2,1,0:T(8,128)S(1)}, f32[5,2,8,128]{3,2,1,0:T(8,128)S(1)}, u32[]{:S(2)}, u32[]{:S(2)}) collective-permute-start(f32[5,2,8,128]{3,2,1,0:T(8,128)S(1)} %get-tuple-element.20), channel_id=1, source_target_pairs={{8,1},{9,2},{1,8},{10,3},{2,9},{3,10},{12,5},{13,6},{5,12},{14,7},... | collective-permute-start | bytes 122888 | tf_op jit(solution)/shard_map/ppermute | solution.py:351
  2.4 9.2 %collective-permute-start = (f32[5,2,8,128]{3,2,1,0:T(8,128)S(1)}, f32[5,2,8,128]{3,2,1,0:T(8,128)S(1)}, u32[]{:S(2)}, u32[]{:S(2)}) collective-permute-start(f32[5,2,8,128]{3,2,1,0:T(8,128)S(1)} %get-tuple-element.21), channel_id=1, source_target_pairs={{0,1},{1,2},{9,8},{2,3},{10,9},{11,10},{4,5},{5,6},{13,12},{6,7},{... | collective-permute-start | bytes 122888 | tf_op jit(solution)/shard_map/ppermute | solution.py:350
  10.1 5.6 %collective-permute-start.2 = (f32[21,2,8,128]{3,2,1,0:T(8,128)S(1)}, f32[21,2,8,128]{3,2,1,0:T(8,128)S(1)}, u32[]{:S(2)}, u32[]{:S(2)}) collective-permute-start(f32[21,2,8,128]{3,2,1,0:T(8,128)S(1)} %get-tuple-element.23), channel_id=1, source_target_pairs={{0,8},{4,12},{8,0},{12,4},{1,9},{5,13},{9,1},{13,5},{2,10},{6,14},... | collective-permute-start | bytes 516104 | tf_op jit(solution)/shard_map/ppermute | solution.py:324
  15.8 1.6 %collective-permute-start.3 = (f32[18,2,16,128]{3,2,1,0:T(8,128)S(1)}, f32[18,2,16,128]{3,2,1,0:T(8,128)S(1)}, u32[]{:S(2)}, u32[]{:S(2)}) collective-permute-start(f32[18,2,16,128]{3,2,1,0:T(8,128)S(1)} %get-tuple-element.15), channel_id=1, source_target_pairs={{0,4},{4,0},{8,12},{12,8},{1,5},{5,1},{9,13},{13,9},{2,6},{6,2},{1... | collective-permute-start | bytes 884744 | tf_op jit(solution)/shard_map/ppermute | solution.py:324
  27.0 6.0 %collective-permute-start.5 = (f32[8,2,128]{2,1,0:T(2,128)S(1)}, f32[8,2,128]{2,1,0:T(2,128)S(1)}, u32[]{:S(2)}, u32[]{:S(2)}) collective-permute-start(f32[8,2,128]{2,1,0:T(2,128)S(1)} %bitcast.41), channel_id=1, source_target_pairs={{0,16},{4,20},{8,24},{12,28},{1,17},{5,21},{9,25},{13,29},{2,18},{... | collective-permute-start | bytes 24584 | tf_op jit(solution)/shard_map/ppermute | solution.py:402
  30.4 2.6 %collective-permute-start.4 = (f32[5,2,128]{2,1,0:T(2,128)S(1)}, f32[5,2,128]{2,1,0:T(2,128)S(1)}, u32[]{:S(2)}, u32[]{:S(2)}) collective-permute-start(f32[5,2,128]{2,1,0:T(2,128)S(1)} %get-tuple-element.28), channel_id=1, source_target_pairs={{0,20},{4,24},{8,28},{12,17},{1,21},{5,25},{9,29},{13,18},{2,22},{... | collective-permute-start | bytes 15368 | tf_op jit(solution)/shard_map/ppermute | solution.py:402
  31.7 1.3 %collective-permute-start.6 = (f32[5,2,128]{2,1,0:T(2,128)S(1)}, f32[5,2,128]{2,1,0:T(2,128)S(1)}, u32[]{:S(2)}, u32[]{:S(2)}) collective-permute-start(f32[5,2,128]{2,1,0:T(2,128)S(1)} %get-tuple-element.29), channel_id=1, source_target_pairs={{4,16},{8,20},{12,24},{1,28},{5,17},{9,21},{13,25},{2,29},{6,18},{... | collective-permute-start | bytes 15368 | tf_op jit(solution)/shard_map/ppermute | solution.py:402
  36.8 7.0 %collective-permute-start.7 = (f32[2,17,8,128]{3,2,1,0:T(8,128)S(1)}, f32[2,17,8,128]{3,2,1,0:T(8,128)S(1)}, u32[]{:S(2)}, u32[]{:S(2)}) collective-permute-start(f32[2,17,8,128]{3,2,1,0:T(8,128)S(1)} %pad_maximum_fusion.1), channel_id=1, source_target_pairs={{0,8},{4,12},{8,0},{12,4},{1,9},{5,13},{9,1},{13,5},{2,10},{6,14},... | collective-permute-start | bytes 417800 | tf_op jit(solution)/shard_map/ppermute | solution.py:324
  43.8 1.4 %collective-permute-start.8 = (f32[2,2,9,8,128]{4,3,2,1,0:T(8,128)S(1)}, f32[2,2,9,8,128]{4,3,2,1,0:T(8,128)S(1)}, u32[]{:S(2)}, u32[]{:S(2)}) collective-permute-start(f32[2,2,9,8,128]{4,3,2,1,0:T(8,128)S(1)} %pad_maximum_fusion), channel_id=1, source_target_pairs={{0,4},{4,0},{8,12},{12,8},{1,5},{5,1},{9,13},{13,9},{2,6},{6,2},{1... | collective-permute-start | bytes 442376 | tf_op jit(solution)/shard_map/ppermute | solution.py:324

commit v4 on v3

--- a/solution.py
+++ b/solution.py
@@ -80,6 +80,10 @@
     return ref[place[:-1] + (pl.ds(place[-1], SUB, stride=0), slice(None))]
 
 
+def pitch(dates):
+    return dates if (dates // SUB) % 2 else dates + SUB
+
+
 def accumulate(total, term):
     return term if total is None else total + term
 
@@ -90,9 +94,9 @@
     for q in range(dates):
         v_real, v_imag = spread(v_ref, 0, q), spread(v_ref, 1, q)
         for b in range(blocks):
-            at = q * dates + b * SUB
+            at = q * pitch(dates) + b * SUB
             s_real = s_ref[pl.ds(base + at, SUB), :]
-            s_imag = s_ref[pl.ds(base + dates * dates + at, SUB), :]
+            s_imag = s_ref[pl.ds(base + dates * pitch(dates) + at, SUB), :]
             real[b] = accumulate(real[b], s_real * v_real - s_imag * v_imag)
             imag[b] = accumulate(imag[b], s_real * v_imag + s_imag * v_real)
     return jnp.concatenate(real, 0), jnp.concatenate(imag, 0)
@@ -101,16 +105,16 @@
 def fill_and_apply(s_ref, v_ref, base, dates):
     blocks = dates // SUB
     real, imag = [None] * blocks, [None] * blocks
-    half = dates * dates
+    half = dates * pitch(dates)
     for q in range(dates):
         v_real = spread(v_ref, 0, q)
         for b in range(blocks):
-            at = pl.ds(base + q * dates + b * SUB, SUB)
-            at_imag = pl.ds(base + half + q * dates + b * SUB, SUB)
+            at = pl.ds(base + q * pitch(dates) + b * SUB, SUB)
+            at_imag = pl.ds(base + half + q * pitch(dates) + b * SUB, SUB)
             if b < q // SUB:
-                turned = base + b * SUB * dates + q
-                s_real = s_ref[pl.ds(turned, SUB, stride=dates), :]
-                s_imag = -s_ref[pl.ds(turned + half, SUB, stride=dates), :]
+                turned = base + b * SUB * pitch(dates) + q
+                s_real = s_ref[pl.ds(turned, SUB, stride=pitch(dates)), :]
+                s_imag = -s_ref[pl.ds(turned + half, SUB, stride=pitch(dates)), :]
                 s_ref[at, :] = s_real
                 s_ref[at_imag, :] = s_imag
             else:
@@ -132,7 +136,7 @@
 def own_kernel(a_ref, band_ref, s_ref, r_ref, w_ref, comp_ref, v_ref, *x_refs):
     rows, chunks, dates, _ = r_ref.shape
     blocks = dates // SUB
-    half = dates * dates
+    half = dates * pitch(dates)
     group = len(x_refs)
 
     energies(x_refs[0], a_ref, rows, chunks, dates)
@@ -158,7 +162,7 @@
                         for place, (_, first) in enumerate(kept):
                             for c in range(2):
                                 value = summed[((row * len(kept) + place) * 2 + c) * SUB :][:SUB]
-                                at = (row * chunks + chunk) * 2 * half + c * half + q * dates + first
+                                at = (row * chunks + chunk) * 2 * half + c * half + q * pitch(dates) + first
                                 s_ref[pl.ds(pl.multiple_of(at, SUB), SUB), :] = value
             return carry
 
@@ -193,22 +197,59 @@
     each_row(rows, chunks, one_row)
 
 
-def window_kernel(
-    slots, a_ref, z_ref, band_ref, s_ref, r_ref, w_ref, out_ref, x_ref, m_ref, zz_ref, rz_ref, v_ref, vz_ref
-):
+def block_of(date, slab):
+    return date ^ (2 * (slab & 1))
+
+
+def fill_window(z_ref, images):
+    centre_ref, sibling_ref, other_ref = images
+    slab, slabs = lax.axis_index("pix"), lax.axis_size("pix")
+    block = block_of(lax.axis_index("date"), slab)
+    even = (block & 1) == 0
+    known = lax.axis_index("ms") > 0
+    inner = known & jnp.logical_not(((slab == 0) & (block == 0)) | ((slab == slabs - 1) & (block == 3)))
+    sibling = jnp.where(known, sibling_ref[...], 0.0)
+    other = jnp.where(inner, other_ref[...], 0.0)
+    z_ref[0] = jnp.where(even, other, sibling)
+    z_ref[1] = jnp.where(known, centre_ref[...], 0.0)
+    z_ref[2] = jnp.where(even, sibling, other)
+
+
+class Row:
+    def __init__(self, z_ref, rows):
+        self.z_ref, self.rows = z_ref, rows
+
+    def __getitem__(self, index):
+        row, c, chunk = index[:3]
+        part, at = divmod(row - HALF + self.rows, self.rows)
+        return spread(self.z_ref, part, c, chunk, at)
+
+
+def window_kernel(slots, paired, *refs):
+    a_ref, band_ref, s_ref, r_ref, w_ref = refs[:5]
     rows, chunks, dates, _ = r_ref.shape
+    count = 3 if paired else 1
+    images = refs[5 : 5 + count]
+    out_ref, x_ref, m_ref, zz_ref, rz_ref, v_ref, vz_ref = refs[5 + count : 12 + count]
     blocks = dates // SUB
-    half = dates * dates
-
-    energies(x_ref, z_ref, rows, chunks, SUB)
-    for chunk in range(chunks):
-        power = across(x_ref, rows * SUB, band_ref, chunk)
-        rz_ref[:, chunk] = lax.rsqrt(power / AREA + EPSILON).reshape(rows, SUB, LANES)
-    kept = [(a_ref, b * SUB) for b in range(blocks)] + [(z_ref, 0)]
+    half = dates * pitch(dates)
+    if paired:
+        fill_window(refs[12 + count], images)
+        z = Row(refs[12 + count], rows)
+    else:
+        z = images[0]
+        energies(x_ref, z, rows, chunks, SUB)
+        for chunk in range(chunks):
+            power = across(x_ref, rows * SUB, band_ref, chunk)
+            rz_ref[:, chunk] = lax.rsqrt(power / AREA + EPSILON).reshape(rows, SUB, LANES)
+
+    kept = [(a_ref, b * SUB) for b in range(blocks)] + [(z, 0)]
     for slot in range(slots):
 
         def other(row, chunk, slot=slot):
-            return spread(z_ref, row, 0, chunk, slot), spread(z_ref, row, 1, chunk, slot)
+            if paired:
+                return z[row, 0, chunk], z[row, 1, chunk]
+            return spread(z, row, 0, chunk, slot), spread(z, row, 1, chunk, slot)
 
         products(x_ref, kept, other, rows, chunks)
         for chunk in range(chunks):
@@ -221,6 +262,8 @@
                             m_ref[slot, row, chunk, c, pl.ds(first, SUB), :] = value
                         else:
                             zz_ref[slot, row, chunk, c] = value
+                            if paired and c == 0:
+                                rz_ref[row, chunk] = lax.rsqrt(value / AREA + EPSILON)
 
     place = lax.broadcasted_iota(jnp.int32, (SUB, LANES), 0)
 
@@ -280,12 +323,12 @@
     return pltpu.CompilerParams(vmem_limit_bytes=limit * 2**20)
 
 
-def link_own(a, band, group=4):
+def link_own(a, band, group=8):
     rows, chunks, dates = a.shape[0] - 2 * HALF, a.shape[2], a.shape[3]
     return pl.pallas_call(
         own_kernel,
         out_shape=(
-            jax.ShapeDtypeStruct((rows * chunks * 2 * dates * dates, LANES), F32),
+            jax.ShapeDtypeStruct((rows * chunks * 2 * dates * pitch(dates), LANES), F32),
             jax.ShapeDtypeStruct((rows, chunks, dates, LANES), F32),
             jax.ShapeDtypeStruct((rows, chunks, 2, dates, LANES), F32),
             jax.ShapeDtypeStruct((2, chunks, rows, LANES), F32),
@@ -299,24 +342,27 @@
     )(a, band)
 
 
-def link_window(a, z, band, s, r, w, slots):
+def link_window(a, images, band, s, r, w, slots, paired):
     rows, chunks, dates, _ = r.shape
+    scratch = [
+        pltpu.VMEM((rows * 2 * (dates + SUB), band.shape[0]), BF16),
+        pltpu.VMEM((slots, rows, chunks, 2, dates, LANES), F32),
+        pltpu.VMEM((slots, rows, chunks, 2, SUB, LANES), F32),
+        pltpu.VMEM((rows, chunks, SUB, LANES), F32),
+        pltpu.VMEM((2, dates, LANES), F32),
+        pltpu.VMEM((2, SUB, LANES), F32),
+    ]
+    if paired:
+        scratch.append(pltpu.VMEM((3, 2, chunks, rows, LANES), F32))
     return pl.pallas_call(
-        functools.partial(window_kernel, slots),
+        functools.partial(window_kernel, slots, paired),
         out_shape=jax.ShapeDtypeStruct((rows, chunks, 2, dates, LANES), F32),
-        in_specs=[vmem()] * 6,
+        in_specs=[vmem()] * (5 + len(images)),
         out_specs=vmem(),
-        scratch_shapes=[
-            pltpu.VMEM((rows * 2 * (dates + SUB), band.shape[0]), BF16),
-            pltpu.VMEM((slots, rows, chunks, 2, dates, LANES), F32),
-            pltpu.VMEM((slots, rows, chunks, 2, SUB, LANES), F32),
-            pltpu.VMEM((rows, chunks, SUB, LANES), F32),
-            pltpu.VMEM((2, dates, LANES), F32),
-            pltpu.VMEM((2, SUB, LANES), F32),
-        ],
+        scratch_shapes=scratch,
         compiler_params=params(),
         name="link_window",
-    )(a, z, band, s, r, w)
+    )(a, band, s, r, w, *images)
 
 
 def swap(value, step):
@@ -328,30 +374,37 @@
     return jnp.where(cond, on_true, on_false)
 
 
+def is_paired(x):
+    return lax.axis_size("ms") == 2 and lax.axis_size("date") == 4 and x.shape[2] % (4 * SUB) == 0
+
+
 def paired_windows(x):
     slabs = lax.axis_size("pix")
-    me = lax.axis_index("date")
-    near = me < 2
-    even = (me & 1) == 0
+    block = block_of(lax.axis_index("date"), lax.axis_index("pix"))
+    near = block < 2
+    even = (block & 1) == 0
     lead = x.transpose(2, 0, 1, 3)
     rows = lead.shape[0] // 4
     reach = 2 * rows + HALF
     low, high = lead[:reach], lead[-reach:]
-    top, bottom = lead[:HALF], lead[-HALF:]
-    straight, crossed = [], []
-    for core in range(2):
+    pairs = []
+    for date in range(4):
         for k in range(slabs):
-            if k + 1 < slabs:
-                straight.append((core * slabs + k, core * slabs + k + 1))
-                crossed.append(((2 + core) * slabs + k, core * slabs + k + 1))
-            if k > 0:
-                straight.append(((2 + core) * slabs + k, (2 + core) * slabs + k - 1))
-                crossed.append((core * slabs + k, (2 + core) * slabs + k - 1))
-    edge_own = lax.ppermute(pick(near, bottom, top), ("date", "pix"), straight)
-    edge_far = lax.ppermute(pick(near, top, bottom), ("date", "pix"), crossed)
+            target = k - 1 if block_of(date, k) < 2 else k + 1
+            if 0 <= target < slabs:
+                pairs.append((date * slabs + k, date * slabs + target))
+            else:
+                pairs.append((date * slabs + k, (date ^ 1) * slabs + k))
+    outer = pick(near, lax.axis_index("pix") == 0, lax.axis_index("pix") == slabs - 1)
+
+    def edge_rows(rows_of):
+        got = lax.ppermute(pick(near, rows_of[:HALF], rows_of[-HALF:]), ("date", "pix"), pairs)
+        return pick(outer, jnp.zeros_like(got), got)
+
+    here = pick(near, low, high)
     far = swap(pick(near, high, low), 2)
-    own = jnp.concatenate([pick(near, low, high), far], 2)
-    edge = jnp.concatenate([edge_own, edge_far], 2)
+    edge = jnp.concatenate([edge_rows(here), edge_rows(far)], 2)
+    own = jnp.concatenate([here, far], 2)
     both = pick(near, jnp.concatenate([edge, own], 0), jnp.concatenate([own, edge], 0))
     tall = rows + 2 * HALF
     first, second = both[:tall], both[rows:]
@@ -403,12 +456,14 @@
     return jnp.concatenate(parts, 0)
 
 
-def assemble_kernel(offsets, place_ref, *refs):
+def assemble_kernel(offsets, *refs):
+    date = lax.axis_index("date")
+    block = block_of(date, lax.axis_index("pix"))
     pieces, (out_ref, mine_ref, whole_ref, sem) = refs[: len(offsets)], refs[len(offsets) :]
     own, rows = out_ref.shape[1], pieces[0].shape[2]
     copies = []
     for offset, piece in zip(offsets, pieces):
-        row = pl.multiple_of((place_ref[0] ^ offset) * rows, rows)
+        row = pl.multiple_of((block ^ offset) * rows, rows)
         copy = pltpu.make_async_copy(
             piece.at[:, pl.ds(0, own)], out_ref.at[:, :, pl.ds(row, rows), :], sem.at[len(copies)]
         )
@@ -418,13 +473,13 @@
     width = mine_ref.shape[3]
     cols = whole_ref.shape[2]
     for c in range(2):
-        rolled = pltpu.roll(whole_ref[c], lax.rem(cols - place_ref[0] * width, cols), 1)
+        rolled = pltpu.roll(whole_ref[c], lax.rem(cols - date * width, cols), 1)
         mine_ref[c, 0] = rolled[:, :width]
     for copy in copies:
         copy.wait()
 
 
-def assemble(pieces, offsets, place, count):
+def assemble(pieces, offsets, count):
     _, own, rows, cols = pieces[0].shape
     own = own - 1
     return pl.pallas_call(
@@ -433,18 +488,18 @@
             jax.ShapeDtypeStruct((2, own, rows * count, cols), F32),
             jax.ShapeDtypeStruct((2, 1, rows * count, cols // count), F32),
         ),
-        in_specs=[pl.BlockSpec(memory_space=pltpu.SMEM)] + [vmem()] * len(pieces),
+        in_specs=[vmem()] * len(pieces),
         out_specs=(pl.BlockSpec(memory_space=pl.ANY), vmem()),
         scratch_shapes=[pltpu.VMEM((2, rows * count, cols), F32), pltpu.SemaphoreType.DMA((len(pieces),))],
         compiler_params=params(8),
         name="assemble",
-    )(place, *pieces)
-
-
-def scatter(blocks, compressed, me, place):
+    )(*pieces)
+
+
+def scatter(blocks, compressed, me, paired):
     count = lax.axis_size("date")
     _, own, rows, cols = blocks[0].shape
-    if count == 4 and rows % SUB == 0:
+    if paired:
         image = compressed[:, None]
         mine, far, sibling, far_sibling = blocks
         got = swap(jnp.concatenate([far, far_sibling, image], 1), 2)
@@ -458,7 +513,7 @@
             near[0],
             near[1],
         ]
-        return assemble(pieces, (0, 2, 1, 3), place, count)
+        return assemble(pieces, (0, 2, 1, 3), count)
     out = jnp.zeros((2, own + 1, rows * count, cols), F32)
     for step in range(count):
         piece = jnp.concatenate([blocks[step], compressed[:, None]], 1)
@@ -468,10 +523,32 @@
     return (out[:, :own], lax.dynamic_slice_in_dim(out[:, own:], me * width, width, 3))
 
 
+def earlier_images(compressed):
+    slabs = lax.axis_size("pix")
+    blocks = 4 * slabs
+
+    def index(stack, block):
+        k, t = divmod(block, 4)
+        return (stack * 4 + block_of(t, k)) * slabs + k
+
+    def crossing(block):
+        target = block + 1 if block & 1 else block - 1
+        return target if 0 <= target < blocks else block
+
+    def move(target_of):
+        pairs = [
+            (index(stack, block), index(1 - stack, target_of(block))) for stack in range(2) for block in range(blocks)
+        ]
+        return lax.ppermute(compressed, ("ms", "date", "pix"), pairs)
+
+    return [move(lambda block: block), move(lambda block: block ^ 1), move(crossing)]
+
+
 def body(slc_stack):
     count = lax.axis_size("date")
     rows = slc_stack.shape[2] // count
-    a = paired_windows(slc_stack) if count == 4 and rows >= HALF else plain_windows(slc_stack)
+    paired = is_paired(slc_stack)
+    a = paired_windows(slc_stack) if paired else plain_windows(slc_stack)
     cols = a.shape[3]
     chunks = cols // LANES
     a = a.reshape(a.shape[:3] + (chunks, LANES)).transpose(0, 1, 3, 2, 4)
@@ -479,21 +556,23 @@
     band = (jnp.abs(places[:, None] - places[None, :]) <= HALF).astype(BF16)
     band = jnp.concatenate([band, band], 0)
     me = lax.axis_index("date").astype(jnp.uint32)
-    place = lax.axis_index("date").astype(jnp.int32).reshape(1)
-    a, me, place = lax.optimization_barrier((a, me, place))
+    a, me = lax.optimization_barrier((a, me))
     s, r, w, compressed = link_own(a, band)
-    compressed = compressed.transpose(0, 2, 1, 3).reshape(2, rows, cols)
     slots = min(3, lax.axis_size("ms") - 1)
-    z = jnp.stack([earlier_windows(compressed, shift_by) for shift_by in range(1, slots + 1)], 2)
-    z = jnp.pad(z, ((0, 0), (0, 0), (0, SUB - slots), (0, 0)))
-    z = z.reshape(z.shape[:3] + (chunks, LANES)).transpose(0, 1, 3, 2, 4)
-    linked = link_window(a, z, band, s, r, w, slots)
+    image = compressed.transpose(0, 2, 1, 3).reshape(2, rows, cols)
+    if paired:
+        images = earlier_images(compressed)
+    else:
+        z = jnp.stack([earlier_windows(image, shift_by) for shift_by in range(1, slots + 1)], 2)
+        z = jnp.pad(z, ((0, 0), (0, 0), (0, SUB - slots), (0, 0)))
+        images = [z.reshape(z.shape[:3] + (chunks, LANES)).transpose(0, 1, 3, 2, 4)]
+    linked = link_window(a, images, band, s, r, w, slots, paired)
     own = slc_stack.shape[1]
     blocks = [
         linked[:, :, :, j * own : (j + 1) * own].transpose(2, 3, 0, 1, 4).reshape(2, own, rows, cols)
         for j in range(count)
     ]
-    return scatter(blocks, compressed, me, place)
+    return scatter(blocks, image, me, paired)
 
 
 def solution(mesh):

time: 47.2 us -> 40.4 us (0.86); the launches traced: 46.6 us -> 40.3 us
  starting transfers between devices: 16.5 us -> 12.2 us
  Pallas kernels: 14.4 us -> 11.9 us
  waiting for transfers between devices: 13.3 us -> 13.8 us
    ppermute x5, starting transfers between devices: 13.6 us -> 7.27 us  [the longest x3 7.26 us: move(): return lax.ppermute(compressed, ('ms', 'date', 'pix'), pairs)]
    pallas_call x1, Pallas kernels: 9.45 us -> 6.89 us  [link_own(): pl.pallas_call(own_kernel, out_shape=(jax.ShapeDtypeStruct((rows * chunks...]
    ppermute x4, starting transfers between devices: 2.88 us -> 4.97 us  [swap(): return lax.ppermute(value, 'date', [(i, i ^ step) for i in range(count)])]
    ppermute x5, waiting for transfers between devices: 2.19 us -> 3.34 us  [the longest x3 2.15 us: move(): return lax.ppermute(compressed, ('ms', 'date', 'pix'), pairs)]
    ppermute x4, waiting for transfers between devices: 11.1 us -> 10.4 us  [swap(): return lax.ppermute(value, 'date', [(i, i ^ step) for i in range(count)])]
    unnamed x2 -> x1, local copies, waits for them, and re-layouts: 1.11 us -> 1.11 us
where the time goes in v4:
time: 40.4 us; the launch traced here: 40.3 us
  waiting for transfers between devices  13.8 us (34%)
  starting transfers between devices  12.2 us (30%)
  Pallas kernels  11.9 us (29%)
  local copies, waits for them, and re-layouts  1.24 us (3%)
  between operations  0.82 us (2%)
    ppermute x4, waiting for transfers between devices, swap(): return lax.ppermute(value, 'date', [(i, i ^ step) for i in range(count)])  10.4 us
    ppermute x3, starting transfers between devices, move(): return lax.ppermute(compressed, ('ms', 'date', 'pix'), pairs)  7.26 us
    pallas_call x1, Pallas kernels, link_own(): pl.pallas_call(own_kernel, out_shape=(jax.ShapeDtypeStruct((rows * chunks...  6.89 us
    ppermute x4, starting transfers between devices, swap(): return lax.ppermute(value, 'date', [(i, i ^ step) for i in range(count)])  4.97 us
    pallas_call x1, Pallas kernels, link_window(): pl.pallas_call(functools.partial(window_kernel, slots, paired), out_shape...  3.64 us
    ppermute x3, waiting for transfers between devices, move(): return lax.ppermute(compressed, ('ms', 'date', 'pix'), pairs)  2.15 us
    pallas_call x1, Pallas kernels, assemble(): pl.pallas_call(functools.partial(assemble_kernel, offsets), out_shape=(ja...  1.35 us
    ppermute x2, waiting for transfers between devices, edge_rows(): lax.ppermute(pick(near, rows_of[:HALF], rows_of[-HALF:]), ('date', 'pix')...  1.18 us
  transfers between devices with their start and end apart: 9, of which 6 were waited for; matrix products, arithmetic and copies ran while one was open for 0% of the time, Pallas kernels for 0%

profile of v4, /device:TPU:0, one launch (start us, length us, event | category | flops | bytes accessed | tf_op | source)
XLA Modules:
  0.0 40.3 jit_solution(11222952434892292860)
XLA Ops:
  0.6 1.1 %copy.17 = f32[2,8,32,128]{3,1,0,2:T(8,128)S(1)} copy(f32[2,8,32,128]{3,2,1,0:T(8,128)} %param.1) | data formatting | bytes 524288 | tf_op args[0]
  1.8 3.0 %collective-permute-start.1 = (f32[21,2,8,128]{3,2,1,0:T(8,128)S(1)}, f32[21,2,8,128]{3,2,1,0:T(8,128)S(1)}, u32[]{:S(2)}, u32[]{:S(2)}) collective-permute-start(f32[21,2,8,128]{3,2,1,0:T(8,128)S(1)} %get-tuple-element.17), channel_id=1, source_target_pairs={{0,8},{4,12},{8,0},{12,4},{1,9},{5,13},{9,1},{13,5},{2,10},{6,14},... | collective-permute-start | bytes 516104 | tf_op jit(solution)/shard_map/ppermute | solution.py:370
  4.8 0.0 collective-permute-start
  4.8 4.3 %collective-permute-done.1 = f32[21,2,8,128]{3,2,1,0:T(8,128)S(1)} collective-permute-done((f32[21,2,8,128]{3,2,1,0:T(8,128)S(1)}, f32[21,2,8,128]{3,2,1,0:T(8,128)S(1)}, u32[]{:S(2)}, u32[]{:S(2)}) %collective-permute-start.1) | collective-permute-done | bytes 172064 | tf_op jit(solution)/shard_map/ppermute | solution.py:370
  9.2 0.0 collective-permute-start.2
  9.2 0.0 collective-permute-done
  9.2 1.2 %collective-permute-done.2 = f32[5,2,8,128]{3,2,1,0:T(8,128)S(1)} collective-permute-done((f32[5,2,8,128]{3,2,1,0:T(8,128)S(1)}, f32[5,2,8,128]{3,2,1,0:T(8,128)S(1)}, u32[]{:S(2)}, u32[]{:S(2)}) %collective-permute-start.2) | collective-permute-done | bytes 40992 | tf_op jit(solution)/shard_map/ppermute | solution.py:401
  10.5 0.1 slice_select_fusion.1
  10.5 0.2 collective-permute-start.3
  10.8 1.4 %collective-permute-done.3 = f32[18,2,16,128]{3,2,1,0:T(8,128)S(1)} collective-permute-done((f32[18,2,16,128]{3,2,1,0:T(8,128)S(1)}, f32[18,2,16,128]{3,2,1,0:T(8,128)S(1)}, u32[]{:S(2)}, u32[]{:S(2)}) %collective-permute-start.3) | collective-permute-done | bytes 294944 | tf_op jit(solution)/shard_map/ppermute | solution.py:370
  12.2 0.1 maximum_bitcast_fusion.a_ref.refs_0_
  12.3 6.9 %link_own.1 = (f32[20480,128]{1,0:T(8,128)S(1)}, f32[8,1,32,128]{3,2,1,0:T(8,128)S(1)}, f32[8,1,2,32,128]{4,3,2,1,0:T(8,128)S(1)}, f32[2,1,8,128]{3,2,1,0:T(8,128)S(1)}) custom-call(f32[18,2,1,32,128]{4,3,2,1,0:T(8,128)S(1)} %maximum_bitcast_fusion.a_ref.refs_0_, bf16[256,128]{1,0:T(8,128)(2,1)S(1)} %add_convert_fusion.band_ref.refs_1_), custom_call_target="tpu_custom_call" | custom-call | tf_op jit(solution)/shard_map/link_own/pallas_call | solution.py:328
  19.2 1.8 %collective-permute-start.6 = (f32[2,1,8,128]{3,2,1,0:T(8,128)S(1)}, f32[2,1,8,128]{3,2,1,0:T(8,128)S(1)}, u32[]{:S(2)}, u32[]{:S(2)}) collective-permute-start(f32[2,1,8,128]{3,2,1,0:T(8,128)S(1)} %get-tuple-element.9), channel_id=1, source_target_pairs={{0,16},{4,24},{8,20},{12,25},{9,28},{13,17},{1,29},{5,18},{2,21},{... | collective-permute-start | bytes 24584 | tf_op jit(solution)/shard_map/ppermute | solution.py:542
  20.9 4.0 %collective-permute-start.5 = (f32[2,1,8,128]{3,2,1,0:T(8,128)S(1)}, f32[2,1,8,128]{3,2,1,0:T(8,128)S(1)}, u32[]{:S(2)}, u32[]{:S(2)}) collective-permute-start(f32[2,1,8,128]{3,2,1,0:T(8,128)S(1)} %get-tuple-element.9), channel_id=1, source_target_pairs={{0,20},{4,16},{8,28},{12,24},{9,29},{13,25},{1,21},{5,17},{2,22},{... | collective-permute-start | bytes 24584 | tf_op jit(solution)/shard_map/ppermute | solution.py:542
  24.9 1.5 %collective-permute-start.4 = (f32[2,1,8,128]{3,2,1,0:T(8,128)S(1)}, f32[2,1,8,128]{3,2,1,0:T(8,128)S(1)}, u32[]{:S(2)}, u32[]{:S(2)}) collective-permute-start(f32[2,1,8,128]{3,2,1,0:T(8,128)S(1)} %get-tuple-element.9), channel_id=1, source_target_pairs={{0,16},{4,20},{8,24},{12,28},{9,25},{13,29},{1,17},{5,21},{2,18},{... | collective-permute-start | bytes 24584 | tf_op jit(solution)/shard_map/ppermute | solution.py:542
  26.4 0.0 collective-permute-done.6.refs_7_
  26.4 0.0 collective-permute-done.5.refs_6_
  26.4 2.1 %collective-permute-done.4.refs_5_ = f32[2,1,8,128]{3,2,1,0:T(8,128)S(1)} collective-permute-done((f32[2,1,8,128]{3,2,1,0:T(8,128)S(1)}, f32[2,1,8,128]{3,2,1,0:T(8,128)S(1)}, u32[]{:S(2)}, u32[]{:S(2)}) %collective-permute-start.4) | collective-permute-done | bytes 8224 | tf_op jit(solution)/shard_map/ppermute | solution.py:542
  28.6 3.6 %link_window.1 = f32[8,1,2,32,128]{4,3,2,1,0:T(8,128)S(1)} custom-call(f32[18,2,1,32,128]{4,3,2,1,0:T(8,128)S(1)} %maximum_bitcast_fusion.a_ref.refs_0_, bf16[256,128]{1,0:T(8,128)(2,1)S(1)} %add_convert_fusion.band_ref.refs_1_, f32[20480,128]{1,0:T(8,128)S(1)} %get-tuple-element.6.refs_2_, f32[8,1,32,128]{3,2,1,0:T(8,128)S(1)} %get-tuple-element.7.refs_3_, ...), custom_call_target="tpu_custom_call" | custom-call | tf_op jit(solution)/shard_map/link_window/pallas_call | solution.py:357
  32.3 1.6 %collective-permute-start.7 = (f32[2,17,8,128]{3,2,1,0:T(8,128)S(1)}, f32[2,17,8,128]{3,2,1,0:T(8,128)S(1)}, u32[]{:S(2)}, u32[]{:S(2)}) collective-permute-start(f32[2,17,8,128]{3,2,1,0:T(8,128)S(1)} %pad_maximum_fusion.1), channel_id=1, source_target_pairs={{0,8},{4,12},{8,0},{12,4},{1,9},{5,13},{9,1},{13,5},{2,10},{6,14},... | collective-permute-start | bytes 417800 | tf_op jit(solution)/shard_map/ppermute | solution.py:370
  34.0 3.4 %collective-permute-done.7 = f32[2,17,8,128]{3,2,1,0:T(8,128)S(1)} collective-permute-done((f32[2,17,8,128]{3,2,1,0:T(8,128)S(1)}, f32[2,17,8,128]{3,2,1,0:T(8,128)S(1)}, u32[]{:S(2)}, u32[]{:S(2)}) %collective-permute-start.7) | collective-permute-done | bytes 139296 | tf_op jit(solution)/shard_map/ppermute | solution.py:370
  37.5 0.1 collective-permute-start.8
  37.6 1.3 %collective-permute-done.8 = f32[2,2,9,8,128]{4,3,2,1,0:T(8,128)S(1)} collective-permute-done((f32[2,2,9,8,128]{4,3,2,1,0:T(8,128)S(1)}, f32[2,2,9,8,128]{4,3,2,1,0:T(8,128)S(1)}, u32[]{:S(2)}, u32[]{:S(2)}) %collective-permute-start.8) | collective-permute-done | bytes 147488 | tf_op jit(solution)/shard_map/ppermute | solution.py:370
  38.9 1.4 %assemble.1 = (f32[2,8,32,128]{3,2,1,0:T(8,128)}, f32[2,1,32,32]{3,2,1,0:T(8,128)}) custom-call(f32[2,9,8,128]{3,2,1,0:T(8,128)S(1)} %get-tuple-element.21.refs_0_, f32[2,9,8,128]{3,2,1,0:T(8,128)S(1)} %pad_maximum_fusion.4.refs_1_, f32[2,9,8,128]{3,2,1,0:T(8,128)S(1)} %get-tuple-element.19.refs_2_, f32[2,9,8,128]{3,2,1,0:T(8,128)S(1)} %get-tuple-element.18.refs_3_), custom_call_target="tpu_custom_call" | custom-call | tf_op jit(solution)/shard_map/assemble/pallas_call | solution.py:485
  (19 shorter events, 0.3 us)
Async XLA Ops:
  1.8 7.4 %collective-permute-start.1 = (f32[21,2,8,128]{3,2,1,0:T(8,128)S(1)}, f32[21,2,8,128]{3,2,1,0:T(8,128)S(1)}, u32[]{:S(2)}, u32[]{:S(2)}) collective-permute-start(f32[21,2,8,128]{3,2,1,0:T(8,128)S(1)} %get-tuple-element.17), channel_id=1, source_target_pairs={{0,8},{4,12},{8,0},{12,4},{1,9},{5,13},{9,1},{13,5},{2,10},{6,14},... | collective-permute-start | bytes 516104 | tf_op jit(solution)/shard_map/ppermute | solution.py:370
  4.8 4.4 %collective-permute-start = (f32[5,2,8,128]{3,2,1,0:T(8,128)S(1)}, f32[5,2,8,128]{3,2,1,0:T(8,128)S(1)}, u32[]{:S(2)}, u32[]{:S(2)}) collective-permute-start(f32[5,2,8,128]{3,2,1,0:T(8,128)S(1)} %slice_select_fusion.5), channel_id=1, source_target_pairs={{0,4},{1,2},{2,1},{3,7},{4,0},{5,6},{6,5},{7,3},{8,9},{9,8},{10,11... | collective-permute-start | bytes 122888 | tf_op jit(solution)/shard_map/ppermute | solution.py:401
  9.2 1.2 %collective-permute-start.2 = (f32[5,2,8,128]{3,2,1,0:T(8,128)S(1)}, f32[5,2,8,128]{3,2,1,0:T(8,128)S(1)}, u32[]{:S(2)}, u32[]{:S(2)}) collective-permute-start(f32[5,2,8,128]{3,2,1,0:T(8,128)S(1)} %slice_select_fusion.4), channel_id=1, source_target_pairs={{0,4},{1,2},{2,1},{3,7},{4,0},{5,6},{6,5},{7,3},{8,9},{9,8},{10,11... | collective-permute-start | bytes 122888 | tf_op jit(solution)/shard_map/ppermute | solution.py:401
  10.5 1.6 %collective-permute-start.3 = (f32[18,2,16,128]{3,2,1,0:T(8,128)S(1)}, f32[18,2,16,128]{3,2,1,0:T(8,128)S(1)}, u32[]{:S(2)}, u32[]{:S(2)}) collective-permute-start(f32[18,2,16,128]{3,2,1,0:T(8,128)S(1)} %get-tuple-element.11), channel_id=1, source_target_pairs={{0,4},{4,0},{8,12},{12,8},{1,5},{5,1},{9,13},{13,9},{2,6},{6,2},{1... | collective-permute-start | bytes 884744 | tf_op jit(solution)/shard_map/ppermute | solution.py:370
  19.2 7.3 %collective-permute-start.6 = (f32[2,1,8,128]{3,2,1,0:T(8,128)S(1)}, f32[2,1,8,128]{3,2,1,0:T(8,128)S(1)}, u32[]{:S(2)}, u32[]{:S(2)}) collective-permute-start(f32[2,1,8,128]{3,2,1,0:T(8,128)S(1)} %get-tuple-element.9), channel_id=1, source_target_pairs={{0,16},{4,24},{8,20},{12,25},{9,28},{13,17},{1,29},{5,18},{2,21},{... | collective-permute-start | bytes 24584 | tf_op jit(solution)/shard_map/ppermute | solution.py:542
  20.9 5.5 %collective-permute-start.5 = (f32[2,1,8,128]{3,2,1,0:T(8,128)S(1)}, f32[2,1,8,128]{3,2,1,0:T(8,128)S(1)}, u32[]{:S(2)}, u32[]{:S(2)}) collective-permute-start(f32[2,1,8,128]{3,2,1,0:T(8,128)S(1)} %get-tuple-element.9), channel_id=1, source_target_pairs={{0,20},{4,16},{8,28},{12,24},{9,29},{13,25},{1,21},{5,17},{2,22},{... | collective-permute-start | bytes 24584 | tf_op jit(solution)/shard_map/ppermute | solution.py:542
  24.9 3.7 %collective-permute-start.4 = (f32[2,1,8,128]{3,2,1,0:T(8,128)S(1)}, f32[2,1,8,128]{3,2,1,0:T(8,128)S(1)}, u32[]{:S(2)}, u32[]{:S(2)}) collective-permute-start(f32[2,1,8,128]{3,2,1,0:T(8,128)S(1)} %get-tuple-element.9), channel_id=1, source_target_pairs={{0,16},{4,20},{8,24},{12,28},{9,25},{13,29},{1,17},{5,21},{2,18},{... | collective-permute-start | bytes 24584 | tf_op jit(solution)/shard_map/ppermute | solution.py:542
  32.3 5.1 %collective-permute-start.7 = (f32[2,17,8,128]{3,2,1,0:T(8,128)S(1)}, f32[2,17,8,128]{3,2,1,0:T(8,128)S(1)}, u32[]{:S(2)}, u32[]{:S(2)}) collective-permute-start(f32[2,17,8,128]{3,2,1,0:T(8,128)S(1)} %pad_maximum_fusion.1), channel_id=1, source_target_pairs={{0,8},{4,12},{8,0},{12,4},{1,9},{5,13},{9,1},{13,5},{2,10},{6,14},... | collective-permute-start | bytes 417800 | tf_op jit(solution)/shard_map/ppermute | solution.py:370
  37.5 1.4 %collective-permute-start.8 = (f32[2,2,9,8,128]{4,3,2,1,0:T(8,128)S(1)}, f32[2,2,9,8,128]{4,3,2,1,0:T(8,128)S(1)}, u32[]{:S(2)}, u32[]{:S(2)}) collective-permute-start(f32[2,2,9,8,128]{4,3,2,1,0:T(8,128)S(1)} %pad_maximum_fusion), channel_id=1, source_target_pairs={{0,4},{4,0},{8,12},{12,8},{1,5},{5,1},{9,13},{13,9},{2,6},{6,2},{1... | collective-permute-start | bytes 442376 | tf_op jit(solution)/shard_map/ppermute | solution.py:370

commit v5 on v4

--- a/solution.py
+++ b/solution.py
@@ -387,23 +387,22 @@
     rows = lead.shape[0] // 4
     reach = 2 * rows + HALF
     low, high = lead[:reach], lead[-reach:]
-    pairs = []
+    own_pairs, far_pairs = [], []
     for date in range(4):
         for k in range(slabs):
-            target = k - 1 if block_of(date, k) < 2 else k + 1
-            if 0 <= target < slabs:
-                pairs.append((date * slabs + k, date * slabs + target))
-            else:
-                pairs.append((date * slabs + k, (date ^ 1) * slabs + k))
+            upper = block_of(date, k) < 2
+            target = k - 1 if upper else k + 1
+            inside = 0 <= target < slabs
+            own_pairs.append((date * slabs + k, date * slabs + target if inside else (date ^ 1) * slabs + k))
+            far_pairs.append(((date ^ 2) * slabs + (target if inside else k), date * slabs + k))
     outer = pick(near, lax.axis_index("pix") == 0, lax.axis_index("pix") == slabs - 1)
-
-    def edge_rows(rows_of):
-        got = lax.ppermute(pick(near, rows_of[:HALF], rows_of[-HALF:]), ("date", "pix"), pairs)
-        return pick(outer, jnp.zeros_like(got), got)
-
+    top, bottom = lead[:HALF], lead[-HALF:]
+    edge_own = lax.ppermute(pick(near, top, bottom), ("date", "pix"), own_pairs)
+    edge_far = lax.ppermute(pick(near, bottom, top), ("date", "pix"), far_pairs)
     here = pick(near, low, high)
     far = swap(pick(near, high, low), 2)
-    edge = jnp.concatenate([edge_rows(here), edge_rows(far)], 2)
+    edge = jnp.concatenate([edge_own, edge_far], 2)
+    edge = pick(outer, jnp.zeros_like(edge), edge)
     own = jnp.concatenate([here, far], 2)
     both = pick(near, jnp.concatenate([edge, own], 0), jnp.concatenate([own, edge], 0))
     tall = rows + 2 * HALF

time: 40.4 us -> 37.4 us (0.926)
  waiting for transfers between devices: 13.8 us -> 12.1 us
  starting transfers between devices: 12.2 us -> 10.9 us
    ppermute x4, waiting for transfers between devices: 10.4 us -> 6.34 us  [swap(): return lax.ppermute(value, 'date', [(i, i ^ step) for i in range(count)])]
    ppermute x3, starting transfers between devices: 7.26 us -> 4.54 us  [move(): return lax.ppermute(compressed, ('ms', 'date', 'pix'), pairs)]
    ppermute x2, waiting for transfers between devices: 1.18 us -> 3.59 us  [the longest x1 3.59 us: paired_windows(): edge_far = lax.ppermute(pick(near, bottom, top), ('date', 'pix'), far_pairs)]
    ppermute x2, starting transfers between devices: 0.01 us -> 1.64 us  [the longest x1 1.57 us: paired_windows(): edge_far = lax.ppermute(pick(near, bottom, top), ('date', 'pix'), far_pairs)]
where the time goes in v5:
time: 37.4 us; the launch traced here: 37.2 us
  waiting for transfers between devices  12.1 us (32%)
  Pallas kernels  11.9 us (32%)
  starting transfers between devices  10.9 us (29%)
  local copies, waits for them, and re-layouts  1.24 us (3%)
  between operations  0.8 us (2%)
    pallas_call x1, Pallas kernels, link_own(): pl.pallas_call(own_kernel, out_shape=(jax.ShapeDtypeStruct((rows * chunks...  6.89 us
    ppermute x4, waiting for transfers between devices, swap(): return lax.ppermute(value, 'date', [(i, i ^ step) for i in range(count)])  6.34 us
    ppermute x4, starting transfers between devices, swap(): return lax.ppermute(value, 'date', [(i, i ^ step) for i in range(count)])  4.72 us
    ppermute x3, starting transfers between devices, move(): return lax.ppermute(compressed, ('ms', 'date', 'pix'), pairs)  4.54 us
    pallas_call x1, Pallas kernels, link_window(): pl.pallas_call(functools.partial(window_kernel, slots, paired), out_shape...  3.64 us
    ppermute x1, waiting for transfers between devices, paired_windows(): edge_far = lax.ppermute(pick(near, bottom, top), ('date', 'pix'), far_pairs)  3.59 us
    ppermute x3, waiting for transfers between devices, move(): return lax.ppermute(compressed, ('ms', 'date', 'pix'), pairs)  2.16 us
    ppermute x1, starting transfers between devices, paired_windows(): edge_far = lax.ppermute(pick(near, bottom, top), ('date', 'pix'), far_pairs)  1.57 us
  transfers between devices with their start and end apart: 9, of which 6 were waited for; matrix products, arithmetic and copies ran while one was open for 0% of the time, Pallas kernels for 0%

profile of v5, /device:TPU:0, one launch (start us, length us, event | category | flops | bytes accessed | tf_op | source)
XLA Modules:
  0.0 37.2 jit_solution(18168434520083727025)
XLA Ops:
  0.6 1.1 %copy.17 = f32[2,8,32,128]{3,1,0,2:T(8,128)S(1)} copy(f32[2,8,32,128]{3,2,1,0:T(8,128)} %param.1) | data formatting | bytes 524288 | tf_op args[0]
  1.8 3.0 %collective-permute-start.2 = (f32[21,2,8,128]{3,2,1,0:T(8,128)S(1)}, f32[21,2,8,128]{3,2,1,0:T(8,128)S(1)}, u32[]{:S(2)}, u32[]{:S(2)}) collective-permute-start(f32[21,2,8,128]{3,2,1,0:T(8,128)S(1)} %get-tuple-element.19), channel_id=1, source_target_pairs={{0,8},{4,12},{8,0},{12,4},{1,9},{5,13},{9,1},{13,5},{2,10},{6,14},... | collective-permute-start | bytes 516104 | tf_op jit(solution)/shard_map/ppermute | solution.py:370
  4.8 0.1 collective-permute-start
  4.9 1.6 %collective-permute-start.1 = (f32[5,2,8,128]{3,2,1,0:T(8,128)S(1)}, f32[5,2,8,128]{3,2,1,0:T(8,128)S(1)}, u32[]{:S(2)}, u32[]{:S(2)}) collective-permute-start(f32[5,2,8,128]{3,2,1,0:T(8,128)S(1)} %get-tuple-element.17), channel_id=1, source_target_pairs={{8,0},{10,1},{9,2},{11,3},{12,4},{14,5},{13,6},{15,7},{1,8},{0,9},... | collective-permute-start | bytes 122888 | tf_op jit(solution)/shard_map/ppermute | solution.py:401
  6.5 0.0 collective-permute-done
  6.5 3.6 %collective-permute-done.1 = f32[5,2,8,128]{3,2,1,0:T(8,128)S(1)} collective-permute-done((f32[5,2,8,128]{3,2,1,0:T(8,128)S(1)}, f32[5,2,8,128]{3,2,1,0:T(8,128)S(1)}, u32[]{:S(2)}, u32[]{:S(2)}) %collective-permute-start.1) | collective-permute-done | bytes 40992 | tf_op jit(solution)/shard_map/ppermute | solution.py:401
  10.1 0.0 collective-permute-done.2
  10.1 0.1 slice_select_fusion.1
  10.2 0.1 collective-permute-start.3
  10.3 1.5 %collective-permute-done.3 = f32[18,2,16,128]{3,2,1,0:T(8,128)S(1)} collective-permute-done((f32[18,2,16,128]{3,2,1,0:T(8,128)S(1)}, f32[18,2,16,128]{3,2,1,0:T(8,128)S(1)}, u32[]{:S(2)}, u32[]{:S(2)}) %collective-permute-start.3) | collective-permute-done | bytes 294944 | tf_op jit(solution)/shard_map/ppermute | solution.py:370
  11.9 0.1 maximum_bitcast_fusion.a_ref.refs_0_
  11.9 6.9 %link_own.1 = (f32[20480,128]{1,0:T(8,128)S(1)}, f32[8,1,32,128]{3,2,1,0:T(8,128)S(1)}, f32[8,1,2,32,128]{4,3,2,1,0:T(8,128)S(1)}, f32[2,1,8,128]{3,2,1,0:T(8,128)S(1)}) custom-call(f32[18,2,1,32,128]{4,3,2,1,0:T(8,128)S(1)} %maximum_bitcast_fusion.a_ref.refs_0_, bf16[256,128]{1,0:T(8,128)(2,1)S(1)} %add_convert_fusion.band_ref.refs_1_), custom_call_target="tpu_custom_call" | custom-call | tf_op jit(solution)/shard_map/link_own/pallas_call | solution.py:328
  18.8 1.8 %collective-permute-start.6 = (f32[2,1,8,128]{3,2,1,0:T(8,128)S(1)}, f32[2,1,8,128]{3,2,1,0:T(8,128)S(1)}, u32[]{:S(2)}, u32[]{:S(2)}) collective-permute-start(f32[2,1,8,128]{3,2,1,0:T(8,128)S(1)} %get-tuple-element.9), channel_id=1, source_target_pairs={{0,16},{4,24},{8,20},{12,25},{9,28},{13,17},{1,29},{5,18},{2,21},{... | collective-permute-start | bytes 24584 | tf_op jit(solution)/shard_map/ppermute | solution.py:541
  20.6 1.3 %collective-permute-start.5 = (f32[2,1,8,128]{3,2,1,0:T(8,128)S(1)}, f32[2,1,8,128]{3,2,1,0:T(8,128)S(1)}, u32[]{:S(2)}, u32[]{:S(2)}) collective-permute-start(f32[2,1,8,128]{3,2,1,0:T(8,128)S(1)} %get-tuple-element.9), channel_id=1, source_target_pairs={{0,20},{4,16},{8,28},{12,24},{9,29},{13,25},{1,21},{5,17},{2,22},{... | collective-permute-start | bytes 24584 | tf_op jit(solution)/shard_map/ppermute | solution.py:541
  21.9 1.5 %collective-permute-start.4 = (f32[2,1,8,128]{3,2,1,0:T(8,128)S(1)}, f32[2,1,8,128]{3,2,1,0:T(8,128)S(1)}, u32[]{:S(2)}, u32[]{:S(2)}) collective-permute-start(f32[2,1,8,128]{3,2,1,0:T(8,128)S(1)} %get-tuple-element.9), channel_id=1, source_target_pairs={{0,16},{4,20},{8,24},{12,28},{9,25},{13,29},{1,17},{5,21},{2,18},{... | collective-permute-start | bytes 24584 | tf_op jit(solution)/shard_map/ppermute | solution.py:541
  23.4 0.0 collective-permute-done.6.refs_7_
  23.4 0.3 collective-permute-done.5.refs_6_
  23.7 1.9 %collective-permute-done.4.refs_5_ = f32[2,1,8,128]{3,2,1,0:T(8,128)S(1)} collective-permute-done((f32[2,1,8,128]{3,2,1,0:T(8,128)S(1)}, f32[2,1,8,128]{3,2,1,0:T(8,128)S(1)}, u32[]{:S(2)}, u32[]{:S(2)}) %collective-permute-start.4) | collective-permute-done | bytes 8224 | tf_op jit(solution)/shard_map/ppermute | solution.py:541
  25.5 3.6 %link_window.1 = f32[8,1,2,32,128]{4,3,2,1,0:T(8,128)S(1)} custom-call(f32[18,2,1,32,128]{4,3,2,1,0:T(8,128)S(1)} %maximum_bitcast_fusion.a_ref.refs_0_, bf16[256,128]{1,0:T(8,128)(2,1)S(1)} %add_convert_fusion.band_ref.refs_1_, f32[20480,128]{1,0:T(8,128)S(1)} %get-tuple-element.6.refs_2_, f32[8,1,32,128]{3,2,1,0:T(8,128)S(1)} %get-tuple-element.7.refs_3_, ...), custom_call_target="tpu_custom_call" | custom-call | tf_op jit(solution)/shard_map/link_window/pallas_call | solution.py:357
  29.3 1.6 %collective-permute-start.7 = (f32[2,17,8,128]{3,2,1,0:T(8,128)S(1)}, f32[2,17,8,128]{3,2,1,0:T(8,128)S(1)}, u32[]{:S(2)}, u32[]{:S(2)}) collective-permute-start(f32[2,17,8,128]{3,2,1,0:T(8,128)S(1)} %pad_maximum_fusion.1), channel_id=1, source_target_pairs={{0,8},{4,12},{8,0},{12,4},{1,9},{5,13},{9,1},{13,5},{2,10},{6,14},... | collective-permute-start | bytes 417800 | tf_op jit(solution)/shard_map/ppermute | solution.py:370
  30.9 3.5 %collective-permute-done.7 = f32[2,17,8,128]{3,2,1,0:T(8,128)S(1)} collective-permute-done((f32[2,17,8,128]{3,2,1,0:T(8,128)S(1)}, f32[2,17,8,128]{3,2,1,0:T(8,128)S(1)}, u32[]{:S(2)}, u32[]{:S(2)}) %collective-permute-start.7) | collective-permute-done | bytes 139296 | tf_op jit(solution)/shard_map/ppermute | solution.py:370
  34.4 0.1 collective-permute-start.8
  34.5 1.3 %collective-permute-done.8 = f32[2,2,9,8,128]{4,3,2,1,0:T(8,128)S(1)} collective-permute-done((f32[2,2,9,8,128]{4,3,2,1,0:T(8,128)S(1)}, f32[2,2,9,8,128]{4,3,2,1,0:T(8,128)S(1)}, u32[]{:S(2)}, u32[]{:S(2)}) %collective-permute-start.8) | collective-permute-done | bytes 147488 | tf_op jit(solution)/shard_map/ppermute | solution.py:370
  35.9 1.4 %assemble.1 = (f32[2,8,32,128]{3,2,1,0:T(8,128)}, f32[2,1,32,32]{3,2,1,0:T(8,128)}) custom-call(f32[2,9,8,128]{3,2,1,0:T(8,128)S(1)} %get-tuple-element.23.refs_0_, f32[2,9,8,128]{3,2,1,0:T(8,128)S(1)} %pad_maximum_fusion.4.refs_1_, f32[2,9,8,128]{3,2,1,0:T(8,128)S(1)} %get-tuple-element.21.refs_2_, f32[2,9,8,128]{3,2,1,0:T(8,128)S(1)} %get-tuple-element.20.refs_3_), custom_call_target="tpu_custom_call" | custom-call | tf_op jit(solution)/shard_map/assemble/pallas_call | solution.py:484
  (17 shorter events, 0.3 us)
Async XLA Ops:
  1.8 8.3 %collective-permute-start.2 = (f32[21,2,8,128]{3,2,1,0:T(8,128)S(1)}, f32[21,2,8,128]{3,2,1,0:T(8,128)S(1)}, u32[]{:S(2)}, u32[]{:S(2)}) collective-permute-start(f32[21,2,8,128]{3,2,1,0:T(8,128)S(1)} %get-tuple-element.19), channel_id=1, source_target_pairs={{0,8},{4,12},{8,0},{12,4},{1,9},{5,13},{9,1},{13,5},{2,10},{6,14},... | collective-permute-start | bytes 516104 | tf_op jit(solution)/shard_map/ppermute | solution.py:370
  4.8 1.7 %collective-permute-start = (f32[5,2,8,128]{3,2,1,0:T(8,128)S(1)}, f32[5,2,8,128]{3,2,1,0:T(8,128)S(1)}, u32[]{:S(2)}, u32[]{:S(2)}) collective-permute-start(f32[5,2,8,128]{3,2,1,0:T(8,128)S(1)} %get-tuple-element.16), channel_id=1, source_target_pairs={{0,4},{1,2},{2,1},{3,7},{4,0},{5,6},{6,5},{7,3},{8,9},{9,8},{10,11... | collective-permute-start | bytes 122888 | tf_op jit(solution)/shard_map/ppermute | solution.py:400
  4.9 5.2 %collective-permute-start.1 = (f32[5,2,8,128]{3,2,1,0:T(8,128)S(1)}, f32[5,2,8,128]{3,2,1,0:T(8,128)S(1)}, u32[]{:S(2)}, u32[]{:S(2)}) collective-permute-start(f32[5,2,8,128]{3,2,1,0:T(8,128)S(1)} %get-tuple-element.17), channel_id=1, source_target_pairs={{8,0},{10,1},{9,2},{11,3},{12,4},{14,5},{13,6},{15,7},{1,8},{0,9},... | collective-permute-start | bytes 122888 | tf_op jit(solution)/shard_map/ppermute | solution.py:401
  10.2 1.6 %collective-permute-start.3 = (f32[18,2,16,128]{3,2,1,0:T(8,128)S(1)}, f32[18,2,16,128]{3,2,1,0:T(8,128)S(1)}, u32[]{:S(2)}, u32[]{:S(2)}) collective-permute-start(f32[18,2,16,128]{3,2,1,0:T(8,128)S(1)} %get-tuple-element.11), channel_id=1, source_target_pairs={{0,4},{4,0},{8,12},{12,8},{1,5},{5,1},{9,13},{13,9},{2,6},{6,2},{1... | collective-permute-start | bytes 884744 | tf_op jit(solution)/shard_map/ppermute | solution.py:370
  18.8 4.5 %collective-permute-start.6 = (f32[2,1,8,128]{3,2,1,0:T(8,128)S(1)}, f32[2,1,8,128]{3,2,1,0:T(8,128)S(1)}, u32[]{:S(2)}, u32[]{:S(2)}) collective-permute-start(f32[2,1,8,128]{3,2,1,0:T(8,128)S(1)} %get-tuple-element.9), channel_id=1, source_target_pairs={{0,16},{4,24},{8,20},{12,25},{9,28},{13,17},{1,29},{5,18},{2,21},{... | collective-permute-start | bytes 24584 | tf_op jit(solution)/shard_map/ppermute | solution.py:541
  20.6 3.1 %collective-permute-start.5 = (f32[2,1,8,128]{3,2,1,0:T(8,128)S(1)}, f32[2,1,8,128]{3,2,1,0:T(8,128)S(1)}, u32[]{:S(2)}, u32[]{:S(2)}) collective-permute-start(f32[2,1,8,128]{3,2,1,0:T(8,128)S(1)} %get-tuple-element.9), channel_id=1, source_target_pairs={{0,20},{4,16},{8,28},{12,24},{9,29},{13,25},{1,21},{5,17},{2,22},{... | collective-permute-start | bytes 24584 | tf_op jit(solution)/shard_map/ppermute | solution.py:541
  21.9 3.7 %collective-permute-start.4 = (f32[2,1,8,128]{3,2,1,0:T(8,128)S(1)}, f32[2,1,8,128]{3,2,1,0:T(8,128)S(1)}, u32[]{:S(2)}, u32[]{:S(2)}) collective-permute-start(f32[2,1,8,128]{3,2,1,0:T(8,128)S(1)} %get-tuple-element.9), channel_id=1, source_target_pairs={{0,16},{4,20},{8,24},{12,28},{9,25},{13,29},{1,17},{5,21},{2,18},{... | collective-permute-start | bytes 24584 | tf_op jit(solution)/shard_map/ppermute | solution.py:541
  29.3 5.1 %collective-permute-start.7 = (f32[2,17,8,128]{3,2,1,0:T(8,128)S(1)}, f32[2,17,8,128]{3,2,1,0:T(8,128)S(1)}, u32[]{:S(2)}, u32[]{:S(2)}) collective-permute-start(f32[2,17,8,128]{3,2,1,0:T(8,128)S(1)} %pad_maximum_fusion.1), channel_id=1, source_target_pairs={{0,8},{4,12},{8,0},{12,4},{1,9},{5,13},{9,1},{13,5},{2,10},{6,14},... | collective-permute-start | bytes 417800 | tf_op jit(solution)/shard_map/ppermute | solution.py:370
  34.4 1.4 %collective-permute-start.8 = (f32[2,2,9,8,128]{4,3,2,1,0:T(8,128)S(1)}, f32[2,2,9,8,128]{4,3,2,1,0:T(8,128)S(1)}, u32[]{:S(2)}, u32[]{:S(2)}) collective-permute-start(f32[2,2,9,8,128]{4,3,2,1,0:T(8,128)S(1)} %pad_maximum_fusion), channel_id=1, source_target_pairs={{0,4},{4,0},{8,12},{12,8},{1,5},{5,1},{9,13},{13,9},{2,6},{6,2},{1... | collective-permute-start | bytes 442376 | tf_op jit(solution)/shard_map/ppermute | solution.py:370

commit v6 on v5

--- a/solution.py
+++ b/solution.py
@@ -1,4 +1,5 @@
 import functools
+import itertools
 import math
 
 import jax
@@ -15,6 +16,7 @@
 EPSILON = 1e-06
 SUB = 8
 LANES = 128
+TURNS = 2
 F32 = jnp.float32
 BF16 = jnp.bfloat16
 
@@ -129,8 +131,16 @@
 
 
 def each_row(rows, chunks, one_row):
+    turns = math.gcd(rows, TURNS)
     for chunk in range(chunks):
-        lax.fori_loop(0, rows, functools.partial(one_row, chunk), 0)
+
+        def together(step, carry, chunk=chunk):
+            running = [one_row(chunk, step * turns + turn, turn) for turn in range(turns)]
+            for _ in itertools.zip_longest(*running):
+                pass
+            return carry
+
+        lax.fori_loop(0, rows // turns, together, 0)
 
 
 def own_kernel(a_ref, band_ref, s_ref, r_ref, w_ref, comp_ref, v_ref, *x_refs):
@@ -168,15 +178,16 @@
 
         lax.fori_loop(0, SUB // group, one_group, 0)
 
-    def one_row(chunk, row, carry):
+    def one_row(chunk, row, turn):
+        v = v_ref.at[turn]
         base = pl.multiple_of((row * chunks + chunk) * 2 * half, SUB)
         scale = r_ref[row, chunk]
-        v_ref[0] = scale
+        v[0] = scale
         for repeat in range(ITERS):
             if repeat == 0:
-                real, imag = fill_and_apply(s_ref, v_ref, base, dates)
+                real, imag = fill_and_apply(s_ref, v, base, dates)
             else:
-                real, imag = matvec(s_ref, v_ref, base, dates)
+                real, imag = matvec(s_ref, v, base, dates)
             real, imag = real * (scale / AREA), imag * (scale / AREA)
             if repeat == 0:
                 w_ref[row, chunk, 0] = real
@@ -184,15 +195,15 @@
             factor = lax.rsqrt(total_square(real, imag) / dates + EPSILON)
             real, imag = real * factor, imag * factor
             if repeat < ITERS - 1:
-                v_ref[0] = real * scale
-                v_ref[1] = imag * scale
+                v[0] = real * scale
+                v[1] = imag * scale
+            yield
         centre_real, centre_imag = a_ref[row + HALF, 0, chunk], a_ref[row + HALF, 1, chunk]
         root = math.sqrt(dates)
         comp_real = jnp.sum(real * centre_real + imag * centre_imag, axis=0, keepdims=True)
         comp_imag = jnp.sum(real * centre_imag - imag * centre_real, axis=0, keepdims=True)
         comp_ref[0, chunk, pl.ds(row, 1), :] = comp_real / root
         comp_ref[1, chunk, pl.ds(row, 1), :] = comp_imag / root
-        return carry
 
     each_row(rows, chunks, one_row)
 
@@ -267,25 +278,26 @@
 
     place = lax.broadcasted_iota(jnp.int32, (SUB, LANES), 0)
 
-    def one_row(chunk, row, carry):
+    def one_row(chunk, row, turn):
+        v, vz = v_ref.at[turn], vz_ref.at[turn]
         base = pl.multiple_of((row * chunks + chunk) * 2 * half, SUB)
         scale = r_ref[row, chunk]
         scale_z = rz_ref[row, chunk]
-        v_ref[0] = scale
-        v_ref[1] = jnp.zeros_like(scale)
-        vz_ref[0] = scale_z
-        vz_ref[1] = jnp.zeros_like(scale_z)
+        v[0] = scale
+        v[1] = jnp.zeros_like(scale)
+        vz[0] = scale_z
+        vz[1] = jnp.zeros_like(scale_z)
         for repeat in range(ITERS):
             if repeat == 0:
                 real, imag = w_ref[row, chunk, 0], w_ref[row, chunk, 1]
             else:
-                real, imag = matvec(s_ref, v_ref, base, dates)
+                real, imag = matvec(s_ref, v, base, dates)
                 real, imag = real * (scale / AREA), imag * (scale / AREA)
             add_real, add_imag = jnp.zeros_like(real), jnp.zeros_like(imag)
             z_real, z_imag = jnp.zeros_like(scale_z), jnp.zeros_like(scale_z)
-            old_real, old_imag = v_ref[0], v_ref[1]
+            old_real, old_imag = v[0], v[1]
             for slot in range(slots):
-                v_real, v_imag = vz_ref[0, pl.ds(slot, 1), :], vz_ref[1, pl.ds(slot, 1), :]
+                v_real, v_imag = vz[0, pl.ds(slot, 1), :], vz[1, pl.ds(slot, 1), :]
                 m_real, m_imag = m_ref[slot, row, chunk, 0], m_ref[slot, row, chunk, 1]
                 add_real = add_real + m_real * v_real - m_imag * v_imag
                 add_imag = add_imag + m_real * v_imag + m_imag * v_real
@@ -304,13 +316,13 @@
             factor = lax.rsqrt(square / (slots + dates) + EPSILON)
             real, imag = real * factor, imag * factor
             if repeat < ITERS - 1:
-                v_ref[0] = real * scale
-                v_ref[1] = imag * scale
-                vz_ref[0] = z_real * factor * scale_z
-                vz_ref[1] = z_imag * factor * scale_z
+                v[0] = real * scale
+                v[1] = imag * scale
+                vz[0] = z_real * factor * scale_z
+                vz[1] = z_imag * factor * scale_z
+            yield
         out_ref[row, chunk, 0] = real
         out_ref[row, chunk, 1] = imag
-        return carry
 
     each_row(rows, chunks, one_row)
 
@@ -335,7 +347,7 @@
         ),
         in_specs=[vmem()] * 2,
         out_specs=[vmem()] * 4,
-        scratch_shapes=[pltpu.VMEM((2, dates, LANES), F32)]
+        scratch_shapes=[pltpu.VMEM((TURNS, 2, dates, LANES), F32)]
         + [pltpu.VMEM((rows * 2 * dates, band.shape[0]), BF16)] * group,
         compiler_params=params(),
         name="link_own",
@@ -349,8 +361,8 @@
         pltpu.VMEM((slots, rows, chunks, 2, dates, LANES), F32),
         pltpu.VMEM((slots, rows, chunks, 2, SUB, LANES), F32),
         pltpu.VMEM((rows, chunks, SUB, LANES), F32),
-        pltpu.VMEM((2, dates, LANES), F32),
-        pltpu.VMEM((2, SUB, LANES), F32),
+        pltpu.VMEM((TURNS, 2, dates, LANES), F32),
+        pltpu.VMEM((TURNS, 2, SUB, LANES), F32),
     ]
     if paired:
         scratch.append(pltpu.VMEM((3, 2, chunks, rows, LANES), F32))

time: 37.4 us -> 36.4 us (0.973)
  Pallas kernels: 11.9 us -> 10.9 us
    pallas_call x1, Pallas kernels: 6.89 us -> 6.4 us  [link_own(): pl.pallas_call(own_kernel, out_shape=(jax.ShapeDtypeStruct((rows * chunks...]
    pallas_call x1, Pallas kernels: 3.64 us -> 3.17 us  [link_window(): pl.pallas_call(functools.partial(window_kernel, slots, paired), out_shape...]
where the time goes in v6:
time: 36.4 us; the launch traced here: 36.3 us
  waiting for transfers between devices  12.1 us (33%)
  starting transfers between devices  10.9 us (30%)
  Pallas kernels  10.9 us (30%)
  local copies, waits for them, and re-layouts  1.24 us (3%)
  between operations  0.8 us (2%)
    pallas_call x1, Pallas kernels, link_own(): pl.pallas_call(own_kernel, out_shape=(jax.ShapeDtypeStruct((rows * chunks...  6.4 us
    ppermute x4, waiting for transfers between devices, swap(): return lax.ppermute(value, 'date', [(i, i ^ step) for i in range(count)])  6.34 us
    ppermute x4, starting transfers between devices, swap(): return lax.ppermute(value, 'date', [(i, i ^ step) for i in range(count)])  4.72 us
    ppermute x3, starting transfers between devices, move(): return lax.ppermute(compressed, ('ms', 'date', 'pix'), pairs)  4.54 us
    ppermute x1, waiting for transfers between devices, paired_windows(): edge_far = lax.ppermute(pick(near, bottom, top), ('date', 'pix'), far_pairs)  3.59 us
    pallas_call x1, Pallas kernels, link_window(): pl.pallas_call(functools.partial(window_kernel, slots, paired), out_shape...  3.17 us
    ppermute x3, waiting for transfers between devices, move(): return lax.ppermute(compressed, ('ms', 'date', 'pix'), pairs)  2.16 us
    ppermute x1, starting transfers between devices, paired_windows(): edge_far = lax.ppermute(pick(near, bottom, top), ('date', 'pix'), far_pairs)  1.57 us
  transfers between devices with their start and end apart: 9, of which 6 were waited for; matrix products, arithmetic and copies ran while one was open for 0% of the time, Pallas kernels for 0%

profile of v6, /device:TPU:0, one launch (start us, length us, event | category | flops | bytes accessed | tf_op | source)
XLA Modules:
  0.0 36.3 jit_solution(12859625664168681079)
XLA Ops:
  0.6 1.1 %copy.17 = f32[2,8,32,128]{3,1,0,2:T(8,128)S(1)} copy(f32[2,8,32,128]{3,2,1,0:T(8,128)} %param.1) | data formatting | bytes 524288 | tf_op args[0]
  1.8 3.0 %collective-permute-start.2 = (f32[21,2,8,128]{3,2,1,0:T(8,128)S(1)}, f32[21,2,8,128]{3,2,1,0:T(8,128)S(1)}, u32[]{:S(2)}, u32[]{:S(2)}) collective-permute-start(f32[21,2,8,128]{3,2,1,0:T(8,128)S(1)} %get-tuple-element.19), channel_id=1, source_target_pairs={{0,8},{4,12},{8,0},{12,4},{1,9},{5,13},{9,1},{13,5},{2,10},{6,14},... | collective-permute-start | bytes 516104 | tf_op jit(solution)/shard_map/ppermute | solution.py:382
  4.8 0.1 collective-permute-start
  4.9 1.6 %collective-permute-start.1 = (f32[5,2,8,128]{3,2,1,0:T(8,128)S(1)}, f32[5,2,8,128]{3,2,1,0:T(8,128)S(1)}, u32[]{:S(2)}, u32[]{:S(2)}) collective-permute-start(f32[5,2,8,128]{3,2,1,0:T(8,128)S(1)} %get-tuple-element.17), channel_id=1, source_target_pairs={{8,0},{10,1},{9,2},{11,3},{12,4},{14,5},{13,6},{15,7},{1,8},{0,9},... | collective-permute-start | bytes 122888 | tf_op jit(solution)/shard_map/ppermute | solution.py:413
  6.5 0.0 collective-permute-done
  6.5 3.6 %collective-permute-done.1 = f32[5,2,8,128]{3,2,1,0:T(8,128)S(1)} collective-permute-done((f32[5,2,8,128]{3,2,1,0:T(8,128)S(1)}, f32[5,2,8,128]{3,2,1,0:T(8,128)S(1)}, u32[]{:S(2)}, u32[]{:S(2)}) %collective-permute-start.1) | collective-permute-done | bytes 40992 | tf_op jit(solution)/shard_map/ppermute | solution.py:413
  10.1 0.0 collective-permute-done.2
  10.1 0.1 slice_select_fusion.1
  10.2 0.1 collective-permute-start.3
  10.3 1.5 %collective-permute-done.3 = f32[18,2,16,128]{3,2,1,0:T(8,128)S(1)} collective-permute-done((f32[18,2,16,128]{3,2,1,0:T(8,128)S(1)}, f32[18,2,16,128]{3,2,1,0:T(8,128)S(1)}, u32[]{:S(2)}, u32[]{:S(2)}) %collective-permute-start.3) | collective-permute-done | bytes 294944 | tf_op jit(solution)/shard_map/ppermute | solution.py:382
  11.9 0.1 maximum_bitcast_fusion.a_ref.refs_0_
  11.9 6.4 %link_own.1 = (f32[20480,128]{1,0:T(8,128)S(1)}, f32[8,1,32,128]{3,2,1,0:T(8,128)S(1)}, f32[8,1,2,32,128]{4,3,2,1,0:T(8,128)S(1)}, f32[2,1,8,128]{3,2,1,0:T(8,128)S(1)}) custom-call(f32[18,2,1,32,128]{4,3,2,1,0:T(8,128)S(1)} %maximum_bitcast_fusion.a_ref.refs_0_, bf16[256,128]{1,0:T(8,128)(2,1)S(1)} %add_convert_fusion.band_ref.refs_1_), custom_call_target="tpu_custom_call" | custom-call | tf_op jit(solution)/shard_map/link_own/pallas_call | solution.py:340
  18.3 1.8 %collective-permute-start.6 = (f32[2,1,8,128]{3,2,1,0:T(8,128)S(1)}, f32[2,1,8,128]{3,2,1,0:T(8,128)S(1)}, u32[]{:S(2)}, u32[]{:S(2)}) collective-permute-start(f32[2,1,8,128]{3,2,1,0:T(8,128)S(1)} %get-tuple-element.9), channel_id=1, source_target_pairs={{0,16},{4,24},{8,20},{12,25},{9,28},{13,17},{1,29},{5,18},{2,21},{... | collective-permute-start | bytes 24584 | tf_op jit(solution)/shard_map/ppermute | solution.py:553
  20.1 1.3 %collective-permute-start.5 = (f32[2,1,8,128]{3,2,1,0:T(8,128)S(1)}, f32[2,1,8,128]{3,2,1,0:T(8,128)S(1)}, u32[]{:S(2)}, u32[]{:S(2)}) collective-permute-start(f32[2,1,8,128]{3,2,1,0:T(8,128)S(1)} %get-tuple-element.9), channel_id=1, source_target_pairs={{0,20},{4,16},{8,28},{12,24},{9,29},{13,25},{1,21},{5,17},{2,22},{... | collective-permute-start | bytes 24584 | tf_op jit(solution)/shard_map/ppermute | solution.py:553
  21.4 1.5 %collective-permute-start.4 = (f32[2,1,8,128]{3,2,1,0:T(8,128)S(1)}, f32[2,1,8,128]{3,2,1,0:T(8,128)S(1)}, u32[]{:S(2)}, u32[]{:S(2)}) collective-permute-start(f32[2,1,8,128]{3,2,1,0:T(8,128)S(1)} %get-tuple-element.9), channel_id=1, source_target_pairs={{0,16},{4,20},{8,24},{12,28},{9,25},{13,29},{1,17},{5,21},{2,18},{... | collective-permute-start | bytes 24584 | tf_op jit(solution)/shard_map/ppermute | solution.py:553
  22.9 0.0 collective-permute-done.6.refs_7_
  22.9 0.3 collective-permute-done.5.refs_6_
  23.2 1.9 %collective-permute-done.4.refs_5_ = f32[2,1,8,128]{3,2,1,0:T(8,128)S(1)} collective-permute-done((f32[2,1,8,128]{3,2,1,0:T(8,128)S(1)}, f32[2,1,8,128]{3,2,1,0:T(8,128)S(1)}, u32[]{:S(2)}, u32[]{:S(2)}) %collective-permute-start.4) | collective-permute-done | bytes 8224 | tf_op jit(solution)/shard_map/ppermute | solution.py:553
  25.0 3.2 %link_window.1 = f32[8,1,2,32,128]{4,3,2,1,0:T(8,128)S(1)} custom-call(f32[18,2,1,32,128]{4,3,2,1,0:T(8,128)S(1)} %maximum_bitcast_fusion.a_ref.refs_0_, bf16[256,128]{1,0:T(8,128)(2,1)S(1)} %add_convert_fusion.band_ref.refs_1_, f32[20480,128]{1,0:T(8,128)S(1)} %get-tuple-element.6.refs_2_, f32[8,1,32,128]{3,2,1,0:T(8,128)S(1)} %get-tuple-element.7.refs_3_, ...), custom_call_target="tpu_custom_call" | custom-call | tf_op jit(solution)/shard_map/link_window/pallas_call | solution.py:369
  28.3 1.6 %collective-permute-start.7 = (f32[2,17,8,128]{3,2,1,0:T(8,128)S(1)}, f32[2,17,8,128]{3,2,1,0:T(8,128)S(1)}, u32[]{:S(2)}, u32[]{:S(2)}) collective-permute-start(f32[2,17,8,128]{3,2,1,0:T(8,128)S(1)} %pad_maximum_fusion.1), channel_id=1, source_target_pairs={{0,8},{4,12},{8,0},{12,4},{1,9},{5,13},{9,1},{13,5},{2,10},{6,14},... | collective-permute-start | bytes 417800 | tf_op jit(solution)/shard_map/ppermute | solution.py:382
  29.9 3.5 %collective-permute-done.7 = f32[2,17,8,128]{3,2,1,0:T(8,128)S(1)} collective-permute-done((f32[2,17,8,128]{3,2,1,0:T(8,128)S(1)}, f32[2,17,8,128]{3,2,1,0:T(8,128)S(1)}, u32[]{:S(2)}, u32[]{:S(2)}) %collective-permute-start.7) | collective-permute-done | bytes 139296 | tf_op jit(solution)/shard_map/ppermute | solution.py:382
  33.5 0.1 collective-permute-start.8
  33.6 1.3 %collective-permute-done.8 = f32[2,2,9,8,128]{4,3,2,1,0:T(8,128)S(1)} collective-permute-done((f32[2,2,9,8,128]{4,3,2,1,0:T(8,128)S(1)}, f32[2,2,9,8,128]{4,3,2,1,0:T(8,128)S(1)}, u32[]{:S(2)}, u32[]{:S(2)}) %collective-permute-start.8) | collective-permute-done | bytes 147488 | tf_op jit(solution)/shard_map/ppermute | solution.py:382
  34.9 1.4 %assemble.1 = (f32[2,8,32,128]{3,2,1,0:T(8,128)}, f32[2,1,32,32]{3,2,1,0:T(8,128)}) custom-call(f32[2,9,8,128]{3,2,1,0:T(8,128)S(1)} %get-tuple-element.23.refs_0_, f32[2,9,8,128]{3,2,1,0:T(8,128)S(1)} %pad_maximum_fusion.4.refs_1_, f32[2,9,8,128]{3,2,1,0:T(8,128)S(1)} %get-tuple-element.21.refs_2_, f32[2,9,8,128]{3,2,1,0:T(8,128)S(1)} %get-tuple-element.20.refs_3_), custom_call_target="tpu_custom_call" | custom-call | tf_op jit(solution)/shard_map/assemble/pallas_call | solution.py:496
  (17 shorter events, 0.3 us)
Async XLA Ops:
  1.8 8.3 %collective-permute-start.2 = (f32[21,2,8,128]{3,2,1,0:T(8,128)S(1)}, f32[21,2,8,128]{3,2,1,0:T(8,128)S(1)}, u32[]{:S(2)}, u32[]{:S(2)}) collective-permute-start(f32[21,2,8,128]{3,2,1,0:T(8,128)S(1)} %get-tuple-element.19), channel_id=1, source_target_pairs={{0,8},{4,12},{8,0},{12,4},{1,9},{5,13},{9,1},{13,5},{2,10},{6,14},... | collective-permute-start | bytes 516104 | tf_op jit(solution)/shard_map/ppermute | solution.py:382
  4.8 1.7 %collective-permute-start = (f32[5,2,8,128]{3,2,1,0:T(8,128)S(1)}, f32[5,2,8,128]{3,2,1,0:T(8,128)S(1)}, u32[]{:S(2)}, u32[]{:S(2)}) collective-permute-start(f32[5,2,8,128]{3,2,1,0:T(8,128)S(1)} %get-tuple-element.16), channel_id=1, source_target_pairs={{0,4},{1,2},{2,1},{3,7},{4,0},{5,6},{6,5},{7,3},{8,9},{9,8},{10,11... | collective-permute-start | bytes 122888 | tf_op jit(solution)/shard_map/ppermute | solution.py:412
  4.9 5.2 %collective-permute-start.1 = (f32[5,2,8,128]{3,2,1,0:T(8,128)S(1)}, f32[5,2,8,128]{3,2,1,0:T(8,128)S(1)}, u32[]{:S(2)}, u32[]{:S(2)}) collective-permute-start(f32[5,2,8,128]{3,2,1,0:T(8,128)S(1)} %get-tuple-element.17), channel_id=1, source_target_pairs={{8,0},{10,1},{9,2},{11,3},{12,4},{14,5},{13,6},{15,7},{1,8},{0,9},... | collective-permute-start | bytes 122888 | tf_op jit(solution)/shard_map/ppermute | solution.py:413
  10.2 1.6 %collective-permute-start.3 = (f32[18,2,16,128]{3,2,1,0:T(8,128)S(1)}, f32[18,2,16,128]{3,2,1,0:T(8,128)S(1)}, u32[]{:S(2)}, u32[]{:S(2)}) collective-permute-start(f32[18,2,16,128]{3,2,1,0:T(8,128)S(1)} %get-tuple-element.11), channel_id=1, source_target_pairs={{0,4},{4,0},{8,12},{12,8},{1,5},{5,1},{9,13},{13,9},{2,6},{6,2},{1... | collective-permute-start | bytes 884744 | tf_op jit(solution)/shard_map/ppermute | solution.py:382
  18.3 4.5 %collective-permute-start.6 = (f32[2,1,8,128]{3,2,1,0:T(8,128)S(1)}, f32[2,1,8,128]{3,2,1,0:T(8,128)S(1)}, u32[]{:S(2)}, u32[]{:S(2)}) collective-permute-start(f32[2,1,8,128]{3,2,1,0:T(8,128)S(1)} %get-tuple-element.9), channel_id=1, source_target_pairs={{0,16},{4,24},{8,20},{12,25},{9,28},{13,17},{1,29},{5,18},{2,21},{... | collective-permute-start | bytes 24584 | tf_op jit(solution)/shard_map/ppermute | solution.py:553
  20.1 3.1 %collective-permute-start.5 = (f32[2,1,8,128]{3,2,1,0:T(8,128)S(1)}, f32[2,1,8,128]{3,2,1,0:T(8,128)S(1)}, u32[]{:S(2)}, u32[]{:S(2)}) collective-permute-start(f32[2,1,8,128]{3,2,1,0:T(8,128)S(1)} %get-tuple-element.9), channel_id=1, source_target_pairs={{0,20},{4,16},{8,28},{12,24},{9,29},{13,25},{1,21},{5,17},{2,22},{... | collective-permute-start | bytes 24584 | tf_op jit(solution)/shard_map/ppermute | solution.py:553
  21.4 3.7 %collective-permute-start.4 = (f32[2,1,8,128]{3,2,1,0:T(8,128)S(1)}, f32[2,1,8,128]{3,2,1,0:T(8,128)S(1)}, u32[]{:S(2)}, u32[]{:S(2)}) collective-permute-start(f32[2,1,8,128]{3,2,1,0:T(8,128)S(1)} %get-tuple-element.9), channel_id=1, source_target_pairs={{0,16},{4,20},{8,24},{12,28},{9,25},{13,29},{1,17},{5,21},{2,18},{... | collective-permute-start | bytes 24584 | tf_op jit(solution)/shard_map/ppermute | solution.py:553
  28.3 5.1 %collective-permute-start.7 = (f32[2,17,8,128]{3,2,1,0:T(8,128)S(1)}, f32[2,17,8,128]{3,2,1,0:T(8,128)S(1)}, u32[]{:S(2)}, u32[]{:S(2)}) collective-permute-start(f32[2,17,8,128]{3,2,1,0:T(8,128)S(1)} %pad_maximum_fusion.1), channel_id=1, source_target_pairs={{0,8},{4,12},{8,0},{12,4},{1,9},{5,13},{9,1},{13,5},{2,10},{6,14},... | collective-permute-start | bytes 417800 | tf_op jit(solution)/shard_map/ppermute | solution.py:382
  33.5 1.4 %collective-permute-start.8 = (f32[2,2,9,8,128]{4,3,2,1,0:T(8,128)S(1)}, f32[2,2,9,8,128]{4,3,2,1,0:T(8,128)S(1)}, u32[]{:S(2)}, u32[]{:S(2)}) collective-permute-start(f32[2,2,9,8,128]{4,3,2,1,0:T(8,128)S(1)} %pad_maximum_fusion), channel_id=1, source_target_pairs={{0,4},{4,0},{8,12},{12,8},{1,5},{5,1},{9,13},{13,9},{2,6},{6,2},{1... | collective-permute-start | bytes 442376 | tf_op jit(solution)/shard_map/ppermute | solution.py:382

commit v7 on v6

--- a/solution.py
+++ b/solution.py
@@ -149,12 +149,6 @@
     half = dates * pitch(dates)
     group = len(x_refs)
 
-    energies(x_refs[0], a_ref, rows, chunks, dates)
-    for chunk in range(chunks):
-        power = across(x_refs[0], rows * dates, band_ref, chunk)
-        scale = lax.rsqrt(power / AREA + EPSILON)
-        r_ref[:, chunk] = scale.reshape(rows, dates, LANES)
-
     for q_block in range(blocks):
         kept = [(a_ref, b * SUB) for b in range(q_block, blocks)]
 
@@ -181,7 +175,10 @@
     def one_row(chunk, row, turn):
         v = v_ref.at[turn]
         base = pl.multiple_of((row * chunks + chunk) * 2 * half, SUB)
-        scale = r_ref[row, chunk]
+        step = pitch(dates) + 1
+        power = [s_ref[pl.ds(base + b * SUB * step, SUB, stride=step), :] for b in range(blocks)]
+        scale = lax.rsqrt(jnp.concatenate(power, 0) / AREA + EPSILON)
+        r_ref[row, chunk] = scale
         v[0] = scale
         for repeat in range(ITERS):
             if repeat == 0:
@@ -470,7 +467,7 @@
 def assemble_kernel(offsets, *refs):
     date = lax.axis_index("date")
     block = block_of(date, lax.axis_index("pix"))
-    pieces, (out_ref, mine_ref, whole_ref, sem) = refs[: len(offsets)], refs[len(offsets) :]
+    pieces, (out_ref, mine_out_ref, whole_ref, mine_ref, sem) = refs[: len(offsets)], refs[len(offsets) :]
     own, rows = out_ref.shape[1], pieces[0].shape[2]
     copies = []
     for offset, piece in zip(offsets, pieces):
@@ -486,6 +483,9 @@
     for c in range(2):
         rolled = pltpu.roll(whole_ref[c], lax.rem(cols - date * width, cols), 1)
         mine_ref[c, 0] = rolled[:, :width]
+    copy = pltpu.make_async_copy(mine_ref, mine_out_ref, sem.at[len(copies)])
+    copy.start()
+    copies.append(copy)
     for copy in copies:
         copy.wait()
 
@@ -500,8 +500,12 @@
             jax.ShapeDtypeStruct((2, 1, rows * count, cols // count), F32),
         ),
         in_specs=[vmem()] * len(pieces),
-        out_specs=(pl.BlockSpec(memory_space=pl.ANY), vmem()),
-        scratch_shapes=[pltpu.VMEM((2, rows * count, cols), F32), pltpu.SemaphoreType.DMA((len(pieces),))],
+        out_specs=[pl.BlockSpec(memory_space=pl.ANY)] * 2,
+        scratch_shapes=[
+            pltpu.VMEM((2, rows * count, cols), F32),
+            pltpu.VMEM((2, 1, rows * count, cols // count), F32),
+            pltpu.SemaphoreType.DMA((len(pieces) + 1,)),
+        ],
         compiler_params=params(8),
         name="assemble",
     )(*pieces)

time: 36.4 us -> 35.7 us (0.981)
  Pallas kernels: 10.9 us -> 10.2 us
    pallas_call x1, Pallas kernels: 1.35 us -> 0.77 us  [assemble(): pl.pallas_call(functools.partial(assemble_kernel, offsets), out_shape=(ja...]
where the time goes in v7:
time: 35.7 us; the launch traced here: 35.5 us
  waiting for transfers between devices  12.1 us (34%)
  starting transfers between devices  10.9 us (31%)
  Pallas kernels  10.2 us (29%)
  local copies, waits for them, and re-layouts  1.24 us (3%)
  between operations  0.8 us (2%)
    ppermute x4, waiting for transfers between devices, swap(): return lax.ppermute(value, 'date', [(i, i ^ step) for i in range(count)])  6.35 us
    pallas_call x1, Pallas kernels, link_own(): pl.pallas_call(own_kernel, out_shape=(jax.ShapeDtypeStruct((rows * chunks...  6.23 us
    ppermute x4, starting transfers between devices, swap(): return lax.ppermute(value, 'date', [(i, i ^ step) for i in range(count)])  4.72 us
    ppermute x3, starting transfers between devices, move(): return lax.ppermute(compressed, ('ms', 'date', 'pix'), pairs)  4.55 us
    ppermute x1, waiting for transfers between devices, paired_windows(): edge_far = lax.ppermute(pick(near, bottom, top), ('date', 'pix'), far_pairs)  3.59 us
    pallas_call x1, Pallas kernels, link_window(): pl.pallas_call(functools.partial(window_kernel, slots, paired), out_shape...  3.17 us
    ppermute x3, waiting for transfers between devices, move(): return lax.ppermute(compressed, ('ms', 'date', 'pix'), pairs)  2.16 us
    ppermute x1, starting transfers between devices, paired_windows(): edge_far = lax.ppermute(pick(near, bottom, top), ('date', 'pix'), far_pairs)  1.57 us
  transfers between devices with their start and end apart: 9, of which 6 were waited for; matrix products, arithmetic and copies ran while one was open for 0% of the time, Pallas kernels for 0%

profile of v7, /device:TPU:0, one launch (start us, length us, event | category | flops | bytes accessed | tf_op | source)
XLA Modules:
  0.0 35.5 jit_solution(12934211712631401397)
XLA Ops:
  0.6 1.1 %copy.17 = f32[2,8,32,128]{3,1,0,2:T(8,128)S(1)} copy(f32[2,8,32,128]{3,2,1,0:T(8,128)} %param.1) | data formatting | bytes 524288 | tf_op args[0]
  1.8 3.0 %collective-permute-start.2 = (f32[21,2,8,128]{3,2,1,0:T(8,128)S(1)}, f32[21,2,8,128]{3,2,1,0:T(8,128)S(1)}, u32[]{:S(2)}, u32[]{:S(2)}) collective-permute-start(f32[21,2,8,128]{3,2,1,0:T(8,128)S(1)} %get-tuple-element.19), channel_id=1, source_target_pairs={{0,8},{4,12},{8,0},{12,4},{1,9},{5,13},{9,1},{13,5},{2,10},{6,14},... | collective-permute-start | bytes 516104 | tf_op jit(solution)/shard_map/ppermute | solution.py:379
  4.8 0.1 collective-permute-start
  4.9 1.6 %collective-permute-start.1 = (f32[5,2,8,128]{3,2,1,0:T(8,128)S(1)}, f32[5,2,8,128]{3,2,1,0:T(8,128)S(1)}, u32[]{:S(2)}, u32[]{:S(2)}) collective-permute-start(f32[5,2,8,128]{3,2,1,0:T(8,128)S(1)} %get-tuple-element.17), channel_id=1, source_target_pairs={{8,0},{10,1},{9,2},{11,3},{12,4},{14,5},{13,6},{15,7},{1,8},{0,9},... | collective-permute-start | bytes 122888 | tf_op jit(solution)/shard_map/ppermute | solution.py:410
  6.5 0.0 collective-permute-done
  6.5 3.6 %collective-permute-done.1 = f32[5,2,8,128]{3,2,1,0:T(8,128)S(1)} collective-permute-done((f32[5,2,8,128]{3,2,1,0:T(8,128)S(1)}, f32[5,2,8,128]{3,2,1,0:T(8,128)S(1)}, u32[]{:S(2)}, u32[]{:S(2)}) %collective-permute-start.1) | collective-permute-done | bytes 40992 | tf_op jit(solution)/shard_map/ppermute | solution.py:410
  10.1 0.0 collective-permute-done.2
  10.1 0.1 slice_select_fusion.1
  10.2 0.1 collective-permute-start.3
  10.3 1.5 %collective-permute-done.3 = f32[18,2,16,128]{3,2,1,0:T(8,128)S(1)} collective-permute-done((f32[18,2,16,128]{3,2,1,0:T(8,128)S(1)}, f32[18,2,16,128]{3,2,1,0:T(8,128)S(1)}, u32[]{:S(2)}, u32[]{:S(2)}) %collective-permute-start.3) | collective-permute-done | bytes 294944 | tf_op jit(solution)/shard_map/ppermute | solution.py:379
  11.9 0.1 maximum_bitcast_fusion.a_ref.refs_0_
  11.9 6.2 %link_own.1 = (f32[20480,128]{1,0:T(8,128)S(1)}, f32[8,1,32,128]{3,2,1,0:T(8,128)S(1)}, f32[8,1,2,32,128]{4,3,2,1,0:T(8,128)S(1)}, f32[2,1,8,128]{3,2,1,0:T(8,128)S(1)}) custom-call(f32[18,2,1,32,128]{4,3,2,1,0:T(8,128)S(1)} %maximum_bitcast_fusion.a_ref.refs_0_, bf16[256,128]{1,0:T(8,128)(2,1)S(1)} %add_convert_fusion.band_ref.refs_1_), custom_call_target="tpu_custom_call" | custom-call | tf_op jit(solution)/shard_map/link_own/pallas_call | solution.py:337
  18.2 1.8 %collective-permute-start.6 = (f32[2,1,8,128]{3,2,1,0:T(8,128)S(1)}, f32[2,1,8,128]{3,2,1,0:T(8,128)S(1)}, u32[]{:S(2)}, u32[]{:S(2)}) collective-permute-start(f32[2,1,8,128]{3,2,1,0:T(8,128)S(1)} %get-tuple-element.9), channel_id=1, source_target_pairs={{0,16},{4,24},{8,20},{12,25},{9,28},{13,17},{1,29},{5,18},{2,21},{... | collective-permute-start | bytes 24584 | tf_op jit(solution)/shard_map/ppermute | solution.py:557
  19.9 1.3 %collective-permute-start.5 = (f32[2,1,8,128]{3,2,1,0:T(8,128)S(1)}, f32[2,1,8,128]{3,2,1,0:T(8,128)S(1)}, u32[]{:S(2)}, u32[]{:S(2)}) collective-permute-start(f32[2,1,8,128]{3,2,1,0:T(8,128)S(1)} %get-tuple-element.9), channel_id=1, source_target_pairs={{0,20},{4,16},{8,28},{12,24},{9,29},{13,25},{1,21},{5,17},{2,22},{... | collective-permute-start | bytes 24584 | tf_op jit(solution)/shard_map/ppermute | solution.py:557
  21.2 1.5 %collective-permute-start.4 = (f32[2,1,8,128]{3,2,1,0:T(8,128)S(1)}, f32[2,1,8,128]{3,2,1,0:T(8,128)S(1)}, u32[]{:S(2)}, u32[]{:S(2)}) collective-permute-start(f32[2,1,8,128]{3,2,1,0:T(8,128)S(1)} %get-tuple-element.9), channel_id=1, source_target_pairs={{0,16},{4,20},{8,24},{12,28},{9,25},{13,29},{1,17},{5,21},{2,18},{... | collective-permute-start | bytes 24584 | tf_op jit(solution)/shard_map/ppermute | solution.py:557
  22.7 0.0 collective-permute-done.6.refs_7_
  22.7 0.3 collective-permute-done.5.refs_6_
  23.0 1.9 %collective-permute-done.4.refs_5_ = f32[2,1,8,128]{3,2,1,0:T(8,128)S(1)} collective-permute-done((f32[2,1,8,128]{3,2,1,0:T(8,128)S(1)}, f32[2,1,8,128]{3,2,1,0:T(8,128)S(1)}, u32[]{:S(2)}, u32[]{:S(2)}) %collective-permute-start.4) | collective-permute-done | bytes 8224 | tf_op jit(solution)/shard_map/ppermute | solution.py:557
  24.9 3.2 %link_window.1 = f32[8,1,2,32,128]{4,3,2,1,0:T(8,128)S(1)} custom-call(f32[18,2,1,32,128]{4,3,2,1,0:T(8,128)S(1)} %maximum_bitcast_fusion.a_ref.refs_0_, bf16[256,128]{1,0:T(8,128)(2,1)S(1)} %add_convert_fusion.band_ref.refs_1_, f32[20480,128]{1,0:T(8,128)S(1)} %get-tuple-element.6.refs_2_, f32[8,1,32,128]{3,2,1,0:T(8,128)S(1)} %get-tuple-element.7.refs_3_, ...), custom_call_target="tpu_custom_call" | custom-call | tf_op jit(solution)/shard_map/link_window/pallas_call | solution.py:366
  28.1 1.5 %collective-permute-start.7 = (f32[2,17,8,128]{3,2,1,0:T(8,128)S(1)}, f32[2,17,8,128]{3,2,1,0:T(8,128)S(1)}, u32[]{:S(2)}, u32[]{:S(2)}) collective-permute-start(f32[2,17,8,128]{3,2,1,0:T(8,128)S(1)} %pad_maximum_fusion.1), channel_id=1, source_target_pairs={{0,8},{4,12},{8,0},{12,4},{1,9},{5,13},{9,1},{13,5},{2,10},{6,14},... | collective-permute-start | bytes 417800 | tf_op jit(solution)/shard_map/ppermute | solution.py:379
  29.8 3.5 %collective-permute-done.7 = f32[2,17,8,128]{3,2,1,0:T(8,128)S(1)} collective-permute-done((f32[2,17,8,128]{3,2,1,0:T(8,128)S(1)}, f32[2,17,8,128]{3,2,1,0:T(8,128)S(1)}, u32[]{:S(2)}, u32[]{:S(2)}) %collective-permute-start.7) | collective-permute-done | bytes 139296 | tf_op jit(solution)/shard_map/ppermute | solution.py:379
  33.3 0.1 collective-permute-start.8
  33.4 1.3 %collective-permute-done.8 = f32[2,2,9,8,128]{4,3,2,1,0:T(8,128)S(1)} collective-permute-done((f32[2,2,9,8,128]{4,3,2,1,0:T(8,128)S(1)}, f32[2,2,9,8,128]{4,3,2,1,0:T(8,128)S(1)}, u32[]{:S(2)}, u32[]{:S(2)}) %collective-permute-start.8) | collective-permute-done | bytes 147488 | tf_op jit(solution)/shard_map/ppermute | solution.py:379
  34.7 0.8 %assemble.1 = (f32[2,8,32,128]{3,2,1,0:T(8,128)}, f32[2,1,32,32]{3,2,1,0:T(8,128)}) custom-call(f32[2,9,8,128]{3,2,1,0:T(8,128)S(1)} %get-tuple-element.23.refs_0_, f32[2,9,8,128]{3,2,1,0:T(8,128)S(1)} %pad_maximum_fusion.4.refs_1_, f32[2,9,8,128]{3,2,1,0:T(8,128)S(1)} %get-tuple-element.21.refs_2_, f32[2,9,8,128]{3,2,1,0:T(8,128)S(1)} %get-tuple-element.20.refs_3_), custom_call_target="tpu_custom_call" | custom-call | tf_op jit(solution)/shard_map/assemble/pallas_call | solution.py:496
  (17 shorter events, 0.3 us)
Async XLA Ops:
  1.8 8.3 %collective-permute-start.2 = (f32[21,2,8,128]{3,2,1,0:T(8,128)S(1)}, f32[21,2,8,128]{3,2,1,0:T(8,128)S(1)}, u32[]{:S(2)}, u32[]{:S(2)}) collective-permute-start(f32[21,2,8,128]{3,2,1,0:T(8,128)S(1)} %get-tuple-element.19), channel_id=1, source_target_pairs={{0,8},{4,12},{8,0},{12,4},{1,9},{5,13},{9,1},{13,5},{2,10},{6,14},... | collective-permute-start | bytes 516104 | tf_op jit(solution)/shard_map/ppermute | solution.py:379
  4.8 1.7 %collective-permute-start = (f32[5,2,8,128]{3,2,1,0:T(8,128)S(1)}, f32[5,2,8,128]{3,2,1,0:T(8,128)S(1)}, u32[]{:S(2)}, u32[]{:S(2)}) collective-permute-start(f32[5,2,8,128]{3,2,1,0:T(8,128)S(1)} %get-tuple-element.16), channel_id=1, source_target_pairs={{0,4},{1,2},{2,1},{3,7},{4,0},{5,6},{6,5},{7,3},{8,9},{9,8},{10,11... | collective-permute-start | bytes 122888 | tf_op jit(solution)/shard_map/ppermute | solution.py:409
  4.9 5.2 %collective-permute-start.1 = (f32[5,2,8,128]{3,2,1,0:T(8,128)S(1)}, f32[5,2,8,128]{3,2,1,0:T(8,128)S(1)}, u32[]{:S(2)}, u32[]{:S(2)}) collective-permute-start(f32[5,2,8,128]{3,2,1,0:T(8,128)S(1)} %get-tuple-element.17), channel_id=1, source_target_pairs={{8,0},{10,1},{9,2},{11,3},{12,4},{14,5},{13,6},{15,7},{1,8},{0,9},... | collective-permute-start | bytes 122888 | tf_op jit(solution)/shard_map/ppermute | solution.py:410
  10.2 1.6 %collective-permute-start.3 = (f32[18,2,16,128]{3,2,1,0:T(8,128)S(1)}, f32[18,2,16,128]{3,2,1,0:T(8,128)S(1)}, u32[]{:S(2)}, u32[]{:S(2)}) collective-permute-start(f32[18,2,16,128]{3,2,1,0:T(8,128)S(1)} %get-tuple-element.11), channel_id=1, source_target_pairs={{0,4},{4,0},{8,12},{12,8},{1,5},{5,1},{9,13},{13,9},{2,6},{6,2},{1... | collective-permute-start | bytes 884744 | tf_op jit(solution)/shard_map/ppermute | solution.py:379
  18.2 4.6 %collective-permute-start.6 = (f32[2,1,8,128]{3,2,1,0:T(8,128)S(1)}, f32[2,1,8,128]{3,2,1,0:T(8,128)S(1)}, u32[]{:S(2)}, u32[]{:S(2)}) collective-permute-start(f32[2,1,8,128]{3,2,1,0:T(8,128)S(1)} %get-tuple-element.9), channel_id=1, source_target_pairs={{0,16},{4,24},{8,20},{12,25},{9,28},{13,17},{1,29},{5,18},{2,21},{... | collective-permute-start | bytes 24584 | tf_op jit(solution)/shard_map/ppermute | solution.py:557
  19.9 3.1 %collective-permute-start.5 = (f32[2,1,8,128]{3,2,1,0:T(8,128)S(1)}, f32[2,1,8,128]{3,2,1,0:T(8,128)S(1)}, u32[]{:S(2)}, u32[]{:S(2)}) collective-permute-start(f32[2,1,8,128]{3,2,1,0:T(8,128)S(1)} %get-tuple-element.9), channel_id=1, source_target_pairs={{0,20},{4,16},{8,28},{12,24},{9,29},{13,25},{1,21},{5,17},{2,22},{... | collective-permute-start | bytes 24584 | tf_op jit(solution)/shard_map/ppermute | solution.py:557
  21.2 3.7 %collective-permute-start.4 = (f32[2,1,8,128]{3,2,1,0:T(8,128)S(1)}, f32[2,1,8,128]{3,2,1,0:T(8,128)S(1)}, u32[]{:S(2)}, u32[]{:S(2)}) collective-permute-start(f32[2,1,8,128]{3,2,1,0:T(8,128)S(1)} %get-tuple-element.9), channel_id=1, source_target_pairs={{0,16},{4,20},{8,24},{12,28},{9,25},{13,29},{1,17},{5,21},{2,18},{... | collective-permute-start | bytes 24584 | tf_op jit(solution)/shard_map/ppermute | solution.py:557
  28.1 5.1 %collective-permute-start.7 = (f32[2,17,8,128]{3,2,1,0:T(8,128)S(1)}, f32[2,17,8,128]{3,2,1,0:T(8,128)S(1)}, u32[]{:S(2)}, u32[]{:S(2)}) collective-permute-start(f32[2,17,8,128]{3,2,1,0:T(8,128)S(1)} %pad_maximum_fusion.1), channel_id=1, source_target_pairs={{0,8},{4,12},{8,0},{12,4},{1,9},{5,13},{9,1},{13,5},{2,10},{6,14},... | collective-permute-start | bytes 417800 | tf_op jit(solution)/shard_map/ppermute | solution.py:379
  33.3 1.4 %collective-permute-start.8 = (f32[2,2,9,8,128]{4,3,2,1,0:T(8,128)S(1)}, f32[2,2,9,8,128]{4,3,2,1,0:T(8,128)S(1)}, u32[]{:S(2)}, u32[]{:S(2)}) collective-permute-start(f32[2,2,9,8,128]{4,3,2,1,0:T(8,128)S(1)} %pad_maximum_fusion), channel_id=1, source_target_pairs={{0,4},{4,0},{8,12},{12,8},{1,5},{5,1},{9,13},{13,9},{2,6},{6,2},{1... | collective-permute-start | bytes 442376 | tf_op jit(solution)/shard_map/ppermute | solution.py:379

commit v8 on v7

--- a/solution.py
+++ b/solution.py
@@ -556,7 +556,8 @@
         ]
         return lax.ppermute(compressed, ("ms", "date", "pix"), pairs)
 
-    return [move(lambda block: block), move(lambda block: block ^ 1), move(crossing)]
+    centre, other = move(lambda block: block), move(crossing)
+    return [centre, swap(centre, 1), other]
 
 
 def body(slc_stack):

time: 35.7 us -> 35.3 us (0.989)
  starting transfers between devices: 10.9 us -> 8.89 us
  waiting for transfers between devices: 12.1 us -> 13.7 us
    ppermute x3 -> x2, starting transfers between devices: 4.55 us -> 2.09 us  [move(): return lax.ppermute(compressed, ('ms', 'date', 'pix'), pairs)]
    ppermute x3 -> x2, waiting for transfers between devices: 2.16 us -> 3.34 us  [move(): return lax.ppermute(compressed, ('ms', 'date', 'pix'), pairs)]
    ppermute x4 -> x5, starting transfers between devices: 4.72 us -> 5.15 us  [swap(): return lax.ppermute(value, 'date', [(i, i ^ step) for i in range(count)])]
    ppermute x4 -> x5, waiting for transfers between devices: 6.35 us -> 6.72 us  [swap(): return lax.ppermute(value, 'date', [(i, i ^ step) for i in range(count)])]
where the time goes in v8:
time: 35.3 us; the launch traced here: 35 us
  waiting for transfers between devices  13.7 us (39%)
  Pallas kernels  10.2 us (29%)
  starting transfers between devices  8.89 us (25%)
  local copies, waits for them, and re-layouts  1.24 us (4%)
  between operations  0.8 us (2%)
    ppermute x5, waiting for transfers between devices, swap(): return lax.ppermute(value, 'date', [(i, i ^ step) for i in range(count)])  6.72 us
    pallas_call x1, Pallas kernels, link_own(): pl.pallas_call(own_kernel, out_shape=(jax.ShapeDtypeStruct((rows * chunks...  6.23 us
    ppermute x5, starting transfers between devices, swap(): return lax.ppermute(value, 'date', [(i, i ^ step) for i in range(count)])  5.15 us
    ppermute x1, waiting for transfers between devices, paired_windows(): edge_far = lax.ppermute(pick(near, bottom, top), ('date', 'pix'), far_pairs)  3.59 us
    ppermute x2, waiting for transfers between devices, move(): return lax.ppermute(compressed, ('ms', 'date', 'pix'), pairs)  3.34 us
    pallas_call x1, Pallas kernels, link_window(): pl.pallas_call(functools.partial(window_kernel, slots, paired), out_shape...  3.17 us
    ppermute x2, starting transfers between devices, move(): return lax.ppermute(compressed, ('ms', 'date', 'pix'), pairs)  2.09 us
    ppermute x1, starting transfers between devices, paired_windows(): edge_far = lax.ppermute(pick(near, bottom, top), ('date', 'pix'), far_pairs)  1.57 us
  transfers between devices with their start and end apart: 9, of which 6 were waited for; matrix products, arithmetic and copies ran while one was open for 0% of the time, Pallas kernels for 0%

profile of v8, /device:TPU:0, one launch (start us, length us, event | category | flops | bytes accessed | tf_op | source)
XLA Modules:
  0.0 35.0 jit_solution(12817409634414024237)
XLA Ops:
  0.6 1.1 %copy.17 = f32[2,8,32,128]{3,1,0,2:T(8,128)S(1)} copy(f32[2,8,32,128]{3,2,1,0:T(8,128)} %param.1) | data formatting | bytes 524288 | tf_op args[0]
  1.8 3.0 %collective-permute-start.2 = (f32[21,2,8,128]{3,2,1,0:T(8,128)S(1)}, f32[21,2,8,128]{3,2,1,0:T(8,128)S(1)}, u32[]{:S(2)}, u32[]{:S(2)}) collective-permute-start(f32[21,2,8,128]{3,2,1,0:T(8,128)S(1)} %get-tuple-element.19), channel_id=1, source_target_pairs={{0,8},{4,12},{8,0},{12,4},{1,9},{5,13},{9,1},{13,5},{2,10},{6,14},... | collective-permute-start | bytes 516104 | tf_op jit(solution)/shard_map/ppermute | solution.py:379
  4.8 0.1 collective-permute-start
  4.9 1.6 %collective-permute-start.1 = (f32[5,2,8,128]{3,2,1,0:T(8,128)S(1)}, f32[5,2,8,128]{3,2,1,0:T(8,128)S(1)}, u32[]{:S(2)}, u32[]{:S(2)}) collective-permute-start(f32[5,2,8,128]{3,2,1,0:T(8,128)S(1)} %get-tuple-element.17), channel_id=1, source_target_pairs={{8,0},{10,1},{9,2},{11,3},{12,4},{14,5},{13,6},{15,7},{1,8},{0,9},... | collective-permute-start | bytes 122888 | tf_op jit(solution)/shard_map/ppermute | solution.py:410
  6.5 0.0 collective-permute-done
  6.5 3.6 %collective-permute-done.1 = f32[5,2,8,128]{3,2,1,0:T(8,128)S(1)} collective-permute-done((f32[5,2,8,128]{3,2,1,0:T(8,128)S(1)}, f32[5,2,8,128]{3,2,1,0:T(8,128)S(1)}, u32[]{:S(2)}, u32[]{:S(2)}) %collective-permute-start.1) | collective-permute-done | bytes 40992 | tf_op jit(solution)/shard_map/ppermute | solution.py:410
  10.1 0.0 collective-permute-done.2
  10.1 0.1 slice_select_fusion.1
  10.2 0.1 collective-permute-start.3
  10.3 1.5 %collective-permute-done.3 = f32[18,2,16,128]{3,2,1,0:T(8,128)S(1)} collective-permute-done((f32[18,2,16,128]{3,2,1,0:T(8,128)S(1)}, f32[18,2,16,128]{3,2,1,0:T(8,128)S(1)}, u32[]{:S(2)}, u32[]{:S(2)}) %collective-permute-start.3) | collective-permute-done | bytes 294944 | tf_op jit(solution)/shard_map/ppermute | solution.py:379
  11.9 0.1 maximum_bitcast_fusion.a_ref.refs_0_
  11.9 6.2 %link_own.1 = (f32[20480,128]{1,0:T(8,128)S(1)}, f32[8,1,32,128]{3,2,1,0:T(8,128)S(1)}, f32[8,1,2,32,128]{4,3,2,1,0:T(8,128)S(1)}, f32[2,1,8,128]{3,2,1,0:T(8,128)S(1)}) custom-call(f32[18,2,1,32,128]{4,3,2,1,0:T(8,128)S(1)} %maximum_bitcast_fusion.a_ref.refs_0_, bf16[256,128]{1,0:T(8,128)(2,1)S(1)} %add_convert_fusion.band_ref.refs_1_), custom_call_target="tpu_custom_call" | custom-call | tf_op jit(solution)/shard_map/link_own/pallas_call | solution.py:337
  18.2 1.8 %collective-permute-start.4 = (f32[2,1,8,128]{3,2,1,0:T(8,128)S(1)}, f32[2,1,8,128]{3,2,1,0:T(8,128)S(1)}, u32[]{:S(2)}, u32[]{:S(2)}) collective-permute-start(f32[2,1,8,128]{3,2,1,0:T(8,128)S(1)} %get-tuple-element.9), channel_id=1, source_target_pairs={{0,16},{4,20},{8,24},{12,28},{9,25},{13,29},{1,17},{5,21},{2,18},{... | collective-permute-start | bytes 24584 | tf_op jit(solution)/shard_map/ppermute | solution.py:557
  19.9 0.3 collective-permute-start.6
  20.3 1.6 %collective-permute-done.4.refs_5_ = f32[2,1,8,128]{3,2,1,0:T(8,128)S(1)} collective-permute-done((f32[2,1,8,128]{3,2,1,0:T(8,128)S(1)}, f32[2,1,8,128]{3,2,1,0:T(8,128)S(1)}, u32[]{:S(2)}, u32[]{:S(2)}) %collective-permute-start.4) | collective-permute-done | bytes 8224 | tf_op jit(solution)/shard_map/ppermute | solution.py:557
  21.9 0.0 collective-permute-start.5
  21.9 1.7 %collective-permute-done.6.refs_7_ = f32[2,1,8,128]{3,2,1,0:T(8,128)S(1)} collective-permute-done((f32[2,1,8,128]{3,2,1,0:T(8,128)S(1)}, f32[2,1,8,128]{3,2,1,0:T(8,128)S(1)}, u32[]{:S(2)}, u32[]{:S(2)}) %collective-permute-start.6) | collective-permute-done | bytes 8224 | tf_op jit(solution)/shard_map/ppermute | solution.py:557
  23.6 0.0 collective-permute-done.5.refs_6_
  23.6 3.2 %link_window.1 = f32[8,1,2,32,128]{4,3,2,1,0:T(8,128)S(1)} custom-call(f32[18,2,1,32,128]{4,3,2,1,0:T(8,128)S(1)} %maximum_bitcast_fusion.a_ref.refs_0_, bf16[256,128]{1,0:T(8,128)(2,1)S(1)} %add_convert_fusion.band_ref.refs_1_, f32[20480,128]{1,0:T(8,128)S(1)} %get-tuple-element.6.refs_2_, f32[8,1,32,128]{3,2,1,0:T(8,128)S(1)} %get-tuple-element.7.refs_3_, ...), custom_call_target="tpu_custom_call" | custom-call | tf_op jit(solution)/shard_map/link_window/pallas_call | solution.py:366
  26.9 2.0 %collective-permute-start.7 = (f32[2,17,8,128]{3,2,1,0:T(8,128)S(1)}, f32[2,17,8,128]{3,2,1,0:T(8,128)S(1)}, u32[]{:S(2)}, u32[]{:S(2)}) collective-permute-start(f32[2,17,8,128]{3,2,1,0:T(8,128)S(1)} %pad_maximum_fusion.1), channel_id=1, source_target_pairs={{0,8},{4,12},{8,0},{12,4},{1,9},{5,13},{9,1},{13,5},{2,10},{6,14},... | collective-permute-start | bytes 417800 | tf_op jit(solution)/shard_map/ppermute | solution.py:379
  28.9 3.9 %collective-permute-done.7 = f32[2,17,8,128]{3,2,1,0:T(8,128)S(1)} collective-permute-done((f32[2,17,8,128]{3,2,1,0:T(8,128)S(1)}, f32[2,17,8,128]{3,2,1,0:T(8,128)S(1)}, u32[]{:S(2)}, u32[]{:S(2)}) %collective-permute-start.7) | collective-permute-done | bytes 139296 | tf_op jit(solution)/shard_map/ppermute | solution.py:379
  32.8 0.1 collective-permute-start.8
  32.9 1.3 %collective-permute-done.8 = f32[2,2,9,8,128]{4,3,2,1,0:T(8,128)S(1)} collective-permute-done((f32[2,2,9,8,128]{4,3,2,1,0:T(8,128)S(1)}, f32[2,2,9,8,128]{4,3,2,1,0:T(8,128)S(1)}, u32[]{:S(2)}, u32[]{:S(2)}) %collective-permute-start.8) | collective-permute-done | bytes 147488 | tf_op jit(solution)/shard_map/ppermute | solution.py:379
  34.3 0.8 %assemble.1 = (f32[2,8,32,128]{3,2,1,0:T(8,128)}, f32[2,1,32,32]{3,2,1,0:T(8,128)}) custom-call(f32[2,9,8,128]{3,2,1,0:T(8,128)S(1)} %get-tuple-element.23.refs_0_, f32[2,9,8,128]{3,2,1,0:T(8,128)S(1)} %pad_maximum_fusion.4.refs_1_, f32[2,9,8,128]{3,2,1,0:T(8,128)S(1)} %get-tuple-element.21.refs_2_, f32[2,9,8,128]{3,2,1,0:T(8,128)S(1)} %get-tuple-element.20.refs_3_), custom_call_target="tpu_custom_call" | custom-call | tf_op jit(solution)/shard_map/assemble/pallas_call | solution.py:496
  (17 shorter events, 0.3 us)
Async XLA Ops:
  1.8 8.3 %collective-permute-start.2 = (f32[21,2,8,128]{3,2,1,0:T(8,128)S(1)}, f32[21,2,8,128]{3,2,1,0:T(8,128)S(1)}, u32[]{:S(2)}, u32[]{:S(2)}) collective-permute-start(f32[21,2,8,128]{3,2,1,0:T(8,128)S(1)} %get-tuple-element.19), channel_id=1, source_target_pairs={{0,8},{4,12},{8,0},{12,4},{1,9},{5,13},{9,1},{13,5},{2,10},{6,14},... | collective-permute-start | bytes 516104 | tf_op jit(solution)/shard_map/ppermute | solution.py:379
  4.8 1.7 %collective-permute-start = (f32[5,2,8,128]{3,2,1,0:T(8,128)S(1)}, f32[5,2,8,128]{3,2,1,0:T(8,128)S(1)}, u32[]{:S(2)}, u32[]{:S(2)}) collective-permute-start(f32[5,2,8,128]{3,2,1,0:T(8,128)S(1)} %get-tuple-element.16), channel_id=1, source_target_pairs={{0,4},{1,2},{2,1},{3,7},{4,0},{5,6},{6,5},{7,3},{8,9},{9,8},{10,11... | collective-permute-start | bytes 122888 | tf_op jit(solution)/shard_map/ppermute | solution.py:409
  4.9 5.2 %collective-permute-start.1 = (f32[5,2,8,128]{3,2,1,0:T(8,128)S(1)}, f32[5,2,8,128]{3,2,1,0:T(8,128)S(1)}, u32[]{:S(2)}, u32[]{:S(2)}) collective-permute-start(f32[5,2,8,128]{3,2,1,0:T(8,128)S(1)} %get-tuple-element.17), channel_id=1, source_target_pairs={{8,0},{10,1},{9,2},{11,3},{12,4},{14,5},{13,6},{15,7},{1,8},{0,9},... | collective-permute-start | bytes 122888 | tf_op jit(solution)/shard_map/ppermute | solution.py:410
  10.2 1.6 %collective-permute-start.3 = (f32[18,2,16,128]{3,2,1,0:T(8,128)S(1)}, f32[18,2,16,128]{3,2,1,0:T(8,128)S(1)}, u32[]{:S(2)}, u32[]{:S(2)}) collective-permute-start(f32[18,2,16,128]{3,2,1,0:T(8,128)S(1)} %get-tuple-element.11), channel_id=1, source_target_pairs={{0,4},{4,0},{8,12},{12,8},{1,5},{5,1},{9,13},{13,9},{2,6},{6,2},{1... | collective-permute-start | bytes 884744 | tf_op jit(solution)/shard_map/ppermute | solution.py:379
  18.2 3.7 %collective-permute-start.4 = (f32[2,1,8,128]{3,2,1,0:T(8,128)S(1)}, f32[2,1,8,128]{3,2,1,0:T(8,128)S(1)}, u32[]{:S(2)}, u32[]{:S(2)}) collective-permute-start(f32[2,1,8,128]{3,2,1,0:T(8,128)S(1)} %get-tuple-element.9), channel_id=1, source_target_pairs={{0,16},{4,20},{8,24},{12,28},{9,25},{13,29},{1,17},{5,21},{2,18},{... | collective-permute-start | bytes 24584 | tf_op jit(solution)/shard_map/ppermute | solution.py:557
  19.9 3.7 %collective-permute-start.6 = (f32[2,1,8,128]{3,2,1,0:T(8,128)S(1)}, f32[2,1,8,128]{3,2,1,0:T(8,128)S(1)}, u32[]{:S(2)}, u32[]{:S(2)}) collective-permute-start(f32[2,1,8,128]{3,2,1,0:T(8,128)S(1)} %get-tuple-element.9), channel_id=1, source_target_pairs={{0,16},{4,24},{8,20},{12,25},{9,28},{13,17},{1,29},{5,18},{2,21},{... | collective-permute-start | bytes 24584 | tf_op jit(solution)/shard_map/ppermute | solution.py:557
  21.9 1.7 %collective-permute-start.5 = (f32[2,1,8,128]{3,2,1,0:T(8,128)S(1)}, f32[2,1,8,128]{3,2,1,0:T(8,128)S(1)}, u32[]{:S(2)}, u32[]{:S(2)}) collective-permute-start(f32[2,1,8,128]{3,2,1,0:T(8,128)S(1)} %collective-permute-done.4.refs_5_), channel_id=1, source_target_pairs={{0,4},{4,0},{8,12},{12,8},{1,5},{5,1},{9,13},{13,9},{2,6},{6,2},{1... | collective-permute-start | bytes 24584 | tf_op jit(solution)/shard_map/ppermute | solution.py:379
  26.9 5.9 %collective-permute-start.7 = (f32[2,17,8,128]{3,2,1,0:T(8,128)S(1)}, f32[2,17,8,128]{3,2,1,0:T(8,128)S(1)}, u32[]{:S(2)}, u32[]{:S(2)}) collective-permute-start(f32[2,17,8,128]{3,2,1,0:T(8,128)S(1)} %pad_maximum_fusion.1), channel_id=1, source_target_pairs={{0,8},{4,12},{8,0},{12,4},{1,9},{5,13},{9,1},{13,5},{2,10},{6,14},... | collective-permute-start | bytes 417800 | tf_op jit(solution)/shard_map/ppermute | solution.py:379
  32.8 1.4 %collective-permute-start.8 = (f32[2,2,9,8,128]{4,3,2,1,0:T(8,128)S(1)}, f32[2,2,9,8,128]{4,3,2,1,0:T(8,128)S(1)}, u32[]{:S(2)}, u32[]{:S(2)}) collective-permute-start(f32[2,2,9,8,128]{4,3,2,1,0:T(8,128)S(1)} %pad_maximum_fusion), channel_id=1, source_target_pairs={{0,4},{4,0},{8,12},{12,8},{1,5},{5,1},{9,13},{13,9},{2,6},{6,2},{1... | collective-permute-start | bytes 442376 | tf_op jit(solution)/shard_map/ppermute | solution.py:379
